TPU v7x, 256 devices: a whole 4x4x8 slice. The times are simulated.
256 devices in a mesh: curve: 128 (over y, z, x_lo, core), chan: 2 (over x_hi).
Axes of the slice: x: 4 (x_hi: 2, x_lo: 2; x = x_hi * 2 + x_lo), y: 4, z: 8, core: 2. Of those that a mesh axis runs over, the one named last changes fastest.
Arguments:
- features: bfloat16 [524288, 256], P('curve', 'chan'), may hold values from -6 to 6
- cotangent: bfloat16 [524288, 256], P('curve', 'chan'), may hold values from -6 to 6
- near_kernel: bfloat16 [4096, 8, 128, 128], P('curve'), may hold values from -0.1875 to 0.1875
- near_index: int32 [4096, 8], P('curve'), may hold values from 0 to 4095, as said below
- near_count: int32 [4096], P('curve'), may hold values from 1 to 8, as said below
- basis_in: bfloat16 [4096, 16, 128], P('curve'), may hold values from -0.09375 to 0.09375
- basis_out: bfloat16 [4096, 128, 16], P('curve'), may hold values from -1.5 to 1.5
- far_kernel: float32 [128, 8, 16, 16], P('curve'), may hold values from -0.5 to 0.5
- far_index: int32 [128, 8], P('curve'), may hold values from 0 to 127, as said below
- channel_mix: float32 [256, 256], replicated, may hold values from -0.375 to 0.375
Outputs:
- layer_out: bfloat16 [524288, 256], P('curve', 'chan')
- feature_grad: bfloat16 [524288, 256], P('curve', 'chan')
Inputs may be any that keep to these rules, and one draw needn't show every extreme that they name: `near_index`: slot 0 of block b holds b; every slot of block b holds a block from b - 32 to b. `near_count`: in every group of 32 blocks one block has all 8 slots live and another block has one. `far_index`: every partner of group g differs from g by 2 or more.
All inputs are finite; a program needn't handle non-finite values.
Results may differ from a plain program's by a relative error of at most 0.006.
Values may be sent and summed in bfloat16 or wider, within the bound.
No kernel may reach another device: no remote copies, remote signals or barrier semaphores. Data moves between devices by JAX's collectives and lax.ppermute only.
A program may use at most 128 MiB of HBM per device.

v0:
```python
import jax
import jax.numpy as jnp
from jax import lax
from jax.sharding import PartitionSpec as P


def shifted(value, axis, steps):
    count = lax.axis_size(axis)
    leading, last = (max(0, -steps), min(count, count - steps))
    return lax.ppermute(value, axis, [(source, source + steps) for source in range(leading, last)])


def split_up(value, dim, count):
    before, after = (value.shape[:dim], value.shape[dim + 1 :])
    return jnp.moveaxis(value.reshape(*before, count, -1, *after), dim, 0)


def sent_and_summed(value, axis, dim):
    blocks = split_up(value, dim, lax.axis_size(axis))
    arrived = lax.all_to_all(blocks, axis, split_axis=0, concat_axis=0, tiled=True)
    return arrived.sum(axis=0)


def body(
    features,
    cotangent,
    near_kernel,
    near_index,
    near_count,
    basis_in,
    basis_out,
    far_kernel,
    far_index,
    channel_mix,
):
    exact = lax.Precision.HIGHEST
    blocks, slots, panels, _ = near_kernel.shape
    width = features.shape[1]
    groups = lax.axis_size("curve")
    position = lax.axis_index("curve")
    chan_pos = lax.axis_index("chan")
    feat_blocks = features.reshape(blocks, panels, width)
    cot_blocks = cotangent.reshape(blocks, panels, width)
    live_slot = lax.iota(jnp.int32, slots)[None, :] < near_count[:, None]
    local_rows = near_index - (position * blocks - blocks)
    coarse = jnp.einsum(
        "brp,bpc->rc", basis_in, feat_blocks, preferred_element_type=jnp.float32
    ).astype(jnp.bfloat16)
    dfar = jnp.einsum("bpr,bpc->rc", basis_out, cot_blocks, preferred_element_type=jnp.float32)
    before = shifted(features, "curve", 1)
    extended = jnp.concatenate([before.reshape(blocks, panels, width), feat_blocks], axis=0)
    picked = extended[local_rows] * live_slot[:, :, None, None].astype(jnp.bfloat16)
    near = jnp.einsum("bspq,bsqc->bpc", near_kernel, picked, preferred_element_type=jnp.float32)
    mix_cols = lax.dynamic_slice_in_dim(channel_mix, chan_pos * width, width, 1)
    far_mats = far_kernel[0]
    partners = far_index[0]
    one_hot = (partners[:, None] == lax.iota(jnp.int32, groups)[None, :]).astype(jnp.float32)
    every = lax.all_gather(coarse[None], "curve", axis=0, tiled=True)
    chosen = jnp.einsum("ag,grc->arc", one_hot, every.astype(jnp.float32), precision=exact)
    partial_coef = jnp.einsum("aqr,arc->qc", far_mats, chosen, precision=exact)
    mix_rows = lax.dynamic_slice_in_dim(channel_mix, chan_pos * width, width, 0)
    term = jnp.dot(partial_coef, mix_rows, precision=exact, preferred_element_type=jnp.float32)
    far_coef = sent_and_summed(term, "chan", 1)
    far_low = far_coef.astype(jnp.bfloat16)
    layer = near + jnp.einsum("bpr,rc->bpc", basis_out, far_low, preferred_element_type=jnp.float32)
    layer_out = layer.astype(jnp.bfloat16).reshape(blocks * panels, width)
    contrib = jnp.einsum(
        "bspq,bpc->bsqc", near_kernel, cot_blocks, preferred_element_type=jnp.float32
    )
    slot_hot = (
        (local_rows[:, :, None] == lax.iota(jnp.int32, 2 * blocks)[None, None, :])
        & live_slot[:, :, None]
    ).astype(jnp.bfloat16)
    contrib_high = contrib.astype(jnp.bfloat16)
    contrib_low = (contrib - contrib_high.astype(jnp.float32)).astype(jnp.bfloat16)
    spread_near = jnp.einsum(
        "bse,bsqc->eqc", slot_hot, contrib_high, preferred_element_type=jnp.float32
    )
    spread_near = spread_near + jnp.einsum(
        "bse,bsqc->eqc", slot_hot, contrib_low, preferred_element_type=jnp.float32
    )
    arrived = shifted(spread_near[:blocks].astype(jnp.bfloat16), "curve", -1).astype(jnp.float32)
    nearback = spread_near[blocks:] + arrived
    unmix_term = jnp.dot(dfar, mix_cols.T, precision=exact, preferred_element_type=jnp.float32)
    dz_share = sent_and_summed(unmix_term, "chan", 1)
    spread = jnp.einsum("aqr,qc->arc", far_mats, dz_share, precision=exact)
    grad_terms = jnp.einsum("ag,arc->grc", one_hot, spread, precision=exact)
    dcoarse = lax.psum_scatter(grad_terms, "curve", scatter_dimension=0, tiled=True)[0]
    dcoarse_low = dcoarse.astype(jnp.bfloat16)
    grad = nearback + jnp.einsum(
        "brp,rc->bpc", basis_in, dcoarse_low, preferred_element_type=jnp.float32
    )
    feature_grad = grad.astype(jnp.bfloat16).reshape(blocks * panels, width)
    return (layer_out, feature_grad)


def solution(mesh):
    return jax.shard_map(
        body,
        mesh=mesh,
        in_specs=(
            P("curve", "chan"),
            P("curve", "chan"),
            P("curve", None, None, None),
            P("curve", None),
            P("curve"),
            P("curve", None, None),
            P("curve", None, None),
            P("curve", None, None, None),
            P("curve", None),
            P(),
        ),
        out_specs=(P("curve", "chan"), P("curve", "chan")),
        check_vma=False,
    )
```

profile of v0, /device:TPU:0, one launch (start us, length us, event | category | flops | bytes accessed | tf_op | source)
XLA Modules:
  0.0 787.8 jit_solution(6620656626656210797)
XLA Ops:
  7.2 0.0 copy-start
  7.2 0.7 iota_compare_fusion.2
  7.9 0.7 compare_select_fusion
  8.6 0.0 copy-done
  8.6 7.9 %subtract_convert_fusion = (bf16[32,8,128,128]{3,2,1,0:T(8,128)(2,1)}, bf16[32,8,128,128]{3,2,1,0:T(8,128)(2,1)S(1)}) fusion(bf16[32,8,128,128]{3,2,1,0:T(8,128)(2,1)} %param.12, bf16[32,128,128,1]{2,1,3,0:T(8,128)(2,1)S(1)} %bitcast.89), kind=kOutput, calls=%fused_computation.1 | convolution fusion | flops 1090519040 | bytes 26214400 | tf_op jit(solution)/shard_map/bspq,bpc->bsqc/dot_general | solution.py:67
  16.5 8.4 %fusion = f32[64,128,128,1]{2,0,3,1:T(8,128)S(1)} fusion(bf16[32,8,128,128]{3,2,1,0:T(8,128)(2,1)} %get-tuple-element.2, s32[32,8]{0,1:T(8,128)S(1)} %get-tuple-element.5, pred[32,8]{0,1:T(8,128)(4,1)S(1)} %get-tuple-element.6), kind=kOutput, calls=%fused_computation.2 | convolution fusion | flops 536903680 | bytes 12584192 | tf_op jit(solution)/shard_map/bse,bsqc->eqc/dot_general | solution.py:79
  25.0 0.0 copy-start.5
  25.0 0.0 copy-start.6
  25.0 0.0 copy-start.2
  25.0 0.0 copy-start.4
  25.0 0.0 copy-start.7
  25.0 0.0 copy-start.8
  25.1 5.5 bitcast_add_fusion
  30.5 0.0 copy-start.1
  30.5 2.0 copy-done.1
  32.5 1.2 slice.19
  33.7 1.3 collective-permute-start.1
  35.0 0.0 copy-done.5
  35.0 0.2 convolution_bitcast_fusion.3
  35.3 0.0 copy-done.6
  35.3 0.2 convolution_bitcast_fusion.1
  35.5 0.6 copy.55
  36.1 3.2 all-to-all-start.1
  39.4 0.0 reduce-scatter.2.cloned.1.call-start
  39.4 0.0 copy-done.2
  39.4 4.0 collective-permute-start
  43.4 0.0 copy-done.4
  43.4 0.2 fusion.14
  43.7 164.0 %all-gather = bf16[2048,128]{1,0:T(8,128)(2,1)S(1)} all-gather(bf16[16,128]{1,0:T(8,128)(2,1)S(1)} %fusion.14), channel_id=2, replica_groups=mesh['curve'=128,'chan'=2] {'curve'}, dimensions={0}, use_global_device_ids=true | all-gather | bytes 528384 | tf_op jit(solution)/shard_map/all_gather | solution.py:58
  207.6 0.0 copy-done.7
  207.6 0.1 copy.33
  207.7 0.0 all-to-all-done.1
  207.8 0.2 convolution_bitcast_fusion
  208.0 0.0 copy-done.8
  208.0 0.7 fusion.34
  208.7 1.6 copy.34
  210.2 0.0 reduce-scatter.2.cloned.1.call-update
  210.3 0.2 fusion.15
  210.5 0.2 convolution_bitcast_fusion.4
  210.7 0.2 convolution_bitcast_fusion.2
  210.9 0.6 copy.56
  211.6 3.9 all-to-all-start
  215.5 0.1 copy.24
  215.5 0.1 reshape.79
  215.7 1.3 copy.35
  216.9 0.1 copy.25
  217.0 3.9 all-to-all-done
  220.9 1.8 fusion.29
  222.7 0.0 collective-permute-done
  222.7 1.7 pad_maximum_fusion
  224.4 8.5 %gather_fusion = bf16[256,128,128]{2,1,0:T(8,128)(2,1)} fusion(bf16[64,128,128]{2,1,0:T(8,128)(2,1)S(1)} %pad_maximum_fusion, s32[1024]{0:T(1024)S(1)} %pad_clamp_fusion), kind=kCustom, calls=%fused_computation | custom fusion | bytes 16778240 | tf_op jit(solution)/shard_map/gather | solution.py:52
  233.0 0.0 copy-start.3
  233.0 9.9 %fusion.11 = bf16[32,128,128]{2,1,0:T(8,128)(2,1)} fusion(f32[128,32,128]{0,2,1:T(8,128)} %fusion.29, bf16[32,8,128,128]{3,2,1,0:T(8,128)(2,1)} %param.12, bf16[32,8,128,128]{3,2,1,0:T(8,128)(2,1)} %bitcast.91, bf16[32,8]{1,0:T(8,128)(2,1)S(1)} %copy.25), kind=kOutput, calls=%fused_computation.16 | convolution fusion | flops 1091567616 | bytes 19923456 | tf_op jit(solution)/shard_map/bspq,bsqc->bpc/dot_general | solution.py:53
  242.8 0.0 collective-permute-done.1
  242.8 534.3 %reduce-scatter.2.cloned.1.call-done = f32[1,16,128]{2,1,0:T(8,128)} async-done(((f32[128,16,128]{2,1,0:T(8,128)}), f32[1,16,128]{2,1,0:T(8,128)}) %reduce-scatter.2.cloned.1.call-update) | async-done | bytes 8208 | tf_op jit(solution)/shard_map/reduce_scatter | solution.py:88
  777.2 0.0 copy-done.3
  777.2 2.4 fusion.10
  779.6 1.4 copy.36
  (3 shorter events, 0.0 us)
Async XLA Ops:
  7.2 1.5 copy-start
  25.0 10.0 %copy-start.5 = (bf16[32,128,16]{1,2,0:T(8,128)(2,1)S(1)}, bf16[32,128,16]{1,2,0:T(8,128)(2,1)}, u32[]{:S(2)}) copy-start(bf16[32,128,16]{1,2,0:T(8,128)(2,1)} %param.16) | copy-start | bytes 393220
  25.0 10.3 %copy-start.6 = (f32[256,256]{1,0:T(8,128)S(1)}, f32[256,256]{1,0:T(8,128)}, u32[]{:S(2)}) copy-start(f32[256,256]{1,0:T(8,128)} %param.19) | copy-start | bytes 786436
  25.0 14.4 %copy-start.2 = (bf16[4096,128]{1,0:T(8,128)(2,1)S(1)}, bf16[4096,128]{1,0:T(8,128)(2,1)}, u32[]{:S(2)}) copy-start(bf16[4096,128]{1,0:T(8,128)(2,1)} %param.10) | copy-start | bytes 3145732
  25.0 18.4 %copy-start.4 = (bf16[32,16,128]{2,1,0:T(8,128)(2,1)S(1)}, bf16[32,16,128]{2,1,0:T(8,128)(2,1)}, u32[]{:S(2)}) copy-start(bf16[32,16,128]{2,1,0:T(8,128)(2,1)} %param.15) | copy-start | bytes 393220
  25.0 182.6 %copy-start.7 = (f32[1,8,16,16]{3,2,1,0:T(8,128)S(1)}, f32[1,8,16,16]{3,2,1,0:T(8,128)}, u32[]{:S(2)}) copy-start(f32[1,8,16,16]{3,2,1,0:T(8,128)} %param.17) | copy-start | bytes 24580
  25.0 182.9 %copy-start.8 = (s32[1,8]{1,0:T(1,128)S(1)}, s32[1,8]{1,0:T(1,128)}, u32[]{:S(2)}) copy-start(s32[1,8]{1,0:T(1,128)} %param.18) | copy-start | bytes 100
  30.5 2.0 copy-start.1
  33.7 209.1 %collective-permute-start.1 = (bf16[32,128,128]{2,0,1:T(8,128)(2,1)}, bf16[32,128,128]{2,0,1:T(8,128)(2,1)}, u32[]{:S(2)}, u32[]{:S(2)}) collective-permute-start(bf16[32,128,128]{2,0,1:T(8,128)(2,1)} %slice.19), channel_id=1, source_target_pairs={{2,0},{4,2},{6,4},{8,6},{10,8},{12,10},{14,12},{16,14},{18,16},{20... | collective-permute-start | bytes 3145736 | tf_op jit(solution)/shard_map/ppermute | solution.py:10
  36.1 171.6 %all-to-all-start.1 = ((f32[2,16,128]{2,1,0:T(8,128)}), f32[2,16,128]{2,1,0:T(8,128)S(1)}, u32[]{:S(2)}, u32[]{:S(2)}) async-start(f32[2,16,128]{2,1,0:T(8,128)} %bitcast.86), calls=%async_computation.1 | async-start | bytes 32768 | tf_op jit(solution)/shard_map/all_to_all | solution.py:20
  39.4 737.8 %reduce-scatter.2.cloned.1.call-start = ((), (), s32[]{:S(2)}) async-start(), calls=%async_computation.3 | async-start | bytes 1056768 | tf_op jit(solution)/shard_map/reduce_scatter | solution.py:88
  39.4 183.3 %collective-permute-start = (bf16[4096,128]{1,0:T(8,128)(2,1)S(1)}, bf16[4096,128]{1,0:T(8,128)(2,1)}, u32[]{:S(2)}, u32[]{:S(2)}) collective-permute-start(bf16[4096,128]{1,0:T(8,128)(2,1)S(1)} %copy-done.2), channel_id=1, source_target_pairs={{0,2},{2,4},{4,6},{6,8},{8,10},{10,12},{12,14},{14,16},{16,18},{18... | collective-permute-start | bytes 3145736 | tf_op jit(solution)/shard_map/ppermute | solution.py:10
  211.6 9.3 %all-to-all-start = ((f32[2,16,128]{2,1,0:T(8,128)}), f32[2,16,128]{2,1,0:T(8,128)S(1)}, u32[]{:S(2)}, u32[]{:S(2)}) async-start(f32[2,16,128]{2,1,0:T(8,128)} %bitcast.88), calls=%async_computation | async-start | bytes 32768 | tf_op jit(solution)/shard_map/all_to_all | solution.py:20
  233.0 544.2 %copy-start.3 = (bf16[32,16,128]{0,1,2:T(8,128)(2,1)S(1)}, bf16[32,16,128]{0,1,2:T(8,128)(2,1)}, u32[]{:S(2)}) copy-start(bf16[32,16,128]{0,1,2:T(8,128)(2,1)} %copy.35) | copy-start | bytes 393220
Sparse Core Ops, SparseCore 0:
  210.4 566.7 reduce-scatter.1
where the time goes:
time: 788 us
  waiting for transfers between devices  538 us (68%)
  blocking collectives  164 us (21%)
  matrix products  38.2 us (5%)
  local copies, waits for them, and re-layouts  17.6 us (2%)
  between operations  14.2 us (2%)
  starting transfers between devices  12.5 us (2%)
    reduce_scatter x1, waiting for transfers between devices, body(): lax.psum_scatter(grad_terms, 'curve', scatter_dimension=0, tiled=True)[0]  534 us
    all_gather x1, blocking collectives, body(): every = lax.all_gather(coarse[None], 'curve', axis=0, tiled=True)  164 us
  transfers between devices with their start and end apart: 5, of which 2 were waited for; matrix products, arithmetic and copies ran while one was open for 4% of the time, Pallas kernels for 0%

commit v1 on v0

v1 whole, which is shorter than its diff:
```python
import jax
import jax.numpy as jnp
from jax import lax
from jax.experimental import pallas as pl
from jax.experimental.pallas import tpu as pltpu
from jax.sharding import PartitionSpec as P


F32 = jnp.float32
BF16 = jnp.bfloat16
MIB = 1 << 20
QUAD = 4


def params(mib, semantics=("arbitrary",)):
    return pltpu.CompilerParams(dimension_semantics=semantics, vmem_limit_bytes=mib * MIB)


def whole(shape):
    return pl.BlockSpec(shape, lambda *_: (0,) * len(shape))


def dot(a, b, dims=(((1,), (0,)), ((), ()))):
    return lax.dot_general(a, b, dims, preferred_element_type=F32)


def split(value):
    high = value.astype(BF16)
    return high, (value - high.astype(F32)).astype(BF16)


def hbm(value):
    return pltpu.with_memory_space_constraint(value, pltpu.HBM)


def lanes(shape):
    return lax.broadcasted_iota(jnp.int32, shape, 1)


def moved(value, block, keep):
    rolled = pltpu.roll(value, lax.rem(block * 32 + 256, 128), 1)
    return jnp.where(lanes(value.shape) // 32 == keep, rolled, 0.0)


def project_kernel(far_index, feat, cot, b_in, b_out, mix, far, keep, give, pack, acc_f, acc_b):
    step = pl.program_id(0)

    @pl.when(step == 0)
    def _():
        acc_f[...] = jnp.zeros_like(acc_f)
        acc_b[...] = jnp.zeros_like(acc_b)
        wide = jnp.concatenate([far[...], jnp.zeros((128, 112), F32)], axis=1)
        pack[0:16, :] = wide.T[0:16]
        lane = lanes((8, 128)) // 16
        row = jnp.zeros((8, 128), jnp.int32)
        for a in range(8):
            row = jnp.where(lane == a, far_index[0, a], row)
        pack[16:24, :] = row.astype(F32)

    count = b_in.shape[0]
    acc_f[...] += dot(jnp.concatenate([b_in[i] for i in range(count)], axis=1), feat[...])
    acc_b[...] += dot(jnp.concatenate([b_out[i] for i in range(count)], axis=1), cot[...])

    @pl.when(step == pl.num_programs(0) - 1)
    def _():
        half = lax.axis_index("chan")
        start = pl.multiple_of(half * 128, 128)
        exact = lax.Precision.HIGHEST
        coarse = acc_f[...].astype(BF16).astype(F32)
        for oh, out in enumerate((keep, give)):
            there = pl.multiple_of((half ^ oh) * 128, 128)
            out[0:16, :] = jnp.dot(
                coarse,
                mix[pl.ds(start, 128), pl.ds(there, 128)],
                precision=exact,
                preferred_element_type=F32,
            )
            out[16:32, :] = lax.dot_general(
                acc_b[...],
                mix[pl.ds(there, 128), pl.ds(start, 128)],
                (((1,), (1,)), ((), ())),
                precision=exact,
                preferred_element_type=F32,
            )


def deal_kernel(keep, got, pack, *outs):
    me = lax.rem(lax.axis_index("curve"), QUAD)
    both = keep[...] + got[...]
    for os in range(4):
        outs[os][0:32, :] = moved(both, me - (me ^ os), me)
        outs[os][32:56, :] = pack[...]


def backward_kernel(index, count, near, cot, prev, own, acc):
    step = pl.program_id(0)
    per = near.shape[0]
    base = (lax.axis_index("curve") - 1) * 32

    @pl.when(step == 0)
    def _():
        acc[...] = jnp.zeros_like(acc)

    for i in range(per):
        b = step * per + i
        cot_t = cot[i * 128 : (i + 1) * 128, :].T
        live = count[b]
        for k in range(0, 8, 2):
            pair = jnp.concatenate([near[i, k], near[i, k + 1]], axis=1)
            term = dot(cot_t, pair)
            for j in range(2):
                row = jnp.where(k + j < live, index[k + j, b] - base, 64)
                acc[row] += term[:, j * 128 : (j + 1) * 128]

    @pl.when(step == pl.num_programs(0) - 1)
    def _():
        prev[...] = acc[0:32].astype(BF16)
        own[...] = acc[32:64]


def forward_kernel(index, count, near, halo, feat, out, rows):
    step = pl.program_id(0)
    per = near.shape[0]
    base = (lax.axis_index("curve") - 1) * 32

    @pl.when(step == 0)
    def _():
        rows[0:32] = halo[...]
        rows[32:64] = feat[...]
        rows[64] = jnp.zeros((128, 128), BF16)

    for i in range(per):
        b = step * per + i
        live = count[b]
        picked = [
            rows[jnp.where(k < live, index[k, b] - base, 64)] for k in range(8)
        ]
        tiles = jnp.concatenate([near[i, k] for k in range(8)], axis=1)
        out[i * 128 : (i + 1) * 128, :] = dot(tiles, jnp.concatenate(picked, axis=0))


def spread_kernel(*refs):
    msgs, (out, couple), (total,) = refs[:4], refs[4:6], refs[6:]
    me = lax.rem(lax.axis_index("curve"), QUAD)
    value = msgs[0][0:32, :]
    for ref in msgs[1:]:
        value = value + ref[0:32, :]
    fwd = value[0:16].astype(BF16)
    bwd = value[16:32]
    lane = lanes((24, 128))
    for os in range(4):
        total[me ^ os] = msgs[os][32:56, :]
    packed = []
    for a in range(8):
        group = jnp.zeros((24, 128), F32)
        for g in range(4):
            rolled = pltpu.roll(total[g], (16 * (g - a)) % 128, 1)
            group = jnp.where(lane // 16 == g, rolled, group)
        packed.append(group + pltpu.roll(group, 64, 1))
    lane8 = lanes((8, 128))
    for p in range(2):
        quarter = ((lane8 // 16) % 4 + lane8 // 64 + 2 * p) % 4
        wants = [packed[a][16:24].astype(jnp.int32) - quarter for a in range(8)]
        for t in range(32):
            tile = jnp.zeros((16, 128), F32)
            for a in range(8):
                hit = wants[a] == 4 * t
                hit = jnp.concatenate([hit, hit], axis=0)
                tile = tile + jnp.where(hit, packed[a][0:16], 0.0)
            couple[p, t * 16 : (t + 1) * 16, :] = tile
    lane16 = lanes((16, 128))
    block = jnp.concatenate(
        [jnp.where(lane16 // 32 == g, bwd, 0.0) for g in range(4)], axis=0
    )
    contrib = jnp.zeros((512, 128), F32)
    for p in range(2):
        rhs = jnp.concatenate(
            [block if d == 0 else pltpu.roll(block, 32 * d, 1) for d in (2 * p, 2 * p + 1)],
            axis=0,
        )
        r_hi, r_lo = split(rhs)
        k_hi, k_lo = split(couple[p])
        contrib = contrib + (dot(k_hi, r_lo) + dot(k_lo, r_hi)) + dot(k_hi, r_hi)
    contrib = contrib.astype(BF16)
    for t in range(32):
        out[t, 0:16, :] = fwd
        out[t, 16:32, :] = contrib[t * 16 : (t + 1) * 16]


def collect_kernel(arrived, couple, *refs):
    outs, (picked, summed) = refs[:4], refs[4:]
    me = lax.rem(lax.axis_index("curve"), QUAD)
    total = arrived[0, 16:32, :].astype(F32)
    for t in range(1, 32):
        total = total + arrived[t, 16:32, :].astype(F32)
    source = jnp.concatenate([arrived[t, 0:16, :] for t in range(32)], axis=0)
    over_rows = (((0,), (0,)), ((), ()))
    for p in range(2):
        k_hi, k_lo = split(couple[p])
        picked[p * 128 : (p + 1) * 128, :] = dot(k_hi, source, over_rows) + dot(
            k_lo, source, over_rows
        )
    for os in range(4):
        owner = me ^ os
        far = jnp.zeros((16, 128), F32)
        for d in range(4):
            rows = picked[pl.ds(pl.multiple_of(d * 64 + owner * 16, 16), 16), :]
            far = far + moved(rows, me - owner - d, me)
        outs[os][0:16, :] = far.astype(BF16)
        outs[os][16:32, :] = moved(total, me - owner, me).astype(BF16)


def finish_kernel(near, own, arrived, b_in, b_out, m0, m1, m2, m3, layer, grad):
    value = ((m0[...] + m1[...]) + (m2[...] + m3[...])).astype(BF16)
    far = value[0:16]
    coarse_t = value[16:32].astype(F32).T.astype(BF16)
    for i in range(b_in.shape[0]):
        rows = slice(i * 128, (i + 1) * 128)
        term = dot(b_out[i], far, (((0,), (0,)), ((), ())))
        layer[rows, :] = (near[rows, :] + term).astype(BF16)
        total = own[i] + arrived[i].astype(F32) + dot(coarse_t, b_in[i])
        grad[rows, :] = total.astype(BF16).T


def layer_step(
    features,
    cotangent,
    near_kernel,
    near_index,
    near_count,
    basis_in,
    basis_out,
    far_kernel,
    far_index,
    channel_mix,
):
    groups = lax.axis_size("curve")
    blocks = near_kernel.shape[0]
    places = groups // QUAD
    per = 4
    steps = blocks // per
    index = near_index.T
    cube = (blocks, 128, 128)

    halo = lax.ppermute(features, "curve", [(i, i + 1) for i in range(groups - 1)])

    a_steps = 4
    a_blocks = blocks // a_steps
    strip_a = pl.BlockSpec((a_blocks * 128, 128), lambda i: (i, 0))
    thin_a = pl.BlockSpec((a_blocks, 16, 128), lambda i: (i, 0, 0))
    rows32 = jax.ShapeDtypeStruct((32, 128), F32)
    keep, give, pack = pl.pallas_call(
        project_kernel,
        out_shape=[rows32, rows32, jax.ShapeDtypeStruct((24, 128), F32)],
        grid=(a_steps,),
        in_specs=[
            pl.BlockSpec(memory_space=pltpu.SMEM),
            strip_a,
            strip_a,
            thin_a,
            thin_a,
            whole((256, 256)),
            whole((128, 16)),
        ],
        out_specs=[whole((32, 128)), whole((32, 128)), whole((24, 128))],
        scratch_shapes=[pltpu.VMEM((16, 128), F32)] * 2,
        compiler_params=params(40),
        name="project",
    )(
        far_index,
        hbm(features),
        hbm(cotangent),
        hbm(basis_in),
        hbm(jnp.swapaxes(basis_out, 1, 2)),
        hbm(channel_mix),
        hbm(far_kernel.reshape(128, 16)),
    )
    got = lax.ppermute(give, "chan", [(0, 1), (1, 0)])
    msgs = pl.pallas_call(
        deal_kernel,
        out_shape=[jax.ShapeDtypeStruct((56, 128), F32)] * 4,
        compiler_params=params(8, None),
        name="deal",
    )(keep, got, pack)
    seen = [msgs[0]]
    for o in range(1, 4):
        seen.append(lax.ppermute(msgs[o], "curve", [(i, i ^ o) for i in range(groups)]))

    tiles = pl.BlockSpec((per, 8, 128, 128), lambda i, *_: (i, 0, 0, 0))
    strip = pl.BlockSpec((per * 128, 128), lambda i, *_: (i, 0))
    prev, own = pl.pallas_call(
        backward_kernel,
        out_shape=[jax.ShapeDtypeStruct(cube, BF16), jax.ShapeDtypeStruct(cube, F32)],
        grid_spec=pltpu.PrefetchScalarGridSpec(
            num_scalar_prefetch=2,
            grid=(steps,),
            in_specs=[tiles, strip],
            out_specs=[whole(cube), whole(cube)],
            scratch_shapes=[pltpu.VMEM((65, 128, 128), F32)],
        ),
        compiler_params=params(40),
        cost_estimate=pl.CostEstimate(flops=8 << 30, bytes_accessed=12 << 20, transcendentals=0),
        name="backward",
    )(index, near_count, hbm(near_kernel), hbm(cotangent))
    arrived = lax.ppermute(prev, "curve", [(i + 1, i) for i in range(groups - 1)])

    out_msg, couple = pl.pallas_call(
        spread_kernel,
        out_shape=[
            pltpu.HBM((places, 32, 128), BF16),
            pltpu.HBM((2, places * 16, 128), F32),
        ],
        scratch_shapes=[pltpu.VMEM((4, 24, 128), F32)],
        compiler_params=params(8, None),
        name="spread",
    )(*seen)
    rings = [[t * QUAD + s for t in range(places)] for s in range(QUAD)]
    in_msg = lax.all_to_all(out_msg, "curve", 0, 0, tiled=True, axis_index_groups=rings)

    near = pl.pallas_call(
        forward_kernel,
        out_shape=pltpu.HBM((blocks * 128, 128), F32),
        grid_spec=pltpu.PrefetchScalarGridSpec(
            num_scalar_prefetch=2,
            grid=(steps,),
            in_specs=[tiles, whole(cube), whole(cube)],
            out_specs=strip,
            scratch_shapes=[pltpu.VMEM((65, 128, 128), BF16)],
        ),
        compiler_params=params(40),
        cost_estimate=pl.CostEstimate(flops=8 << 30, bytes_accessed=12 << 20, transcendentals=0),
        name="forward",
    )(index, near_count, hbm(near_kernel), halo.reshape(cube), hbm(features.reshape(cube)))

    back = pl.pallas_call(
        collect_kernel,
        out_shape=[jax.ShapeDtypeStruct((32, 128), BF16)] * 4,
        scratch_shapes=[pltpu.VMEM((256, 128), F32), pltpu.VMEM((16, 128), F32)],
        compiler_params=params(8, None),
        name="collect",
    )(in_msg, hbm(couple))
    home = [back[0]]
    for o in range(1, 4):
        home.append(lax.ppermute(back[o], "curve", [(i, i ^ o) for i in range(groups)]))

    block3 = pl.BlockSpec((per, 128, 128), lambda i: (i, 0, 0))
    thin = pl.BlockSpec((per, 16, 128), lambda i: (i, 0, 0))
    strip1 = pl.BlockSpec((per * 128, 128), lambda i: (i, 0))
    layer, grad = pl.pallas_call(
        finish_kernel,
        out_shape=[jax.ShapeDtypeStruct((blocks * 128, 128), BF16)] * 2,
        grid=(steps,),
        in_specs=[strip1, block3, block3, thin, thin] + [whole((32, 128))] * 4,
        out_specs=[strip1, strip1],
        compiler_params=params(40),
        name="finish",
    )(
        hbm(near), own, arrived, hbm(basis_in), hbm(jnp.swapaxes(basis_out, 1, 2)), *home
    )
    return (layer, grad)


def solution(mesh):
    return jax.shard_map(
        layer_step,
        mesh=mesh,
        in_specs=(
            P("curve", "chan"),
            P("curve", "chan"),
            P("curve", None, None, None),
            P("curve", None),
            P("curve"),
            P("curve", None, None),
            P("curve", None, None),
            P("curve", None, None, None),
            P("curve", None),
            P(),
        ),
        out_specs=(P("curve", "chan"), P("curve", "chan")),
        check_vma=False,
    )
```

time: 788 us -> 64.4 us (0.08)
  the two profiles are of different devices: /device:TPU:0 before, /device:TPU:25 now
where the time goes in v1:
time: 64.4 us; the launch traced here: 63.6 us
  Pallas kernels  33.1 us (51%)
  starting transfers between devices  27.8 us (43%)
  waiting for transfers between devices  1.37 us (2%)
  between operations  0.75 us (1%)
  local copies, waits for them, and re-layouts  0.66 us (1%)
    all_to_all x1, starting transfers between devices, layer_step(): lax.all_to_all(out_msg, 'curve', 0, 0, tiled=True, axis_index_groups=rings)  11 us
    pallas_call x1, Pallas kernels, layer_step(): pl.pallas_call(forward_kernel, out_shape=pltpu.HBM((blocks * 128, 128), F...  9.89 us
    pallas_call x1, Pallas kernels, layer_step(): pl.pallas_call(backward_kernel, out_shape=[jax.ShapeDtypeStruct(cube, BF1...  9.87 us
    pallas_call x1, Pallas kernels, layer_step(): pl.pallas_call(finish_kernel, out_shape=[jax.ShapeDtypeStruct((blocks * 1...  6.77 us
    ppermute x3, starting transfers between devices, layer_step(): lax.ppermute(back[o], 'curve', [(i, i ^ o) for i in range(groups)])  4.81 us
    ppermute x3, starting transfers between devices, layer_step(): lax.ppermute(msgs[o], 'curve', [(i, i ^ o) for i in range(groups)])  3.64 us
    pallas_call x1, Pallas kernels, layer_step(): pl.pallas_call(project_kernel, out_shape=[rows32, rows32, jax.ShapeDtypeS...  3.4 us
    ppermute x1, starting transfers between devices, layer_step(): lax.ppermute(features, 'curve', [(i, i + 1) for i in range(groups - 1)])  3.13 us
  transfers between devices with their start and end apart: 10, of which 1 were waited for; matrix products, arithmetic and copies ran while one was open for 0% of the time, Pallas kernels for 36%

profile of v1, /device:TPU:25, one launch (start us, length us, event | category | flops | bytes accessed | tf_op | source)
XLA Modules:
  0.0 63.6 jit_solution(17292618829960422956)
XLA Ops:
  0.6 0.0 copy-start.2
  0.6 0.0 copy-start
  0.7 0.7 %copy-done = s32[1,8]{1,0:T(1,128)S(1)} copy-done((s32[1,8]{1,0:T(1,128)S(1)}, s32[1,8]{1,0:T(1,128)}, u32[]{:S(2)}) %copy-start) | copy-done | bytes 56
  1.3 0.0 copy-start.1
  1.3 3.4 %project.1 = (f32[32,128]{1,0:T(8,128)S(1)}, f32[32,128]{1,0:T(8,128)S(1)}, f32[24,128]{1,0:T(8,128)S(1)}) custom-call(s32[1,8]{1,0:T(1,128)S(1)} %copy-done, bf16[4096,128]{1,0:T(8,128)(2,1)} %feat.1, bf16[4096,128]{1,0:T(8,128)(2,1)} %cot.3, bf16[32,16,128]{2,1,0:T(8,128)(2,1)} %b_in.3, bf16[32,16,128]{2,1,0:T(8,128)(2,1)} %bitcast.7, f32[256,256]{1,0:T(8,128)} %mix.1, ...), custom_call_target="tpu_custom_call" | custom-call | tf_op jit(solution)/shard_map/project/pallas_call | solution.py:252
  4.7 2.8 %collective-permute-start.2 = (f32[32,128]{1,0:T(8,128)S(1)}, f32[32,128]{1,0:T(8,128)S(1)}, u32[]{:S(2)}, u32[]{:S(2)}) collective-permute-start(f32[32,128]{1,0:T(8,128)S(1)} %get-tuple-element.20), channel_id=1, source_target_pairs={{0,1},{1,0},{2,3},{3,2},{4,5},{5,4},{6,7},{7,6},{8,9},{9,8},{10,11... | collective-permute-start | bytes 49160 | tf_op jit(solution)/shard_map/ppermute | solution.py:278
  7.5 1.4 %collective-permute-done.2.got = f32[32,128]{1,0:T(8,128)S(1)} collective-permute-done((f32[32,128]{1,0:T(8,128)S(1)}, f32[32,128]{1,0:T(8,128)S(1)}, u32[]{:S(2)}, u32[]{:S(2)}) %collective-permute-start.2) | collective-permute-done | bytes 16416 | tf_op jit(solution)/shard_map/ppermute | solution.py:278
  8.9 0.1 deal.1
  8.9 1.9 %collective-permute-start.3 = (f32[56,128]{1,0:T(8,128)S(1)}, f32[56,128]{1,0:T(8,128)S(1)}, u32[]{:S(2)}, u32[]{:S(2)}) collective-permute-start(f32[56,128]{1,0:T(8,128)S(1)} %get-tuple-element.23), channel_id=1, source_target_pairs={{0,2},{2,0},{4,6},{6,4},{8,10},{10,8},{12,14},{14,12},{16,18},{18,... | collective-permute-start | bytes 86024 | tf_op jit(solution)/shard_map/ppermute | solution.py:287
  10.9 1.2 %collective-permute-start.4 = (f32[56,128]{1,0:T(8,128)S(1)}, f32[56,128]{1,0:T(8,128)S(1)}, u32[]{:S(2)}, u32[]{:S(2)}) collective-permute-start(f32[56,128]{1,0:T(8,128)S(1)} %get-tuple-element.24), channel_id=1, source_target_pairs={{0,4},{2,6},{4,0},{6,2},{8,12},{10,14},{12,8},{14,10},{16,20},{18,... | collective-permute-start | bytes 86024 | tf_op jit(solution)/shard_map/ppermute | solution.py:287
  12.1 0.5 collective-permute-start.5
  12.6 3.1 %collective-permute-start = (bf16[4096,128]{1,0:T(8,128)(2,1)}, bf16[4096,128]{1,0:T(8,128)(2,1)}, u32[]{:S(2)}, u32[]{:S(2)}) collective-permute-start(bf16[4096,128]{1,0:T(8,128)(2,1)} %feat.1), channel_id=1, source_target_pairs={{0,2},{2,4},{4,6},{6,8},{8,10},{10,12},{12,14},{14,16},{16,18},{18... | collective-permute-start | bytes 3145736 | tf_op jit(solution)/shard_map/ppermute | solution.py:245
  15.7 0.0 collective-permute-done.3.refs_1_
  15.7 0.0 collective-permute-done.4.refs_2_
  15.7 0.0 collective-permute-done.5.refs_3_
  15.8 1.6 %spread.1 = (bf16[32,32,128]{2,1,0:T(8,128)(2,1)}, f32[2,512,128]{2,1,0:T(8,128)}) custom-call(f32[56,128]{1,0:T(8,128)S(1)} %get-tuple-element.22.refs_0_, f32[56,128]{1,0:T(8,128)S(1)} %collective-permute-done.3.refs_1_, f32[56,128]{1,0:T(8,128)S(1)} %collective-permute-done.4.refs_2_, f32[56,128]{1,0:T(8,128)S(1)} %collective-permute-done.5.refs_3_), custom_call_target="tpu_custom_call" | custom-call | tf_op jit(solution)/shard_map/spread/pallas_call | solution.py:307
  17.3 11.0 %all-to-all-start = ((bf16[32,32,128]{2,1,0:T(8,128)(2,1)}), bf16[32,32,128]{2,1,0:T(8,128)(2,1)S(1)}, u32[]{:S(2)}, u32[]{:S(2)}) async-start(bf16[32,32,128]{2,1,0:T(8,128)(2,1)} %get-tuple-element.26), calls=%async_computation | async-start | bytes 524288 | tf_op jit(solution)/shard_map/all_to_all | solution.py:318
  28.3 0.0 copy-done.2
  28.3 0.0 copy-done.1
  28.3 9.9 %backward.1 = (bf16[32,128,128]{2,1,0:T(8,128)(2,1)}, f32[32,128,128]{2,1,0:T(8,128)S(1)}) custom-call(s32[8,32]{1,0:T(8,128)S(1)} %bitcast.5, s32[32]{0:T(128)S(1)} %copy-done.2, bf16[32,8,128,128]{3,2,1,0:T(8,128)(2,1)} %near.3, bf16[4096,128]{1,0:T(8,128)(2,1)} %cot.3), custom_call_target="tpu_custom_call" | custom-call | flops 8589934592 | bytes 12582912 | tf_op jit(solution)/shard_map/backward/pallas_call | solution.py:291
  38.2 2.4 %collective-permute-start.1 = (bf16[32,128,128]{2,1,0:T(8,128)(2,1)}, bf16[32,128,128]{2,1,0:T(8,128)(2,1)S(1)}, u32[]{:S(2)}, u32[]{:S(2)}) collective-permute-start(bf16[32,128,128]{2,1,0:T(8,128)(2,1)} %get-tuple-element.18), channel_id=1, source_target_pairs={{2,0},{4,2},{6,4},{8,6},{10,8},{12,10},{14,12},{16,14},{18,16},{20... | collective-permute-start | bytes 3145736 | tf_op jit(solution)/shard_map/ppermute | solution.py:305
  40.6 0.0 all-to-all-done.arrived
  40.6 1.5 %collect.1 = (bf16[32,128]{1,0:T(8,128)(2,1)S(1)}, bf16[32,128]{1,0:T(8,128)(2,1)S(1)}, bf16[32,128]{1,0:T(8,128)(2,1)S(1)}, bf16[32,128]{1,0:T(8,128)(2,1)S(1)}) custom-call(bf16[32,32,128]{2,1,0:T(8,128)(2,1)S(1)} %all-to-all-done.arrived, f32[2,512,128]{2,1,0:T(8,128)} %get-tuple-element.27.couple), custom_call_target="tpu_custom_call" | custom-call | tf_op jit(solution)/shard_map/collect/pallas_call | solution.py:335
  42.1 3.1 %collective-permute-start.6 = (bf16[32,128]{1,0:T(8,128)(2,1)S(1)}, bf16[32,128]{1,0:T(8,128)(2,1)S(1)}, u32[]{:S(2)}, u32[]{:S(2)}) collective-permute-start(bf16[32,128]{1,0:T(8,128)(2,1)S(1)} %get-tuple-element.29), channel_id=1, source_target_pairs={{0,2},{2,0},{4,6},{6,4},{8,10},{10,8},{12,14},{14,12},{16,18},{18,... | collective-permute-start | bytes 24584 | tf_op jit(solution)/shard_map/ppermute | solution.py:344
  45.2 0.0 collective-permute-start.7
  45.2 1.7 %collective-permute-start.8 = (bf16[32,128]{1,0:T(8,128)(2,1)S(1)}, bf16[32,128]{1,0:T(8,128)(2,1)S(1)}, u32[]{:S(2)}, u32[]{:S(2)}) collective-permute-start(bf16[32,128]{1,0:T(8,128)(2,1)S(1)} %get-tuple-element.31), channel_id=1, source_target_pairs={{0,6},{2,4},{4,2},{6,0},{8,14},{10,12},{12,10},{14,8},{16,22},{18,... | collective-permute-start | bytes 24584 | tf_op jit(solution)/shard_map/ppermute | solution.py:344
  46.9 0.0 collective-permute-done
  46.9 9.9 %forward.1.near = f32[4096,128]{1,0:T(8,128)} custom-call(s32[8,32]{1,0:T(8,128)S(1)} %bitcast.6, s32[32]{0:T(128)S(1)} %copy-done.2, bf16[32,8,128,128]{3,2,1,0:T(8,128)(2,1)} %near.3, bf16[32,128,128]{2,1,0:T(8,128)(2,1)} %bitcast.1.halo, bf16[32,128,128]{2,1,0:T(8,128)(2,1)} %bitcast.2.feat), custom_call_target="tpu_custom_call" | custom-call | flops 8589934592 | bytes 12582912 | tf_op jit(solution)/shard_map/forward/pallas_call | solution.py:320
  56.8 0.0 collective-permute-done.6.m1
  56.8 0.0 collective-permute-done.7.m2
  56.8 0.0 collective-permute-done.8.m3
  56.8 0.0 collective-permute-done.1.arrived
  56.9 6.8 %finish.1 = (bf16[4096,128]{1,0:T(8,128)(2,1)}, bf16[4096,128]{1,0:T(8,128)(2,1)}) custom-call(f32[4096,128]{1,0:T(8,128)} %forward.1.near, f32[32,128,128]{2,1,0:T(8,128)S(1)} %get-tuple-element.17.own, bf16[32,128,128]{2,1,0:T(8,128)(2,1)S(1)} %collective-permute-done.1.arrived, bf16[32,16,128]{2,1,0:T(8,128)(2,1)} %b_in.3, bf16[32,16,128]{2,1,0:T(8,128)(2,1)} %bitcast.8, ...), custom_call_target="tpu_custom_call" | custom-call | tf_op jit(solution)/shard_map/finish/pallas_call | solution.py:349
Async XLA Ops:
  0.6 27.7 %copy-start.2 = (s32[32]{0:T(128)S(1)}, s32[32]{0:T(128)}, u32[]{:S(2)}) copy-start(s32[32]{0:T(128)} %count.3) | copy-start | bytes 388
  0.6 0.7 %copy-start = (s32[1,8]{1,0:T(1,128)S(1)}, s32[1,8]{1,0:T(1,128)}, u32[]{:S(2)}) copy-start(s32[1,8]{1,0:T(1,128)} %far_index.1) | copy-start | bytes 100
  1.3 27.0 %copy-start.1 = (s32[32,8]{0,1:T(8,128)S(1)}, s32[32,8]{0,1:T(8,128)}, u32[]{:S(2)}) copy-start(s32[32,8]{0,1:T(8,128)} %param.13) | copy-start | bytes 3076
  4.7 4.2 %collective-permute-start.2 = (f32[32,128]{1,0:T(8,128)S(1)}, f32[32,128]{1,0:T(8,128)S(1)}, u32[]{:S(2)}, u32[]{:S(2)}) collective-permute-start(f32[32,128]{1,0:T(8,128)S(1)} %get-tuple-element.20), channel_id=1, source_target_pairs={{0,1},{1,0},{2,3},{3,2},{4,5},{5,4},{6,7},{7,6},{8,9},{9,8},{10,11... | collective-permute-start | bytes 49160 | tf_op jit(solution)/shard_map/ppermute | solution.py:278
  8.9 6.8 %collective-permute-start.3 = (f32[56,128]{1,0:T(8,128)S(1)}, f32[56,128]{1,0:T(8,128)S(1)}, u32[]{:S(2)}, u32[]{:S(2)}) collective-permute-start(f32[56,128]{1,0:T(8,128)S(1)} %get-tuple-element.23), channel_id=1, source_target_pairs={{0,2},{2,0},{4,6},{6,4},{8,10},{10,8},{12,14},{14,12},{16,18},{18,... | collective-permute-start | bytes 86024 | tf_op jit(solution)/shard_map/ppermute | solution.py:287
  10.9 4.9 %collective-permute-start.4 = (f32[56,128]{1,0:T(8,128)S(1)}, f32[56,128]{1,0:T(8,128)S(1)}, u32[]{:S(2)}, u32[]{:S(2)}) collective-permute-start(f32[56,128]{1,0:T(8,128)S(1)} %get-tuple-element.24), channel_id=1, source_target_pairs={{0,4},{2,6},{4,0},{6,2},{8,12},{10,14},{12,8},{14,10},{16,20},{18,... | collective-permute-start | bytes 86024 | tf_op jit(solution)/shard_map/ppermute | solution.py:287
  12.1 3.7 %collective-permute-start.5 = (f32[56,128]{1,0:T(8,128)S(1)}, f32[56,128]{1,0:T(8,128)S(1)}, u32[]{:S(2)}, u32[]{:S(2)}) collective-permute-start(f32[56,128]{1,0:T(8,128)S(1)} %get-tuple-element.25), channel_id=1, source_target_pairs={{0,6},{2,4},{4,2},{6,0},{8,14},{10,12},{12,10},{14,8},{16,22},{18,... | collective-permute-start | bytes 86024 | tf_op jit(solution)/shard_map/ppermute | solution.py:287
  12.6 34.3 %collective-permute-start = (bf16[4096,128]{1,0:T(8,128)(2,1)}, bf16[4096,128]{1,0:T(8,128)(2,1)}, u32[]{:S(2)}, u32[]{:S(2)}) collective-permute-start(bf16[4096,128]{1,0:T(8,128)(2,1)} %feat.1), channel_id=1, source_target_pairs={{0,2},{2,4},{4,6},{6,8},{8,10},{10,12},{12,14},{14,16},{16,18},{18... | collective-permute-start | bytes 3145736 | tf_op jit(solution)/shard_map/ppermute | solution.py:245
  17.3 23.3 %all-to-all-start = ((bf16[32,32,128]{2,1,0:T(8,128)(2,1)}), bf16[32,32,128]{2,1,0:T(8,128)(2,1)S(1)}, u32[]{:S(2)}, u32[]{:S(2)}) async-start(bf16[32,32,128]{2,1,0:T(8,128)(2,1)} %get-tuple-element.26), calls=%async_computation | async-start | bytes 524288 | tf_op jit(solution)/shard_map/all_to_all | solution.py:318
  38.2 18.7 %collective-permute-start.1 = (bf16[32,128,128]{2,1,0:T(8,128)(2,1)}, bf16[32,128,128]{2,1,0:T(8,128)(2,1)S(1)}, u32[]{:S(2)}, u32[]{:S(2)}) collective-permute-start(bf16[32,128,128]{2,1,0:T(8,128)(2,1)} %get-tuple-element.18), channel_id=1, source_target_pairs={{2,0},{4,2},{6,4},{8,6},{10,8},{12,10},{14,12},{16,14},{18,16},{20... | collective-permute-start | bytes 3145736 | tf_op jit(solution)/shard_map/ppermute | solution.py:305
  42.1 14.7 %collective-permute-start.6 = (bf16[32,128]{1,0:T(8,128)(2,1)S(1)}, bf16[32,128]{1,0:T(8,128)(2,1)S(1)}, u32[]{:S(2)}, u32[]{:S(2)}) collective-permute-start(bf16[32,128]{1,0:T(8,128)(2,1)S(1)} %get-tuple-element.29), channel_id=1, source_target_pairs={{0,2},{2,0},{4,6},{6,4},{8,10},{10,8},{12,14},{14,12},{16,18},{18,... | collective-permute-start | bytes 24584 | tf_op jit(solution)/shard_map/ppermute | solution.py:344
  45.2 11.6 %collective-permute-start.7 = (bf16[32,128]{1,0:T(8,128)(2,1)S(1)}, bf16[32,128]{1,0:T(8,128)(2,1)S(1)}, u32[]{:S(2)}, u32[]{:S(2)}) collective-permute-start(bf16[32,128]{1,0:T(8,128)(2,1)S(1)} %get-tuple-element.30), channel_id=1, source_target_pairs={{0,4},{2,6},{4,0},{6,2},{8,12},{10,14},{12,8},{14,10},{16,20},{18,... | collective-permute-start | bytes 24584 | tf_op jit(solution)/shard_map/ppermute | solution.py:344
  45.2 11.6 %collective-permute-start.8 = (bf16[32,128]{1,0:T(8,128)(2,1)S(1)}, bf16[32,128]{1,0:T(8,128)(2,1)S(1)}, u32[]{:S(2)}, u32[]{:S(2)}) collective-permute-start(bf16[32,128]{1,0:T(8,128)(2,1)S(1)} %get-tuple-element.31), channel_id=1, source_target_pairs={{0,6},{2,4},{4,2},{6,0},{8,14},{10,12},{12,10},{14,8},{16,22},{18,... | collective-permute-start | bytes 24584 | tf_op jit(solution)/shard_map/ppermute | solution.py:344

commit v2 on v1

v2 whole, which is shorter than its diff:
```python
import jax
import jax.numpy as jnp
from jax import lax
from jax.experimental import pallas as pl
from jax.experimental.pallas import tpu as pltpu
from jax.sharding import PartitionSpec as P


F32 = jnp.float32
BF16 = jnp.bfloat16
MIB = 1 << 20
QUAD = 4
ZS = 8
PARTS = 4
UNROLL = 4


def params(mib, semantics=("arbitrary",)):
    return pltpu.CompilerParams(dimension_semantics=semantics, vmem_limit_bytes=mib * MIB)


def dot(a, b, dims=(((1,), (0,)), ((), ()))):
    return lax.dot_general(a, b, dims, preferred_element_type=F32)


def split(value):
    high = value.astype(BF16)
    return high, (value - high.astype(F32)).astype(BF16)


def hbm(value):
    return pltpu.with_memory_space_constraint(value, pltpu.HBM)


def lanes(shape):
    return lax.broadcasted_iota(jnp.int32, shape, 1)


def moved(value, block, keep):
    rolled = pltpu.roll(value, lax.rem(block * 32 + 256, 128), 1)
    return jnp.where(lanes(value.shape) // 32 == keep, rolled, 0.0)


def project_kernel(
    far_index, feat, cot, near, b_in, b_out, mix, far,
    keep, give, pack, feat_v, cot_v, near_v,
    b_in_v, b_out_v, mix_v, far_v, sems,
):
    count = feat.shape[0]
    part = count // PARTS
    loads = []
    for n in range(PARTS):
        rows = pl.ds(n * part, part)
        loads.append(
            [
                pltpu.make_async_copy(src.at[rows], dst.at[rows], sems.at[n, j])
                for j, (src, dst) in enumerate(
                    ((feat, feat_v), (b_in, b_in_v), (cot, cot_v), (b_out, b_out_v))
                )
            ]
        )
    small = [
        pltpu.make_async_copy(mix, mix_v, sems.at[PARTS, 0]),
        pltpu.make_async_copy(far, far_v, sems.at[PARTS, 1]),
    ]
    big = [
        pltpu.make_async_copy(near.at[pl.ds(n * part, part)], near_v.at[pl.ds(n * part, part)], sems.at[n, 4])
        for n in range(PARTS)
    ]
    for copy in [c for group in loads for c in group] + small + big:
        copy.start()

    acc_f = jnp.zeros((16, 128), F32)
    acc_b = jnp.zeros((16, 128), F32)
    for n in range(PARTS):
        for copy in loads[n]:
            copy.wait()
        picks = range(n * part, (n + 1) * part)
        acc_f += dot(
            jnp.concatenate([b_in_v[i] for i in picks], axis=1),
            feat_v[n * part : (n + 1) * part].reshape(part * 128, 128),
        )
        acc_b += dot(
            jnp.concatenate([b_out_v[i] for i in picks], axis=1),
            cot_v[n * part : (n + 1) * part].reshape(part * 128, 128),
        )
    for copy in small:
        copy.wait()
    half = lax.axis_index("chan")
    start = pl.multiple_of(half * 128, 128)
    exact = lax.Precision.HIGHEST
    coarse = acc_f.astype(BF16).astype(F32)
    for oh, out in enumerate((keep, give)):
        there = pl.multiple_of((half ^ oh) * 128, 128)
        out[0:16, :] = jnp.dot(
            coarse,
            mix_v[pl.ds(start, 128), pl.ds(there, 128)],
            precision=exact,
            preferred_element_type=F32,
        )
        out[16:32, :] = lax.dot_general(
            acc_b,
            mix_v[pl.ds(there, 128), pl.ds(start, 128)],
            (((1,), (1,)), ((), ())),
            precision=exact,
            preferred_element_type=F32,
        )
    wide = jnp.concatenate([far_v[...], jnp.zeros((128, 112), F32)], axis=1)
    pack[0:16, :] = wide.T[0:16]
    lane = lanes((8, 128)) // 16
    row = jnp.zeros((8, 128), jnp.int32)
    for a in range(8):
        row = jnp.where(lane == a, far_index[0, a], row)
    pack[16:24, :] = row.astype(F32)
    for copy in big:
        copy.wait()


def deal_kernel(keep, got, pack, *outs):
    me = lax.rem(lax.axis_index("curve"), QUAD)
    both = keep[...] + got[...]
    for os in range(4):
        outs[os][0:32, :] = moved(both, me - (me ^ os), me)
        outs[os][32:56, :] = pack[...]


def backward_kernel(index, count, near, cot, prev, acc):
    base = (lax.axis_index("curve") - 1) * 32
    acc[...] = jnp.zeros_like(acc)

    def some(step, carry):
        for i in range(UNROLL):
            b = step * UNROLL + i
            cot_t = cot[b].T
            live = count[b]
            for k in range(0, 8, 2):
                pair = jnp.concatenate([near[b, k], near[b, k + 1]], axis=1)
                term = dot(cot_t, pair)
                for j in range(2):
                    row = jnp.where(k + j < live, index[k + j, b] - base, 64)
                    acc[row] += term[:, j * 128 : (j + 1) * 128]
        return carry

    lax.fori_loop(0, near.shape[0] // UNROLL, some, 0)
    prev[...] = acc[0:32].astype(BF16)


def forward_kernel(first, index, count, near, rows, out):
    base = (lax.axis_index("curve") - 1) * 32

    def some(step, carry):
        for i in range(UNROLL):
            n = step * UNROLL + i
            b = first + n
            live = count[b]
            picked = [rows[jnp.where(k < live, index[k, b] - base, 64)] for k in range(8)]
            tiles = jnp.concatenate([near[b, k] for k in range(8)], axis=1)
            out[n] = dot(tiles, jnp.concatenate(picked, axis=0))
        return carry

    lax.fori_loop(0, out.shape[0] // UNROLL, some, 0)


def forward_a_kernel(index, count, near, halo, feat, rows, out):
    rows[0:32] = halo[...]
    rows[32:64] = feat[...]
    rows[64] = jnp.zeros((128, 128), BF16)
    forward_kernel(0, index, count, near, rows, out)


def forward_b_kernel(index, count, near, rows, out):
    forward_kernel(out.shape[0], index, count, near, rows, out)


def place():
    t = lax.axis_index("curve") // QUAD
    return t // ZS, lax.rem(t, ZS)


def spread_kernel(*refs):
    msgs, outs, couple, total, held = refs[:4], refs[4:8], refs[8], refs[9], refs[10]
    me = lax.rem(lax.axis_index("curve"), QUAD)
    value = msgs[0][0:32, :]
    for ref in msgs[1:]:
        value = value + ref[0:32, :]
    fwd = value[0:16].astype(BF16)
    bwd = value[16:32]
    lane = lanes((24, 128))
    for os in range(4):
        total[me ^ os] = msgs[os][32:56, :]
    packed = []
    for a in range(8):
        group = jnp.zeros((24, 128), F32)
        for g in range(4):
            rolled = pltpu.roll(total[g], (16 * (g - a)) % 128, 1)
            group = jnp.where(lane // 16 == g, rolled, group)
        packed.append(group + pltpu.roll(group, 64, 1))
    lane8 = lanes((8, 128))
    for p in range(2):
        quarter = ((lane8 // 16) % 4 + lane8 // 64 + 2 * p) % 4
        wants = [packed[a][16:24].astype(jnp.int32) - quarter for a in range(8)]
        for t in range(32):
            tile = jnp.zeros((16, 128), F32)
            for a in range(8):
                hit = wants[a] == 4 * t
                hit = jnp.concatenate([hit, hit], axis=0)
                tile = tile + jnp.where(hit, packed[a][0:16], 0.0)
            couple[p, t * 16 : (t + 1) * 16, :] = tile
    lane16 = lanes((16, 128))
    block = jnp.concatenate(
        [jnp.where(lane16 // 32 == g, bwd, 0.0) for g in range(4)], axis=0
    )
    contrib = jnp.zeros((512, 128), F32)
    for p in range(2):
        rhs = jnp.concatenate(
            [block if d == 0 else pltpu.roll(block, 32 * d, 1) for d in (2 * p, 2 * p + 1)],
            axis=0,
        )
        r_hi, r_lo = split(rhs)
        k_hi, k_lo = split(couple[p])
        contrib = contrib + (dot(k_hi, r_lo) + dot(k_lo, r_hi)) + dot(k_hi, r_hi)
    held[...] = contrib.astype(BF16)
    y, _ = place()
    for oy in range(4):
        first = pl.multiple_of((y ^ oy) * (ZS * 16), ZS * 16)
        outs[oy][0:16, :] = fwd
        outs[oy][16:144, :] = held[pl.ds(first, ZS * 16), :]


def block16(n):
    return pl.ds(pl.multiple_of(n * 16, 16), 16)


def along_kernel(r0, r1, r2, r3, up, down, mine, held):
    _, z = place()
    seen = (r0, r1, r2, r3)
    total = r0[16:144, :].astype(F32)
    for ref in seen[1:]:
        total = total + ref[16:144, :].astype(F32)
    held[...] = total
    for oy in range(4):
        piece = seen[oy][0:16, :]
        for out in (up, down, mine):
            out[oy * 16 : oy * 16 + 16, :] = piece

    def target(d):
        return held[block16(lax.rem(z + d + ZS, ZS)), :].astype(BF16)

    for n, d in enumerate((2, 3, 4)):
        up[64 + n * 16 : 80 + n * 16, :] = target(d)
    for n, d in enumerate((-3, -2)):
        down[64 + n * 16 : 80 + n * 16, :] = target(d)
    for n, d in enumerate((-1, 0, 1)):
        mine[64 + n * 16 : 80 + n * 16, :] = target(d)


def beside_kernel(mine, low, high, up, down, kept):
    def part(ref, n):
        return ref[64 + n * 16 : 80 + n * 16, :].astype(F32)

    before = part(mine, 0) + part(low, 0)
    here = part(mine, 1) + part(low, 1) + part(high, 0)
    after = part(mine, 2) + part(low, 2) + part(high, 1)
    up[0:64, :] = mine[0:64, :]
    up[64:128, :] = low[0:64, :]
    up[128:192, :] = high[0:64, :]
    up[192:208, :] = after.astype(BF16)
    down[0:64, :] = mine[0:64, :]
    down[64:128, :] = low[0:64, :]
    down[128:144, :] = before.astype(BF16)
    kept[...] = here


def collect_kernel(mine, low, high, prior, later, kept, couple, *refs):
    outs, (picked, source) = refs[:4], refs[4:]
    me = lax.rem(lax.axis_index("curve"), QUAD)
    y, z = place()
    total = kept[...] + prior[192:208, :].astype(F32) + later[128:144, :].astype(F32)
    held = (
        (mine, 0, 0), (low, 0, -3), (high, 0, 3),
        (prior, 0, -1), (prior, 64, -4), (prior, 128, 2),
        (later, 0, 1), (later, 64, -2),
    )
    for ref, first, d in held:
        column = lax.rem(z + d + ZS, ZS)
        for oy in range(4):
            rows = slice(first + oy * 16, first + oy * 16 + 16)
            source[block16((y ^ oy) * ZS + column), :] = ref[rows, :]
    whole_source = source[...]
    over_rows = (((0,), (0,)), ((), ()))
    for p in range(2):
        k_hi, k_lo = split(couple[p])
        picked[p * 128 : (p + 1) * 128, :] = dot(k_hi, whole_source, over_rows) + dot(
            k_lo, whole_source, over_rows
        )
    for os in range(4):
        owner = me ^ os
        far = jnp.zeros((16, 128), F32)
        for d in range(4):
            rows = picked[pl.ds(pl.multiple_of(d * 64 + owner * 16, 16), 16), :]
            far = far + moved(rows, me - owner - d, me)
        outs[os][0:16, :] = far.astype(BF16)
        outs[os][16:32, :] = moved(total, me - owner, me).astype(BF16)


def finish_kernel(
    near_a, near_b, acc, arrived, b_in, b_out, m0, m1, m2, m3, layer, grad, layer_v, grad_v, sems
):
    value = ((m0[...] + m1[...]) + (m2[...] + m3[...])).astype(BF16)
    far = value[0:16]
    coarse_t = value[16:32].astype(F32).T.astype(BF16)
    copies = []
    cut = near_a.shape[0]
    part = 2 * cut // PARTS
    for n in range(PARTS):
        for i in range(n * part, (n + 1) * part):
            near = near_a[i] if i < cut else near_b[i - cut]
            term = dot(b_out[i], far, (((0,), (0,)), ((), ())))
            layer_v[i] = (near + term).astype(BF16)
            total = acc[32 + i] + arrived[i].astype(F32) + dot(coarse_t, b_in[i])
            grad_v[i] = total.astype(BF16).T
        for j, (src, dst) in enumerate(((layer_v, layer), (grad_v, grad))):
            rows = pl.ds(n * part, part)
            copies.append(pltpu.make_async_copy(src.at[rows], dst.at[rows], sems.at[n, j]))
            copies[-1].start()
    for copy in copies:
        copy.wait()


def layer_step(
    features,
    cotangent,
    near_kernel,
    near_index,
    near_count,
    basis_in,
    basis_out,
    far_kernel,
    far_index,
    channel_mix,
):
    groups = lax.axis_size("curve")
    blocks = near_kernel.shape[0]
    places = groups // QUAD
    index = near_index.T
    cube = (blocks, 128, 128)

    halo = lax.ppermute(features, "curve", [(i, i + 1) for i in range(groups - 1)])

    b_out = jnp.swapaxes(basis_out, 1, 2)
    rows32 = jax.ShapeDtypeStruct((32, 128), F32)
    vmem = pl.BlockSpec(memory_space=pltpu.VMEM)
    smem = pl.BlockSpec(memory_space=pltpu.SMEM)
    raw = pl.BlockSpec(memory_space=pl.ANY)
    keep, give, pack, feat_v, cot_v, near_v = pl.pallas_call(
        project_kernel,
        out_shape=[
            rows32,
            rows32,
            jax.ShapeDtypeStruct((24, 128), F32),
            pltpu.VMEM(cube, BF16),
            pltpu.VMEM(cube, BF16),
            pltpu.VMEM(near_kernel.shape, BF16),
        ],
        in_specs=[smem] + [raw] * 7,
        out_specs=[vmem] * 6,
        scratch_shapes=[
            pltpu.VMEM((blocks, 16, 128), BF16),
            pltpu.VMEM((blocks, 16, 128), BF16),
            pltpu.VMEM((256, 256), F32),
            pltpu.VMEM((128, 16), F32),
            pltpu.SemaphoreType.DMA((PARTS + 1, 5)),
        ],
        compiler_params=params(14, None),
        name="project",
    )(
        far_index,
        hbm(features.reshape(cube)),
        hbm(cotangent.reshape(cube)),
        hbm(near_kernel),
        hbm(basis_in),
        hbm(b_out),
        hbm(channel_mix),
        hbm(far_kernel.reshape(128, 16)),
    )
    got = lax.ppermute(give, "chan", [(0, 1), (1, 0)])
    msgs = pl.pallas_call(
        deal_kernel,
        out_shape=[jax.ShapeDtypeStruct((56, 128), F32)] * 4,
        compiler_params=params(8, None),
        name="deal",
    )(keep, got, pack)
    seen = [msgs[0]]
    for o in range(1, 4):
        seen.append(lax.ppermute(msgs[o], "curve", [(i, i ^ o) for i in range(groups)]))

    prev, acc = pl.pallas_call(
        backward_kernel,
        out_shape=[
            jax.ShapeDtypeStruct(cube, BF16),
            pltpu.VMEM((2 * blocks + 1, 128, 128), F32),
        ],
        in_specs=[smem, smem, vmem, vmem],
        out_specs=[vmem, vmem],
        compiler_params=params(14, None),
        cost_estimate=pl.CostEstimate(flops=8 << 30, bytes_accessed=12 << 20, transcendentals=0),
        name="backward",
    )(index, near_count, near_v, cot_v)
    arrived = lax.ppermute(prev, "curve", [(i + 1, i) for i in range(groups - 1)])

    def bf16_rows(n):
        return jax.ShapeDtypeStruct((n, 128), BF16)

    y0, y1, y2, y3, couple = pl.pallas_call(
        spread_kernel,
        out_shape=[bf16_rows(144)] * 4 + [jax.ShapeDtypeStruct((2, places * 16, 128), F32)],
        scratch_shapes=[pltpu.VMEM((4, 24, 128), F32), pltpu.VMEM((places * 16, 128), BF16)],
        compiler_params=params(6, None),
        name="spread",
    )(*seen)
    ways = [y0]
    for o, sent in ((1, y1), (2, y2), (3, y3)):
        pairs = [(i, i ^ (o * ZS * QUAD)) for i in range(groups)]
        ways.append(lax.ppermute(sent, "curve", pairs))

    half_cube = jax.ShapeDtypeStruct((blocks // 2, 128, 128), F32)
    half_cost = pl.CostEstimate(flops=4 << 30, bytes_accessed=6 << 20, transcendentals=0)
    rows, near_a = pl.pallas_call(
        forward_a_kernel,
        out_shape=[
            pltpu.VMEM((2 * blocks + 1, 128, 128), BF16),
            pltpu.VMEM(half_cube.shape, F32),
        ],
        in_specs=[smem, smem, vmem, vmem, vmem],
        out_specs=[vmem, vmem],
        compiler_params=params(6, None),
        cost_estimate=half_cost,
        name="forward_a",
    )(index, near_count, near_v, halo.reshape(cube), feat_v)

    up3, down3, mine = pl.pallas_call(
        along_kernel,
        out_shape=[bf16_rows(112), bf16_rows(96), bf16_rows(112)],
        scratch_shapes=[pltpu.VMEM((ZS * 16, 128), F32)],
        compiler_params=params(6, None),
        name="along",
    )(*ways)

    def turned(value, shift):
        def at(i):
            z = (i // QUAD) % ZS
            return i + ((z + shift) % ZS - z) * QUAD

        return lax.ppermute(value, "curve", [(i, at(i)) for i in range(groups)])

    low = turned(up3, 3)
    high = turned(down3, -3)
    near_b = pl.pallas_call(
        forward_b_kernel,
        out_shape=pltpu.VMEM(half_cube.shape, F32),
        in_specs=[smem, smem, vmem, vmem],
        out_specs=vmem,
        compiler_params=params(6, None),
        cost_estimate=half_cost,
        name="forward_b",
    )(index, near_count, near_v, rows)

    up1, down1, kept = pl.pallas_call(
        beside_kernel,
        out_shape=[bf16_rows(208), bf16_rows(144), jax.ShapeDtypeStruct((16, 128), F32)],
        compiler_params=params(6, None),
        name="beside",
    )(mine, low, high)
    prior = turned(up1, 1)
    later = turned(down1, -1)

    back = pl.pallas_call(
        collect_kernel,
        out_shape=[bf16_rows(32)] * 4,
        scratch_shapes=[pltpu.VMEM((256, 128), F32), pltpu.VMEM((places * 16, 128), BF16)],
        compiler_params=params(6, None),
        name="collect",
    )(mine, low, high, prior, later, kept, couple)
    home = [back[0]]
    for o in range(1, 4):
        home.append(lax.ppermute(back[o], "curve", [(i, i ^ o) for i in range(groups)]))

    layer, grad = pl.pallas_call(
        finish_kernel,
        out_shape=[pltpu.HBM(cube, BF16)] * 2,
        in_specs=[vmem] * 10,
        out_specs=[raw, raw],
        scratch_shapes=[
            pltpu.VMEM(cube, BF16),
            pltpu.VMEM(cube, BF16),
            pltpu.SemaphoreType.DMA((PARTS, 2)),
        ],
        compiler_params=params(14, None),
        name="finish",
    )(near_a, near_b, acc, arrived, basis_in, b_out, *home)
    return (layer.reshape(features.shape), grad.reshape(features.shape))


def solution(mesh):
    return jax.shard_map(
        layer_step,
        mesh=mesh,
        in_specs=(
            P("curve", "chan"),
            P("curve", "chan"),
            P("curve", None, None, None),
            P("curve", None),
            P("curve"),
            P("curve", None, None),
            P("curve", None, None),
            P("curve", None, None, None),
            P("curve", None),
            P(),
        ),
        out_specs=(P("curve", "chan"), P("curve", "chan")),
        check_vma=False,
    )
```

time: 64.4 us -> 78.8 us (1.22)
  the two profiles are of different devices: /device:TPU:25 before, /device:TPU:1 now
where the time goes in v2:
time: 78.8 us; the launch traced here: 78.6 us
  starting transfers between devices  44.2 us (56%)
  Pallas kernels  18.3 us (23%)
  waiting for transfers between devices  14.7 us (19%)
  between operations  0.82 us (1%)
    ppermute x3, starting transfers between devices, layer_step(): lax.ppermute(msgs[o], 'curve', [(i, i ^ o) for i in range(groups)])  14.3 us
    ppermute x4, starting transfers between devices, turned(): return lax.ppermute(value, 'curve', [(i, at(i)) for i in range(groups)])  9.33 us
    ppermute x3, starting transfers between devices, layer_step(): lax.ppermute(back[o], 'curve', [(i, i ^ o) for i in range(groups)])  6.77 us
    ppermute x4, waiting for transfers between devices, turned(): return lax.ppermute(value, 'curve', [(i, at(i)) for i in range(groups)])  5.62 us
    pallas_call x1, Pallas kernels, layer_step(): pl.pallas_call(backward_kernel, out_shape=[jax.ShapeDtypeStruct(cube, BF1...  5.08 us
    pallas_call x1, Pallas kernels, layer_step(): pl.pallas_call(project_kernel, out_shape=[rows32, rows32, jax.ShapeDtypeS...  5.04 us
    ppermute x3, starting transfers between devices, layer_step(): ways.append(lax.ppermute(sent, 'curve', pairs))  4.72 us
    ppermute x1, starting transfers between devices, layer_step(): lax.ppermute(features, 'curve', [(i, i + 1) for i in range(groups - 1)])  4.63 us
  transfers between devices with their start and end apart: 16, of which 7 were waited for; matrix products, arithmetic and copies ran while one was open for 0% of the time, Pallas kernels for 21%

profile of v2, /device:TPU:1, one launch (start us, length us, event | category | flops | bytes accessed | tf_op | source)
XLA Modules:
  0.0 78.6 jit_solution(13822079469241312279)
XLA Ops:
  0.6 0.0 copy-start.4
  0.6 0.0 copy-start.3
  0.7 4.6 %collective-permute-start = (bf16[4096,128]{1,0:T(8,128)(2,1)}, bf16[4096,128]{1,0:T(8,128)(2,1)S(1)}, u32[]{:S(2)}, u32[]{:S(2)}) collective-permute-start(bf16[4096,128]{1,0:T(8,128)(2,1)} %param.10), channel_id=1, source_target_pairs={{0,2},{2,4},{4,6},{6,8},{8,10},{10,12},{12,14},{14,16},{16,18},{18... | collective-permute-start | bytes 3145736 | tf_op jit(solution)/shard_map/ppermute | solution.py:348
  5.3 0.0 copy-start.2
  5.3 0.6 copy-done.2
  5.9 5.0 %project.1 = (f32[32,128]{1,0:T(8,128)S(1)}, f32[32,128]{1,0:T(8,128)S(1)}, f32[24,128]{1,0:T(8,128)S(1)}, bf16[32,128,128]{2,1,0:T(8,128)(2,1)S(1)}, bf16[32,12...) custom-call(s32[1,8]{1,0:T(1,128)S(1)} %copy-done.2, bf16[32,128,128]{2,1,0:T(8,128)(2,1)} %bitcast.15, ...), custom_call_target="tpu_custom_call" | custom-call | tf_op jit(solution)/shard_map/project/pallas_call | solution.py:355
  11.0 0.0 copy-done.4
  11.0 0.0 copy-done.3
  11.0 5.1 %backward.1 = (bf16[32,128,128]{2,1,0:T(8,128)(2,1)S(1)}, f32[65,128,128]{2,1,0:T(8,128)S(1)}) custom-call(s32[8,32]{1,0:T(8,128)S(1)} %bitcast.11, s32[32]{0:T(128)S(1)} %copy-done.4, bf16[32,8,128,128]{3,2,1,0:T(8,128)(2,1)S(1)} %get-tuple-element.33.near, bf16[32,128,128]{2,1,0:T(8,128)(2,1)S(1)} %get-tuple-element.37.cot), custom_call_target="tpu_custom_call" | custom-call | flops 8589934592 | bytes 12582912 | tf_op jit(solution)/shard_map/backward/pallas_call | solution.py:397
  16.1 2.0 %collective-permute-start.1 = (bf16[32,128,128]{2,1,0:T(8,128)(2,1)S(1)}, bf16[32,128,128]{2,1,0:T(8,128)(2,1)S(1)}, u32[]{:S(2)}, u32[]{:S(2)}) collective-permute-start(bf16[32,128,128]{2,1,0:T(8,128)(2,1)S(1)} %get-tuple-element.39), channel_id=1, source_target_pairs={{2,0},{4,2},{6,4},{8,6},{10,8},{12,10},{14,12},{16,14},{18,16},{20... | collective-permute-start | bytes 3145736 | tf_op jit(solution)/shard_map/ppermute | solution.py:409
  18.1 2.5 %collective-permute-start.2 = (f32[32,128]{1,0:T(8,128)S(1)}, f32[32,128]{1,0:T(8,128)S(1)}, u32[]{:S(2)}, u32[]{:S(2)}) collective-permute-start(f32[32,128]{1,0:T(8,128)S(1)} %get-tuple-element.41), channel_id=1, source_target_pairs={{0,1},{1,0},{2,3},{3,2},{4,5},{5,4},{6,7},{7,6},{8,9},{9,8},{10,11... | collective-permute-start | bytes 49160 | tf_op jit(solution)/shard_map/ppermute | solution.py:386
  20.6 1.8 %collective-permute-done.2.got = f32[32,128]{1,0:T(8,128)S(1)} collective-permute-done((f32[32,128]{1,0:T(8,128)S(1)}, f32[32,128]{1,0:T(8,128)S(1)}, u32[]{:S(2)}, u32[]{:S(2)}) %collective-permute-start.2) | collective-permute-done | bytes 16416 | tf_op jit(solution)/shard_map/ppermute | solution.py:386
  22.4 0.1 deal.1
  22.5 0.5 collective-permute-start.3
  23.0 13.7 %collective-permute-start.4 = (f32[56,128]{1,0:T(8,128)S(1)}, f32[56,128]{1,0:T(8,128)S(1)}, u32[]{:S(2)}, u32[]{:S(2)}) collective-permute-start(f32[56,128]{1,0:T(8,128)S(1)} %get-tuple-element.45), channel_id=1, source_target_pairs={{0,4},{2,6},{4,0},{6,2},{8,12},{10,14},{12,8},{14,10},{16,20},{18,... | collective-permute-start | bytes 86024 | tf_op jit(solution)/shard_map/ppermute | solution.py:395
  36.7 0.1 collective-permute-start.5
  36.8 0.0 collective-permute-done.3.refs_1_
  36.8 1.5 %collective-permute-done.4.refs_2_ = f32[56,128]{1,0:T(8,128)S(1)} collective-permute-done((f32[56,128]{1,0:T(8,128)S(1)}, f32[56,128]{1,0:T(8,128)S(1)}, u32[]{:S(2)}, u32[]{:S(2)}) %collective-permute-start.4) | collective-permute-done | bytes 28704 | tf_op jit(solution)/shard_map/ppermute | solution.py:395
  38.3 1.7 %collective-permute-done.5.refs_3_ = f32[56,128]{1,0:T(8,128)S(1)} collective-permute-done((f32[56,128]{1,0:T(8,128)S(1)}, f32[56,128]{1,0:T(8,128)S(1)}, u32[]{:S(2)}, u32[]{:S(2)}) %collective-permute-start.5) | collective-permute-done | bytes 28704 | tf_op jit(solution)/shard_map/ppermute | solution.py:395
  40.0 0.9 %spread.1 = (bf16[144,128]{1,0:T(8,128)(2,1)S(1)}, bf16[144,128]{1,0:T(8,128)(2,1)S(1)}, bf16[144,128]{1,0:T(8,128)(2,1)S(1)}, bf16[144,128]{1,0:T(8,128)(2,1)S(1)}, f32[2,512,128]{2,1,0:T(8,128)S(1)}) custom-call(f32[56,128]{1,0:T(8,128)S(1)} %get-tuple-element.43.refs_0_, f32[56,128]{1,0:T(8,128)S(1)} %collective-permute-done.3.refs_1_, ...), custom_call_target="tpu_custom_call" | custom-call | tf_op jit(solution)/shard_map/spread/pallas_call | solution.py:414
  40.9 2.1 %collective-permute-start.6 = (bf16[144,128]{1,0:T(8,128)(2,1)S(1)}, bf16[144,128]{1,0:T(8,128)(2,1)S(1)}, u32[]{:S(2)}, u32[]{:S(2)}) collective-permute-start(bf16[144,128]{1,0:T(8,128)(2,1)S(1)} %get-tuple-element.48), channel_id=1, source_target_pairs={{0,64},{2,66},{4,68},{6,70},{8,72},{10,74},{12,76},{14,78},{16,80}... | collective-permute-start | bytes 110600 | tf_op jit(solution)/shard_map/ppermute | solution.py:424
  42.9 2.6 %collective-permute-start.7 = (bf16[144,128]{1,0:T(8,128)(2,1)S(1)}, bf16[144,128]{1,0:T(8,128)(2,1)S(1)}, u32[]{:S(2)}, u32[]{:S(2)}) collective-permute-start(bf16[144,128]{1,0:T(8,128)(2,1)S(1)} %get-tuple-element.49), channel_id=1, source_target_pairs={{0,128},{2,130},{4,132},{6,134},{8,136},{10,138},{12,140},{14,142}... | collective-permute-start | bytes 110600 | tf_op jit(solution)/shard_map/ppermute | solution.py:424
  45.6 0.0 collective-permute-start.8
  45.6 0.0 collective-permute-done.6.r1
  45.6 1.7 %collective-permute-done.7.r2 = bf16[144,128]{1,0:T(8,128)(2,1)S(1)} collective-permute-done((bf16[144,128]{1,0:T(8,128)(2,1)S(1)}, bf16[144,128]{1,0:T(8,128)(2,1)S(1)}, u32[]{:S(2)}, u32[]{:S(2)}) %collective-permute-start.7) | collective-permute-done | bytes 36896 | tf_op jit(solution)/shard_map/ppermute | solution.py:424
  47.3 2.3 %collective-permute-done.8.r3 = bf16[144,128]{1,0:T(8,128)(2,1)S(1)} collective-permute-done((bf16[144,128]{1,0:T(8,128)(2,1)S(1)}, bf16[144,128]{1,0:T(8,128)(2,1)S(1)}, u32[]{:S(2)}, u32[]{:S(2)}) %collective-permute-start.8) | collective-permute-done | bytes 36896 | tf_op jit(solution)/shard_map/ppermute | solution.py:424
  49.6 2.3 %collective-permute-start.9 = (bf16[112,128]{1,0:T(8,128)(2,1)S(1)}, bf16[112,128]{1,0:T(8,128)(2,1)S(1)}, u32[]{:S(2)}, u32[]{:S(2)}) collective-permute-start(bf16[112,128]{1,0:T(8,128)(2,1)S(1)} %get-tuple-element.52), channel_id=1, source_target_pairs={{0,24},{2,26},{4,28},{6,30},{8,32},{10,34},{12,36},{14,38},{16,40}... | collective-permute-start | bytes 86024 | tf_op jit(solution)/shard_map/ppermute | solution.py:454
  51.9 3.4 %collective-permute-start.10 = (bf16[96,128]{1,0:T(8,128)(2,1)S(1)}, bf16[96,128]{1,0:T(8,128)(2,1)S(1)}, u32[]{:S(2)}, u32[]{:S(2)}) collective-permute-start(bf16[96,128]{1,0:T(8,128)(2,1)S(1)} %get-tuple-element.53), channel_id=1, source_target_pairs={{0,40},{2,42},{4,44},{6,46},{8,48},{10,50},{12,52},{14,54},{16,56}... | collective-permute-start | bytes 73736 | tf_op jit(solution)/shard_map/ppermute | solution.py:454
  55.3 2.8 %collective-permute-done.10.high = bf16[96,128]{1,0:T(8,128)(2,1)S(1)} collective-permute-done((bf16[96,128]{1,0:T(8,128)(2,1)S(1)}, bf16[96,128]{1,0:T(8,128)(2,1)S(1)}, u32[]{:S(2)}, u32[]{:S(2)}) %collective-permute-start.10) | collective-permute-done | bytes 24608 | tf_op jit(solution)/shard_map/ppermute | solution.py:454
  58.1 0.0 collective-permute-done.9.low
  58.2 3.6 %collective-permute-start.11 = (bf16[208,128]{1,0:T(8,128)(2,1)S(1)}, bf16[208,128]{1,0:T(8,128)(2,1)S(1)}, u32[]{:S(2)}, u32[]{:S(2)}) collective-permute-start(bf16[208,128]{1,0:T(8,128)(2,1)S(1)} %get-tuple-element.54), channel_id=1, source_target_pairs={{0,8},{2,10},{4,12},{6,14},{8,16},{10,18},{12,20},{14,22},{16,24},... | collective-permute-start | bytes 159752 | tf_op jit(solution)/shard_map/ppermute | solution.py:454
  61.8 0.0 collective-permute-start.12
  61.8 2.8 %collective-permute-done.12.later = bf16[144,128]{1,0:T(8,128)(2,1)S(1)} collective-permute-done((bf16[144,128]{1,0:T(8,128)(2,1)S(1)}, bf16[144,128]{1,0:T(8,128)(2,1)S(1)}, u32[]{:S(2)}, u32[]{:S(2)}) %collective-permute-start.12) | collective-permute-done | bytes 36896 | tf_op jit(solution)/shard_map/ppermute | solution.py:454
  64.6 0.0 collective-permute-done.11.prior
  64.6 0.5 collect.1
  65.1 5.0 %collective-permute-start.13 = (bf16[32,128]{1,0:T(8,128)(2,1)S(1)}, bf16[32,128]{1,0:T(8,128)(2,1)S(1)}, u32[]{:S(2)}, u32[]{:S(2)}) collective-permute-start(bf16[32,128]{1,0:T(8,128)(2,1)S(1)} %get-tuple-element.59), channel_id=1, source_target_pairs={{0,2},{2,0},{4,6},{6,4},{8,10},{10,8},{12,14},{14,12},{16,18},{18,... | collective-permute-start | bytes 24584 | tf_op jit(solution)/shard_map/ppermute | solution.py:486
  70.1 1.1 %collective-permute-start.14 = (bf16[32,128]{1,0:T(8,128)(2,1)S(1)}, bf16[32,128]{1,0:T(8,128)(2,1)S(1)}, u32[]{:S(2)}, u32[]{:S(2)}) collective-permute-start(bf16[32,128]{1,0:T(8,128)(2,1)S(1)} %get-tuple-element.60), channel_id=1, source_target_pairs={{0,4},{2,6},{4,0},{6,2},{8,12},{10,14},{12,8},{14,10},{16,20},{18,... | collective-permute-start | bytes 24584 | tf_op jit(solution)/shard_map/ppermute | solution.py:486
  71.3 0.6 collective-permute-start.15
  71.9 0.0 collective-permute-done
  71.9 2.5 %forward_a.1 = (bf16[65,128,128]{2,1,0:T(8,128)(2,1)S(1)}, f32[16,128,128]{2,1,0:T(8,128)S(1)}) custom-call(s32[8,32]{1,0:T(8,128)S(1)} %bitcast.12, s32[32]{0:T(128)S(1)} %copy-done.4, bf16[32,8,128,128]{3,2,1,0:T(8,128)(2,1)S(1)} %get-tuple-element.33.near, bf16[32,128,128]{2,1,0:T(8,128)(2,1)S(1)} %bitcast.10, ...), custom_call_target="tpu_custom_call" | custom-call | flops 4294967296 | bytes 6291456 | tf_op jit(solution)/shard_map/forward_a/pallas_call | solution.py:428
  74.4 0.0 copy-start
  74.4 0.0 copy-start.1
  74.4 2.4 %forward_b.1.near_b = f32[16,128,128]{2,1,0:T(8,128)S(1)} custom-call(s32[8,32]{1,0:T(8,128)S(1)} %bitcast.13, s32[32]{0:T(128)S(1)} %copy-done.4, bf16[32,8,128,128]{3,2,1,0:T(8,128)(2,1)S(1)} %get-tuple-element.33.near, bf16[65,128,128]{2,1,0:T(8,128)(2,1)S(1)} %get-tuple-element.36.rows), custom_call_target="tpu_custom_call" | custom-call | flops 4294967296 | bytes 6291456 | tf_op jit(solution)/shard_map/forward_b/pallas_call | solution.py:458
  76.8 0.0 collective-permute-done.13.m1
  76.8 0.0 collective-permute-done.14.m2
  76.8 0.0 collective-permute-done.15.m3
  76.8 0.0 collective-permute-done.1.arrived
  76.8 0.0 copy-done
  76.8 0.0 copy-done.1
  76.9 1.8 %finish.1 = (bf16[32,128,128]{2,1,0:T(8,128)(2,1)}, bf16[32,128,128]{2,1,0:T(8,128)(2,1)}) custom-call(f32[16,128,128]{2,1,0:T(8,128)S(1)} %get-tuple-element.35.near_a, f32[16,128,128]{2,1,0:T(8,128)S(1)} %forward_b.1.near_b, f32[65,128,128]{2,1,0:T(8,128)S(1)} %get-tuple-element.38.acc, bf16[32,128,128]{2,1,0:T(8,128)(2,1)S(1)} %collective-permute-done.1.arrived, ...), custom_call_target="tpu_custom_call" | custom-call | tf_op jit(solution)/shard_map/finish/pallas_call | solution.py:488
  (2 shorter events, 0.1 us)
Async XLA Ops:
  0.6 10.4 %copy-start.4 = (s32[32]{0:T(128)S(1)}, s32[32]{0:T(128)}, u32[]{:S(2)}) copy-start(s32[32]{0:T(128)} %count.5) | copy-start | bytes 388
  0.6 10.4 %copy-start.3 = (s32[32,8]{0,1:T(8,128)S(1)}, s32[32,8]{0,1:T(8,128)}, u32[]{:S(2)}) copy-start(s32[32,8]{0,1:T(8,128)} %param.13) | copy-start | bytes 3076
  0.7 71.2 %collective-permute-start = (bf16[4096,128]{1,0:T(8,128)(2,1)}, bf16[4096,128]{1,0:T(8,128)(2,1)S(1)}, u32[]{:S(2)}, u32[]{:S(2)}) collective-permute-start(bf16[4096,128]{1,0:T(8,128)(2,1)} %param.10), channel_id=1, source_target_pairs={{0,2},{2,4},{4,6},{6,8},{8,10},{10,12},{12,14},{14,16},{16,18},{18... | collective-permute-start | bytes 3145736 | tf_op jit(solution)/shard_map/ppermute | solution.py:348
  5.3 0.7 copy-start.2
  16.1 60.7 %collective-permute-start.1 = (bf16[32,128,128]{2,1,0:T(8,128)(2,1)S(1)}, bf16[32,128,128]{2,1,0:T(8,128)(2,1)S(1)}, u32[]{:S(2)}, u32[]{:S(2)}) collective-permute-start(bf16[32,128,128]{2,1,0:T(8,128)(2,1)S(1)} %get-tuple-element.39), channel_id=1, source_target_pairs={{2,0},{4,2},{6,4},{8,6},{10,8},{12,10},{14,12},{16,14},{18,16},{20... | collective-permute-start | bytes 3145736 | tf_op jit(solution)/shard_map/ppermute | solution.py:409
  18.1 4.3 %collective-permute-start.2 = (f32[32,128]{1,0:T(8,128)S(1)}, f32[32,128]{1,0:T(8,128)S(1)}, u32[]{:S(2)}, u32[]{:S(2)}) collective-permute-start(f32[32,128]{1,0:T(8,128)S(1)} %get-tuple-element.41), channel_id=1, source_target_pairs={{0,1},{1,0},{2,3},{3,2},{4,5},{5,4},{6,7},{7,6},{8,9},{9,8},{10,11... | collective-permute-start | bytes 49160 | tf_op jit(solution)/shard_map/ppermute | solution.py:386
  22.5 14.3 %collective-permute-start.3 = (f32[56,128]{1,0:T(8,128)S(1)}, f32[56,128]{1,0:T(8,128)S(1)}, u32[]{:S(2)}, u32[]{:S(2)}) collective-permute-start(f32[56,128]{1,0:T(8,128)S(1)} %get-tuple-element.44), channel_id=1, source_target_pairs={{0,2},{2,0},{4,6},{6,4},{8,10},{10,8},{12,14},{14,12},{16,18},{18,... | collective-permute-start | bytes 86024 | tf_op jit(solution)/shard_map/ppermute | solution.py:395
  23.0 15.3 %collective-permute-start.4 = (f32[56,128]{1,0:T(8,128)S(1)}, f32[56,128]{1,0:T(8,128)S(1)}, u32[]{:S(2)}, u32[]{:S(2)}) collective-permute-start(f32[56,128]{1,0:T(8,128)S(1)} %get-tuple-element.45), channel_id=1, source_target_pairs={{0,4},{2,6},{4,0},{6,2},{8,12},{10,14},{12,8},{14,10},{16,20},{18,... | collective-permute-start | bytes 86024 | tf_op jit(solution)/shard_map/ppermute | solution.py:395
  36.7 3.3 %collective-permute-start.5 = (f32[56,128]{1,0:T(8,128)S(1)}, f32[56,128]{1,0:T(8,128)S(1)}, u32[]{:S(2)}, u32[]{:S(2)}) collective-permute-start(f32[56,128]{1,0:T(8,128)S(1)} %get-tuple-element.46), channel_id=1, source_target_pairs={{0,6},{2,4},{4,2},{6,0},{8,14},{10,12},{12,10},{14,8},{16,22},{18,... | collective-permute-start | bytes 86024 | tf_op jit(solution)/shard_map/ppermute | solution.py:395
  40.9 4.7 %collective-permute-start.6 = (bf16[144,128]{1,0:T(8,128)(2,1)S(1)}, bf16[144,128]{1,0:T(8,128)(2,1)S(1)}, u32[]{:S(2)}, u32[]{:S(2)}) collective-permute-start(bf16[144,128]{1,0:T(8,128)(2,1)S(1)} %get-tuple-element.48), channel_id=1, source_target_pairs={{0,64},{2,66},{4,68},{6,70},{8,72},{10,74},{12,76},{14,78},{16,80}... | collective-permute-start | bytes 110600 | tf_op jit(solution)/shard_map/ppermute | solution.py:424
  42.9 4.4 %collective-permute-start.7 = (bf16[144,128]{1,0:T(8,128)(2,1)S(1)}, bf16[144,128]{1,0:T(8,128)(2,1)S(1)}, u32[]{:S(2)}, u32[]{:S(2)}) collective-permute-start(bf16[144,128]{1,0:T(8,128)(2,1)S(1)} %get-tuple-element.49), channel_id=1, source_target_pairs={{0,128},{2,130},{4,132},{6,134},{8,136},{10,138},{12,140},{14,142}... | collective-permute-start | bytes 110600 | tf_op jit(solution)/shard_map/ppermute | solution.py:424
  45.6 4.0 %collective-permute-start.8 = (bf16[144,128]{1,0:T(8,128)(2,1)S(1)}, bf16[144,128]{1,0:T(8,128)(2,1)S(1)}, u32[]{:S(2)}, u32[]{:S(2)}) collective-permute-start(bf16[144,128]{1,0:T(8,128)(2,1)S(1)} %get-tuple-element.50), channel_id=1, source_target_pairs={{0,192},{2,194},{4,196},{6,198},{8,200},{10,202},{12,204},{14,206}... | collective-permute-start | bytes 110600 | tf_op jit(solution)/shard_map/ppermute | solution.py:424
  49.6 8.5 %collective-permute-start.9 = (bf16[112,128]{1,0:T(8,128)(2,1)S(1)}, bf16[112,128]{1,0:T(8,128)(2,1)S(1)}, u32[]{:S(2)}, u32[]{:S(2)}) collective-permute-start(bf16[112,128]{1,0:T(8,128)(2,1)S(1)} %get-tuple-element.52), channel_id=1, source_target_pairs={{0,24},{2,26},{4,28},{6,30},{8,32},{10,34},{12,36},{14,38},{16,40}... | collective-permute-start | bytes 86024 | tf_op jit(solution)/shard_map/ppermute | solution.py:454
  51.9 6.2 %collective-permute-start.10 = (bf16[96,128]{1,0:T(8,128)(2,1)S(1)}, bf16[96,128]{1,0:T(8,128)(2,1)S(1)}, u32[]{:S(2)}, u32[]{:S(2)}) collective-permute-start(bf16[96,128]{1,0:T(8,128)(2,1)S(1)} %get-tuple-element.53), channel_id=1, source_target_pairs={{0,40},{2,42},{4,44},{6,46},{8,48},{10,50},{12,52},{14,54},{16,56}... | collective-permute-start | bytes 73736 | tf_op jit(solution)/shard_map/ppermute | solution.py:454
  58.2 6.4 %collective-permute-start.11 = (bf16[208,128]{1,0:T(8,128)(2,1)S(1)}, bf16[208,128]{1,0:T(8,128)(2,1)S(1)}, u32[]{:S(2)}, u32[]{:S(2)}) collective-permute-start(bf16[208,128]{1,0:T(8,128)(2,1)S(1)} %get-tuple-element.54), channel_id=1, source_target_pairs={{0,8},{2,10},{4,12},{6,14},{8,16},{10,18},{12,20},{14,22},{16,24},... | collective-permute-start | bytes 159752 | tf_op jit(solution)/shard_map/ppermute | solution.py:454
  61.8 2.8 %collective-permute-start.12 = (bf16[144,128]{1,0:T(8,128)(2,1)S(1)}, bf16[144,128]{1,0:T(8,128)(2,1)S(1)}, u32[]{:S(2)}, u32[]{:S(2)}) collective-permute-start(bf16[144,128]{1,0:T(8,128)(2,1)S(1)} %get-tuple-element.55), channel_id=1, source_target_pairs={{0,56},{2,58},{4,60},{6,62},{8,0},{10,2},{12,4},{14,6},{16,8},{18,... | collective-permute-start | bytes 110600 | tf_op jit(solution)/shard_map/ppermute | solution.py:454
  65.1 11.7 %collective-permute-start.13 = (bf16[32,128]{1,0:T(8,128)(2,1)S(1)}, bf16[32,128]{1,0:T(8,128)(2,1)S(1)}, u32[]{:S(2)}, u32[]{:S(2)}) collective-permute-start(bf16[32,128]{1,0:T(8,128)(2,1)S(1)} %get-tuple-element.59), channel_id=1, source_target_pairs={{0,2},{2,0},{4,6},{6,4},{8,10},{10,8},{12,14},{14,12},{16,18},{18,... | collective-permute-start | bytes 24584 | tf_op jit(solution)/shard_map/ppermute | solution.py:486
  70.1 6.7 %collective-permute-start.14 = (bf16[32,128]{1,0:T(8,128)(2,1)S(1)}, bf16[32,128]{1,0:T(8,128)(2,1)S(1)}, u32[]{:S(2)}, u32[]{:S(2)}) collective-permute-start(bf16[32,128]{1,0:T(8,128)(2,1)S(1)} %get-tuple-element.60), channel_id=1, source_target_pairs={{0,4},{2,6},{4,0},{6,2},{8,12},{10,14},{12,8},{14,10},{16,20},{18,... | collective-permute-start | bytes 24584 | tf_op jit(solution)/shard_map/ppermute | solution.py:486
  71.3 5.6 %collective-permute-start.15 = (bf16[32,128]{1,0:T(8,128)(2,1)S(1)}, bf16[32,128]{1,0:T(8,128)(2,1)S(1)}, u32[]{:S(2)}, u32[]{:S(2)}) collective-permute-start(bf16[32,128]{1,0:T(8,128)(2,1)S(1)} %get-tuple-element.61), channel_id=1, source_target_pairs={{0,6},{2,4},{4,2},{6,0},{8,14},{10,12},{12,10},{14,8},{16,22},{18,... | collective-permute-start | bytes 24584 | tf_op jit(solution)/shard_map/ppermute | solution.py:486
  74.4 2.5 %copy-start = (bf16[32,16,128]{2,1,0:T(8,128)(2,1)S(1)}, bf16[32,16,128]{2,1,0:T(8,128)(2,1)}, u32[]{:S(2)}) copy-start(bf16[32,16,128]{2,1,0:T(8,128)(2,1)} %b_in.3) | copy-start | bytes 393220
  74.4 2.5 %copy-start.1 = (bf16[32,128,16]{1,2,0:T(8,128)(2,1)S(1)}, bf16[32,128,16]{1,2,0:T(8,128)(2,1)}, u32[]{:S(2)}) copy-start(bf16[32,128,16]{1,2,0:T(8,128)(2,1)} %param.16) | copy-start | bytes 393220

commit v3 on v2

v3 whole, which is shorter than its diff:
```python
import jax
import jax.numpy as jnp
from jax import lax
from jax.experimental import pallas as pl
from jax.experimental.pallas import tpu as pltpu
from jax.sharding import PartitionSpec as P


F32 = jnp.float32
BF16 = jnp.bfloat16
MIB = 1 << 20
QUAD = 4
PARTS = 4
CHUNKS = 4
UNROLL = 4


def params(mib, semantics=("arbitrary",)):
    return pltpu.CompilerParams(dimension_semantics=semantics, vmem_limit_bytes=mib * MIB)


def dot(a, b, dims=(((1,), (0,)), ((), ()))):
    return lax.dot_general(a, b, dims, preferred_element_type=F32)


def split(value):
    high = value.astype(BF16)
    return high, (value - high.astype(F32)).astype(BF16)


def hbm(value):
    return pltpu.with_memory_space_constraint(value, pltpu.HBM)


def lanes(shape):
    return lax.broadcasted_iota(jnp.int32, shape, 1)


def moved(value, block, keep):
    rolled = pltpu.roll(value, lax.rem(block * 32 + 256, 128), 1)
    return jnp.where(lanes(value.shape) // 32 == keep, rolled, 0.0)


def project_kernel(feat, cot, b_in, b_out, mix, keep, give, cot_v, feat_v, b_in_v, b_out_v, mix_v, sems):
    count = feat.shape[0]
    part = count // PARTS
    loads = []
    for n in range(PARTS):
        rows = pl.ds(n * part, part)
        loads.append(
            [
                pltpu.make_async_copy(src.at[rows], dst.at[rows], sems.at[n, j])
                for j, (src, dst) in enumerate(
                    ((feat, feat_v), (b_in, b_in_v), (cot, cot_v), (b_out, b_out_v))
                )
            ]
        )
    last = pltpu.make_async_copy(mix, mix_v, sems.at[PARTS, 0])
    for copy in [c for group in loads for c in group] + [last]:
        copy.start()

    acc_f = jnp.zeros((16, 128), F32)
    acc_b = jnp.zeros((16, 128), F32)
    for n in range(PARTS):
        for copy in loads[n]:
            copy.wait()
        picks = range(n * part, (n + 1) * part)
        acc_f += dot(
            jnp.concatenate([b_in_v[i] for i in picks], axis=1),
            feat_v[n * part : (n + 1) * part].reshape(part * 128, 128),
        )
        acc_b += dot(
            jnp.concatenate([b_out_v[i] for i in picks], axis=1),
            cot_v[n * part : (n + 1) * part].reshape(part * 128, 128),
        )
    last.wait()
    half = lax.axis_index("chan")
    start = pl.multiple_of(half * 128, 128)
    exact = lax.Precision.HIGHEST
    coarse = acc_f.astype(BF16).astype(F32)
    for oh, out in enumerate((keep, give)):
        there = pl.multiple_of((half ^ oh) * 128, 128)
        out[0:16, :] = jnp.dot(
            coarse,
            mix_v[pl.ds(start, 128), pl.ds(there, 128)],
            precision=exact,
            preferred_element_type=F32,
        )
        out[16:32, :] = lax.dot_general(
            acc_b,
            mix_v[pl.ds(there, 128), pl.ds(start, 128)],
            (((1,), (1,)), ((), ())),
            precision=exact,
            preferred_element_type=F32,
        )


def deal_kernel(far_index, far, keep, got, *outs):
    me = lax.rem(lax.axis_index("curve"), QUAD)
    both = keep[...] + got[...]
    wide = jnp.concatenate([far[...], jnp.zeros((128, 112), F32)], axis=1)
    pack = wide.T[0:16]
    lane = lanes((8, 128)) // 16
    row = jnp.zeros((8, 128), jnp.int32)
    for a in range(8):
        row = jnp.where(lane == a, far_index[0, a], row)
    for os in range(4):
        outs[os][0:32, :] = moved(both, me - (me ^ os), me)
        outs[os][32:48, :] = pack
        outs[os][48:56, :] = row.astype(F32)


def tile_loads(near, near_v, sems):
    part = near.shape[0] // CHUNKS
    copies = []
    for n in range(CHUNKS):
        rows = pl.ds(n * part, part)
        copies.append(pltpu.make_async_copy(near.at[rows], near_v.at[rows], sems.at[n]))
        copies[-1].start()
    return copies


def backward_kernel(index, count, near, cot, prev, acc, near_v, sems):
    base = (lax.axis_index("curve") - 1) * 32
    copies = tile_loads(near, near_v, sems)
    acc[...] = jnp.zeros_like(acc)
    part = near.shape[0] // CHUNKS
    for n, copy in enumerate(copies):
        copy.wait()

        def some(step, carry):
            for i in range(UNROLL):
                b = n * part + step * UNROLL + i
                cot_t = cot[b].T
                live = count[b]
                for k in range(0, 8, 2):
                    pair = jnp.concatenate([near_v[b, k], near_v[b, k + 1]], axis=1)
                    term = dot(cot_t, pair)
                    for j in range(2):
                        row = jnp.where(k + j < live, index[k + j, b] - base, 64)
                        acc[row] += term[:, j * 128 : (j + 1) * 128]
            return carry

        lax.fori_loop(0, part // UNROLL, some, 0)
    prev[...] = acc[0:32].astype(BF16)


def forward_kernel(index, count, near, halo, feat, out, rows, near_v, out_v, sems, row_sems, out_sems):
    base = (lax.axis_index("curve") - 1) * 32
    heads = [
        pltpu.make_async_copy(feat, rows.at[pl.ds(32, 32)], row_sems.at[0]),
        pltpu.make_async_copy(halo, rows.at[pl.ds(0, 32)], row_sems.at[1]),
    ]
    for copy in heads:
        copy.start()
    copies = tile_loads(near, near_v, sems)
    rows[64] = jnp.zeros((128, 128), BF16)
    for copy in heads:
        copy.wait()
    part = near.shape[0] // CHUNKS
    stores = []
    for n, copy in enumerate(copies):
        copy.wait()

        def some(step, carry):
            for i in range(UNROLL):
                b = n * part + step * UNROLL + i
                live = count[b]
                picked = [rows[jnp.where(k < live, index[k, b] - base, 64)] for k in range(8)]
                tiles = jnp.concatenate([near_v[b, k] for k in range(8)], axis=1)
                out_v[b] = dot(tiles, jnp.concatenate(picked, axis=0))
            return carry

        lax.fori_loop(0, part // UNROLL, some, 0)
        span = pl.ds(n * part, part)
        stores.append(pltpu.make_async_copy(out_v.at[span], out.at[span], out_sems.at[n]))
        stores[-1].start()
    for copy in stores:
        copy.wait()


def spread_kernel(*refs):
    msgs, acc, (out, couple, own), total, sem = refs[:4], refs[4], refs[5:8], refs[8], refs[9]
    saved = pltpu.make_async_copy(acc.at[pl.ds(32, 32)], own, sem)
    saved.start()
    me = lax.rem(lax.axis_index("curve"), QUAD)
    value = msgs[0][0:32, :]
    for ref in msgs[1:]:
        value = value + ref[0:32, :]
    fwd = value[0:16].astype(BF16)
    bwd = value[16:32]
    lane = lanes((24, 128))
    for os in range(4):
        total[me ^ os] = msgs[os][32:56, :]
    packed = []
    for a in range(8):
        group = jnp.zeros((24, 128), F32)
        for g in range(4):
            rolled = pltpu.roll(total[g], (16 * (g - a)) % 128, 1)
            group = jnp.where(lane // 16 == g, rolled, group)
        packed.append(group + pltpu.roll(group, 64, 1))
    lane8 = lanes((8, 128))
    for p in range(2):
        quarter = ((lane8 // 16) % 4 + lane8 // 64 + 2 * p) % 4
        wants = [packed[a][16:24].astype(jnp.int32) - quarter for a in range(8)]
        for t in range(32):
            tile = jnp.zeros((16, 128), F32)
            for a in range(8):
                hit = wants[a] == 4 * t
                hit = jnp.concatenate([hit, hit], axis=0)
                tile = tile + jnp.where(hit, packed[a][0:16], 0.0)
            couple[p, t * 16 : (t + 1) * 16, :] = tile
    lane16 = lanes((16, 128))
    block = jnp.concatenate(
        [jnp.where(lane16 // 32 == g, bwd, 0.0) for g in range(4)], axis=0
    )
    contrib = jnp.zeros((512, 128), F32)
    for p in range(2):
        rhs = jnp.concatenate(
            [block if d == 0 else pltpu.roll(block, 32 * d, 1) for d in (2 * p, 2 * p + 1)],
            axis=0,
        )
        r_hi, r_lo = split(rhs)
        k_hi, k_lo = split(couple[p])
        contrib = contrib + (dot(k_hi, r_lo) + dot(k_lo, r_hi)) + dot(k_hi, r_hi)
    contrib = contrib.astype(BF16)
    for t in range(32):
        out[t, 0:16, :] = fwd
        out[t, 16:32, :] = contrib[t * 16 : (t + 1) * 16]
    saved.wait()


def collect_kernel(arrived, couple, *refs):
    outs, (picked, summed) = refs[:4], refs[4:]
    me = lax.rem(lax.axis_index("curve"), QUAD)
    total = arrived[0, 16:32, :].astype(F32)
    for t in range(1, 32):
        total = total + arrived[t, 16:32, :].astype(F32)
    source = jnp.concatenate([arrived[t, 0:16, :] for t in range(32)], axis=0)
    over_rows = (((0,), (0,)), ((), ()))
    for p in range(2):
        k_hi, k_lo = split(couple[p])
        picked[p * 128 : (p + 1) * 128, :] = dot(k_hi, source, over_rows) + dot(
            k_lo, source, over_rows
        )
    for os in range(4):
        owner = me ^ os
        far = jnp.zeros((16, 128), F32)
        for d in range(4):
            rows = picked[pl.ds(pl.multiple_of(d * 64 + owner * 16, 16), 16), :]
            far = far + moved(rows, me - owner - d, me)
        outs[os][0:16, :] = far.astype(BF16)
        outs[os][16:32, :] = moved(total, me - owner, me).astype(BF16)


def fetch_kernel(near, own, near_v, own_v, sems):
    copies = [
        pltpu.make_async_copy(near, near_v, sems.at[0]),
        pltpu.make_async_copy(own, own_v, sems.at[1]),
    ]
    for copy in copies:
        copy.start()
    for copy in copies:
        copy.wait()


def finish_kernel(
    near, own, arrived, b_in, b_out, m0, m1, m2, m3, layer, grad, layer_v, grad_v, sems
):
    value = ((m0[...] + m1[...]) + (m2[...] + m3[...])).astype(BF16)
    far = value[0:16]
    coarse_t = value[16:32].astype(F32).T.astype(BF16)
    copies = []
    part = near.shape[0] // PARTS
    for n in range(PARTS):
        for i in range(n * part, (n + 1) * part):
            term = dot(b_out[i], far, (((0,), (0,)), ((), ())))
            layer_v[i] = (near[i] + term).astype(BF16)
            total = own[i] + arrived[i].astype(F32) + dot(coarse_t, b_in[i])
            grad_v[i] = total.astype(BF16).T
        for j, (src, dst) in enumerate(((layer_v, layer), (grad_v, grad))):
            rows = pl.ds(n * part, part)
            copies.append(pltpu.make_async_copy(src.at[rows], dst.at[rows], sems.at[n, j]))
            copies[-1].start()
    for copy in copies:
        copy.wait()


def layer_step(
    features,
    cotangent,
    near_kernel,
    near_index,
    near_count,
    basis_in,
    basis_out,
    far_kernel,
    far_index,
    channel_mix,
):
    groups = lax.axis_size("curve")
    blocks = near_kernel.shape[0]
    places = groups // QUAD
    index = near_index.T
    cube = (blocks, 128, 128)

    halo = lax.ppermute(features, "curve", [(i, i + 1) for i in range(groups - 1)])

    b_out = jnp.swapaxes(basis_out, 1, 2)
    rows32 = jax.ShapeDtypeStruct((32, 128), F32)
    vmem = pl.BlockSpec(memory_space=pltpu.VMEM)
    smem = pl.BlockSpec(memory_space=pltpu.SMEM)
    raw = pl.BlockSpec(memory_space=pl.ANY)
    keep, give, cot_v = pl.pallas_call(
        project_kernel,
        out_shape=[rows32, rows32, pltpu.VMEM(cube, BF16)],
        in_specs=[raw] * 5,
        out_specs=[vmem] * 3,
        scratch_shapes=[
            pltpu.VMEM(cube, BF16),
            pltpu.VMEM((blocks, 16, 128), BF16),
            pltpu.VMEM((blocks, 16, 128), BF16),
            pltpu.VMEM((256, 256), F32),
            pltpu.SemaphoreType.DMA((PARTS + 1, 4)),
        ],
        compiler_params=params(14, None),
        name="project",
    )(
        hbm(features.reshape(cube)),
        hbm(cotangent.reshape(cube)),
        hbm(basis_in),
        hbm(b_out),
        hbm(channel_mix),
    )
    got = lax.ppermute(give, "chan", [(0, 1), (1, 0)])
    msgs = pl.pallas_call(
        deal_kernel,
        out_shape=[jax.ShapeDtypeStruct((56, 128), F32)] * 4,
        in_specs=[smem, vmem, vmem, vmem],
        compiler_params=params(6, None),
        name="deal",
    )(far_index, far_kernel.reshape(128, 16), keep, got)
    seen = [msgs[0]]
    for o in range(1, 4):
        seen.append(lax.ppermute(msgs[o], "curve", [(i, i ^ o) for i in range(groups)]))

    prev, acc = pl.pallas_call(
        backward_kernel,
        out_shape=[
            jax.ShapeDtypeStruct(cube, BF16),
            pltpu.VMEM((2 * blocks + 1, 128, 128), F32),
        ],
        in_specs=[smem, smem, raw, vmem],
        out_specs=[vmem, vmem],
        scratch_shapes=[pltpu.VMEM(near_kernel.shape, BF16), pltpu.SemaphoreType.DMA((CHUNKS,))],
        compiler_params=params(16, None),
        cost_estimate=pl.CostEstimate(flops=8 << 30, bytes_accessed=12 << 20, transcendentals=0),
        name="backward",
    )(index, near_count, hbm(near_kernel), cot_v)
    arrived = lax.ppermute(prev, "curve", [(i + 1, i) for i in range(groups - 1)])

    out_msg, couple, own = pl.pallas_call(
        spread_kernel,
        out_shape=[
            jax.ShapeDtypeStruct((places, 32, 128), BF16),
            pltpu.HBM((2, places * 16, 128), F32),
            pltpu.HBM(cube, F32),
        ],
        in_specs=[vmem] * 5,
        out_specs=[vmem, vmem, raw],
        scratch_shapes=[pltpu.VMEM((4, 24, 128), F32), pltpu.SemaphoreType.DMA],
        compiler_params=params(6, None),
        name="spread",
    )(*seen, acc)
    rings = [[t * QUAD + s for t in range(places)] for s in range(QUAD)]
    in_msg = lax.all_to_all(out_msg, "curve", 0, 0, tiled=True, axis_index_groups=rings)

    near = pl.pallas_call(
        forward_kernel,
        out_shape=pltpu.HBM(cube, F32),
        in_specs=[smem, smem, raw, raw, raw],
        out_specs=raw,
        scratch_shapes=[
            pltpu.VMEM((2 * blocks + 1, 128, 128), BF16),
            pltpu.VMEM(near_kernel.shape, BF16),
            pltpu.VMEM(cube, F32),
            pltpu.SemaphoreType.DMA((CHUNKS,)),
            pltpu.SemaphoreType.DMA((2,)),
            pltpu.SemaphoreType.DMA((CHUNKS,)),
        ],
        compiler_params=params(16, None),
        cost_estimate=pl.CostEstimate(flops=8 << 30, bytes_accessed=12 << 20, transcendentals=0),
        name="forward",
    )(index, near_count, hbm(near_kernel), hbm(halo.reshape(cube)), hbm(features.reshape(cube)))

    back = pl.pallas_call(
        collect_kernel,
        out_shape=[jax.ShapeDtypeStruct((32, 128), BF16)] * 4,
        scratch_shapes=[pltpu.VMEM((256, 128), F32), pltpu.VMEM((16, 128), F32)],
        compiler_params=params(6, None),
        name="collect",
    )(in_msg, couple)
    near_back, own_back = pl.pallas_call(
        fetch_kernel,
        out_shape=[pltpu.VMEM(cube, F32)] * 2,
        in_specs=[raw, raw],
        out_specs=[vmem, vmem],
        scratch_shapes=[pltpu.SemaphoreType.DMA((2,))],
        compiler_params=params(6, None),
        cost_estimate=pl.CostEstimate(flops=1 << 20, bytes_accessed=8 << 20, transcendentals=0),
        name="fetch",
    )(hbm(near), hbm(own))
    home = [back[0]]
    for o in range(1, 4):
        home.append(lax.ppermute(back[o], "curve", [(i, i ^ o) for i in range(groups)]))

    layer, grad = pl.pallas_call(
        finish_kernel,
        out_shape=[pltpu.HBM(cube, BF16)] * 2,
        in_specs=[vmem] * 9,
        out_specs=[raw, raw],
        scratch_shapes=[
            pltpu.VMEM(cube, BF16),
            pltpu.VMEM(cube, BF16),
            pltpu.SemaphoreType.DMA((PARTS, 2)),
        ],
        compiler_params=params(14, None),
        name="finish",
    )(near_back, own_back, arrived, basis_in, b_out, *home)
    return (layer.reshape(features.shape), grad.reshape(features.shape))


def solution(mesh):
    return jax.shard_map(
        layer_step,
        mesh=mesh,
        in_specs=(
            P("curve", "chan"),
            P("curve", "chan"),
            P("curve", None, None, None),
            P("curve", None),
            P("curve"),
            P("curve", None, None),
            P("curve", None, None),
            P("curve", None, None, None),
            P("curve", None),
            P(),
        ),
        out_specs=(P("curve", "chan"), P("curve", "chan")),
        check_vma=False,
    )
```

time: 78.8 us -> 68.7 us (0.87)
  starting transfers between devices: 44.2 us -> 28.5 us
  Pallas kernels: 18.3 us -> 24.1 us
  waiting for transfers between devices: 14.7 us -> 13.9 us
    ppermute x7 -> x0, starting transfers between devices: 14 us -> none  [the longest x4 9.33 us: turned(): return lax.ppermute(value, 'curve', [(i, at(i)) for i in range(groups)])]
    ppermute x3, starting transfers between devices: 14.3 us -> 3.61 us  [layer_step(): lax.ppermute(msgs[o], 'curve', [(i, i ^ o) for i in range(groups)])]
    all_to_all x0 -> x1, starting transfers between devices: none -> 10 us  [layer_step(): lax.all_to_all(out_msg, 'curve', 0, 0, tiled=True, axis_index_groups=rings)]
    ppermute x7 -> x0, waiting for transfers between devices: 9.63 us -> none  [the longest x4 5.62 us: turned(): return lax.ppermute(value, 'curve', [(i, at(i)) for i in range(groups)])]
    all_to_all x0 -> x1, waiting for transfers between devices: none -> 7.08 us  [layer_step(): lax.all_to_all(out_msg, 'curve', 0, 0, tiled=True, axis_index_groups=rings)]
    pallas_call x7 -> x5, Pallas kernels: 11.3 us -> 15.2 us  [the longest x1 7.72 us: layer_step(): pl.pallas_call(forward_kernel, out_shape=pltpu.HBM(cube, F32), in_specs=[...]
    ppermute x3, waiting for transfers between devices: 3.21 us -> 6.83 us  [layer_step(): lax.ppermute(msgs[o], 'curve', [(i, i ^ o) for i in range(groups)])]
    ppermute x1, waiting for transfers between devices: 1.82 us -> 0.01 us  [layer_step(): got = lax.ppermute(give, 'chan', [(0, 1), (1, 0)])]
  transfers between devices with their start and end apart: 16 -> 10, of which waited for: 7 -> 3; matrix products, arithmetic and copies ran while one was open for 0% -> 0% of each run, Pallas kernels for 21% -> 29%
where the time goes in v3:
time: 68.7 us; the launch traced here: 68.4 us
  starting transfers between devices  28.5 us (41%)
  Pallas kernels  24.1 us (35%)
  waiting for transfers between devices  13.9 us (20%)
  local copies, waits for them, and re-layouts  1.08 us (2%)
  between operations  0.85 us (1%)
    all_to_all x1, starting transfers between devices, layer_step(): lax.all_to_all(out_msg, 'curve', 0, 0, tiled=True, axis_index_groups=rings)  10 us
    pallas_call x1, Pallas kernels, layer_step(): pl.pallas_call(forward_kernel, out_shape=pltpu.HBM(cube, F32), in_specs=[...  7.72 us
    all_to_all x1, waiting for transfers between devices, layer_step(): lax.all_to_all(out_msg, 'curve', 0, 0, tiled=True, axis_index_groups=rings)  7.08 us
    ppermute x3, waiting for transfers between devices, layer_step(): lax.ppermute(msgs[o], 'curve', [(i, i ^ o) for i in range(groups)])  6.83 us
    pallas_call x1, Pallas kernels, layer_step(): pl.pallas_call(backward_kernel, out_shape=[jax.ShapeDtypeStruct(cube, BF1...  6.46 us
    ppermute x3, starting transfers between devices, layer_step(): lax.ppermute(back[o], 'curve', [(i, i ^ o) for i in range(groups)])  5.52 us
    ppermute x1, starting transfers between devices, layer_step(): got = lax.ppermute(give, 'chan', [(0, 1), (1, 0)])  3.65 us
    ppermute x3, starting transfers between devices, layer_step(): lax.ppermute(msgs[o], 'curve', [(i, i ^ o) for i in range(groups)])  3.61 us
  transfers between devices with their start and end apart: 10, of which 3 were waited for; matrix products, arithmetic and copies ran while one was open for 0% of the time, Pallas kernels for 29%

profile of v3, /device:TPU:1, one launch (start us, length us, event | category | flops | bytes accessed | tf_op | source)
XLA Modules:
  0.0 68.4 jit_solution(694356799030404028)
XLA Ops:
  0.6 0.0 copy-start.7
  0.6 0.0 copy-start.3
  0.7 0.0 copy-start.4
  0.7 0.0 copy-start.5
  0.7 0.0 copy-start.6
  0.7 2.6 %project.1 = (f32[32,128]{1,0:T(8,128)S(1)}, f32[32,128]{1,0:T(8,128)S(1)}, bf16[32,128,128]{2,1,0:T(8,128)(2,1)S(1)}) custom-call(bf16[32,128,128]{2,1,0:T(8,128)(2,1)} %bitcast.14, bf16[32,128,128]{2,1,0:T(8,128)(2,1)} %bitcast.13, bf16[32,16,128]{2,1,0:T(8,128)(2,1)} %b_in.3, bf16[32,16,128]{2,1,0:T(8,128)(2,1)} %bitcast.8, f32[256,256]{1,0:T(8,128)} %mix.1), custom_call_target="tpu_custom_call" | custom-call | tf_op jit(solution)/shard_map/project/pallas_call | solution.py:314
  3.3 3.6 %collective-permute-start.1 = (f32[32,128]{1,0:T(8,128)S(1)}, f32[32,128]{1,0:T(8,128)S(1)}, u32[]{:S(2)}, u32[]{:S(2)}) collective-permute-start(f32[32,128]{1,0:T(8,128)S(1)} %get-tuple-element.23), channel_id=1, source_target_pairs={{0,1},{1,0},{2,3},{3,2},{4,5},{5,4},{6,7},{7,6},{8,9},{9,8},{10,11... | collective-permute-start | bytes 49160 | tf_op jit(solution)/shard_map/ppermute | solution.py:335
  6.9 0.0 copy-done.7
  6.9 3.1 %collective-permute-start = (bf16[4096,128]{1,0:T(8,128)(2,1)S(1)}, bf16[4096,128]{1,0:T(8,128)(2,1)}, u32[]{:S(2)}, u32[]{:S(2)}) collective-permute-start(bf16[4096,128]{1,0:T(8,128)(2,1)S(1)} %copy-done.7), channel_id=1, source_target_pairs={{0,2},{2,4},{4,6},{6,8},{8,10},{10,12},{12,14},{14,16},{16,18},{18... | collective-permute-start | bytes 3145736 | tf_op jit(solution)/shard_map/ppermute | solution.py:307
  10.0 0.0 collective-permute-done.1.got
  10.0 0.0 copy-done.3
  10.0 0.0 copy-done.4
  10.0 0.6 deal.1
  10.6 1.9 %collective-permute-start.2 = (f32[56,128]{1,0:T(8,128)S(1)}, f32[56,128]{1,0:T(8,128)S(1)}, u32[]{:S(2)}, u32[]{:S(2)}) collective-permute-start(f32[56,128]{1,0:T(8,128)S(1)} %get-tuple-element.25), channel_id=1, source_target_pairs={{0,2},{2,0},{4,6},{6,4},{8,10},{10,8},{12,14},{14,12},{16,18},{18,... | collective-permute-start | bytes 86024 | tf_op jit(solution)/shard_map/ppermute | solution.py:345
  12.5 0.8 %collective-permute-start.3 = (f32[56,128]{1,0:T(8,128)S(1)}, f32[56,128]{1,0:T(8,128)S(1)}, u32[]{:S(2)}, u32[]{:S(2)}) collective-permute-start(f32[56,128]{1,0:T(8,128)S(1)} %get-tuple-element.26), channel_id=1, source_target_pairs={{0,4},{2,6},{4,0},{6,2},{8,12},{10,14},{12,8},{14,10},{16,20},{18,... | collective-permute-start | bytes 86024 | tf_op jit(solution)/shard_map/ppermute | solution.py:345
  13.3 0.9 %collective-permute-start.4 = (f32[56,128]{1,0:T(8,128)S(1)}, f32[56,128]{1,0:T(8,128)S(1)}, u32[]{:S(2)}, u32[]{:S(2)}) collective-permute-start(f32[56,128]{1,0:T(8,128)S(1)} %get-tuple-element.27), channel_id=1, source_target_pairs={{0,6},{2,4},{4,2},{6,0},{8,14},{10,12},{12,10},{14,8},{16,22},{18,... | collective-permute-start | bytes 86024 | tf_op jit(solution)/shard_map/ppermute | solution.py:345
  14.3 0.0 copy-done.5
  14.3 0.0 copy-done.6
  14.3 6.5 %backward.1 = (bf16[32,128,128]{2,1,0:T(8,128)(2,1)S(1)}, f32[65,128,128]{2,1,0:T(8,128)S(1)}) custom-call(s32[8,32]{1,0:T(8,128)S(1)} %bitcast.11, s32[32]{0:T(128)S(1)} %copy-done.6, bf16[32,8,128,128]{3,2,1,0:T(8,128)(2,1)} %near.3, bf16[32,128,128]{2,1,0:T(8,128)(2,1)S(1)} %get-tuple-element.28.cot), custom_call_target="tpu_custom_call" | custom-call | flops 8589934592 | bytes 12582912 | tf_op jit(solution)/shard_map/backward/pallas_call | solution.py:347
  20.7 0.0 collective-permute-done.2.refs_1_
  20.7 1.9 %collective-permute-done.3.refs_2_ = f32[56,128]{1,0:T(8,128)S(1)} collective-permute-done((f32[56,128]{1,0:T(8,128)S(1)}, f32[56,128]{1,0:T(8,128)S(1)}, u32[]{:S(2)}, u32[]{:S(2)}) %collective-permute-start.3) | collective-permute-done | bytes 28704 | tf_op jit(solution)/shard_map/ppermute | solution.py:345
  22.6 5.0 %collective-permute-done.4.refs_3_ = f32[56,128]{1,0:T(8,128)S(1)} collective-permute-done((f32[56,128]{1,0:T(8,128)S(1)}, f32[56,128]{1,0:T(8,128)S(1)}, u32[]{:S(2)}, u32[]{:S(2)}) %collective-permute-start.4) | collective-permute-done | bytes 28704 | tf_op jit(solution)/shard_map/ppermute | solution.py:345
  27.6 2.2 %spread.1 = (bf16[32,32,128]{2,1,0:T(8,128)(2,1)}, f32[2,512,128]{2,1,0:T(8,128)}, f32[32,128,128]{2,1,0:T(8,128)}) custom-call(f32[56,128]{1,0:T(8,128)S(1)} %get-tuple-element.24.refs_0_, f32[56,128]{1,0:T(8,128)S(1)} %collective-permute-done.2.refs_1_, f32[56,128]{1,0:T(8,128)S(1)} %collective-permute-done.3.refs_2_, ...), custom_call_target="tpu_custom_call" | custom-call | tf_op jit(solution)/shard_map/spread/pallas_call | solution.py:362
  29.8 10.0 %all-to-all-start = ((bf16[32,32,128]{2,1,0:T(8,128)(2,1)}), bf16[32,32,128]{2,1,0:T(8,128)(2,1)S(1)}, u32[]{:S(2)}, u32[]{:S(2)}) async-start(bf16[32,32,128]{2,1,0:T(8,128)(2,1)} %get-tuple-element.34), calls=%async_computation | async-start | bytes 524288 | tf_op jit(solution)/shard_map/all_to_all | solution.py:376
  39.8 2.6 %collective-permute-start.5 = (bf16[32,128,128]{2,1,0:T(8,128)(2,1)S(1)}, bf16[32,128,128]{2,1,0:T(8,128)(2,1)S(1)}, u32[]{:S(2)}, u32[]{:S(2)}) collective-permute-start(bf16[32,128,128]{2,1,0:T(8,128)(2,1)S(1)} %get-tuple-element.33), channel_id=1, source_target_pairs={{2,0},{4,2},{6,4},{8,6},{10,8},{12,10},{14,12},{16,14},{18,16},{20... | collective-permute-start | bytes 3145736 | tf_op jit(solution)/shard_map/ppermute | solution.py:360
  42.4 7.1 %all-to-all-done.arrived = bf16[32,32,128]{2,1,0:T(8,128)(2,1)S(1)} async-done(((bf16[32,32,128]{2,1,0:T(8,128)(2,1)}), bf16[32,32,128]{2,1,0:T(8,128)(2,1)S(1)}, u32[]{:S(2)}, u32[]{:S(2)}) %all-to-all-start) | async-done | bytes 262176 | tf_op jit(solution)/shard_map/all_to_all | solution.py:376
  49.5 0.0 copy-start.2
  49.5 1.0 %copy-done.2 = f32[2,512,128]{2,1,0:T(8,128)S(1)} copy-done((f32[2,512,128]{2,1,0:T(8,128)S(1)}, f32[2,512,128]{2,1,0:T(8,128)}, u32[]{:S(2)}) %copy-start.2) | copy-done | bytes 524312
  50.5 0.4 collect.1
  51.0 3.8 %collective-permute-start.6 = (bf16[32,128]{1,0:T(8,128)(2,1)S(1)}, bf16[32,128]{1,0:T(8,128)(2,1)S(1)}, u32[]{:S(2)}, u32[]{:S(2)}) collective-permute-start(bf16[32,128]{1,0:T(8,128)(2,1)S(1)} %get-tuple-element.37), channel_id=1, source_target_pairs={{0,2},{2,0},{4,6},{6,4},{8,10},{10,8},{12,14},{14,12},{16,18},{18,... | collective-permute-start | bytes 24584 | tf_op jit(solution)/shard_map/ppermute | solution.py:415
  54.8 0.0 collective-permute-start.7
  54.8 1.7 %collective-permute-start.8 = (bf16[32,128]{1,0:T(8,128)(2,1)S(1)}, bf16[32,128]{1,0:T(8,128)(2,1)S(1)}, u32[]{:S(2)}, u32[]{:S(2)}) collective-permute-start(bf16[32,128]{1,0:T(8,128)(2,1)S(1)} %get-tuple-element.39), channel_id=1, source_target_pairs={{0,6},{2,4},{4,2},{6,0},{8,14},{10,12},{12,10},{14,8},{16,22},{18,... | collective-permute-start | bytes 24584 | tf_op jit(solution)/shard_map/ppermute | solution.py:415
  56.5 0.0 collective-permute-done
  56.5 7.7 %forward.1.near = f32[32,128,128]{2,1,0:T(8,128)} custom-call(s32[8,32]{1,0:T(8,128)S(1)} %bitcast.12, s32[32]{0:T(128)S(1)} %copy-done.6, bf16[32,8,128,128]{3,2,1,0:T(8,128)(2,1)} %near.3, bf16[32,128,128]{2,1,0:T(8,128)(2,1)} %bitcast.1.halo, bf16[32,128,128]{2,1,0:T(8,128)(2,1)} %bitcast.15), custom_call_target="tpu_custom_call" | custom-call | flops 8589934592 | bytes 12582912 | tf_op jit(solution)/shard_map/forward/pallas_call | solution.py:378
  64.2 0.0 copy-start
  64.3 0.0 copy-start.1
  64.3 2.3 %fetch.1 = (f32[32,128,128]{2,1,0:T(8,128)S(1)}, f32[32,128,128]{2,1,0:T(8,128)S(1)}) custom-call(f32[32,128,128]{2,1,0:T(8,128)} %forward.1.near, f32[32,128,128]{2,1,0:T(8,128)} %get-tuple-element.30.own), custom_call_target="tpu_custom_call" | custom-call | flops 1048576 | bytes 8388608 | tf_op jit(solution)/shard_map/fetch/pallas_call | solution.py:403
  66.6 0.0 collective-permute-done.6.m1
  66.6 0.0 collective-permute-done.7.m2
  66.6 0.0 collective-permute-done.8.m3
  66.6 0.0 collective-permute-done.5.arrived
  66.6 0.0 copy-done
  66.6 0.0 copy-done.1
  66.6 1.8 %finish.1 = (bf16[32,128,128]{2,1,0:T(8,128)(2,1)}, bf16[32,128,128]{2,1,0:T(8,128)(2,1)}) custom-call(f32[32,128,128]{2,1,0:T(8,128)S(1)} %get-tuple-element.31.near, f32[32,128,128]{2,1,0:T(8,128)S(1)} %get-tuple-element.32.own, bf16[32,128,128]{2,1,0:T(8,128)(2,1)S(1)} %collective-permute-done.5.arrived, bf16[32,16,128]{2,1,0:T(8,128)(2,1)S(1)} %copy-done, ...), custom_call_target="tpu_custom_call" | custom-call | tf_op jit(solution)/shard_map/finish/pallas_call | solution.py:417
Async XLA Ops:
  0.6 6.3 %copy-start.7 = (bf16[4096,128]{1,0:T(8,128)(2,1)S(1)}, bf16[4096,128]{1,0:T(8,128)(2,1)}, u32[]{:S(2)}) copy-start(bf16[4096,128]{1,0:T(8,128)(2,1)} %param.10) | copy-start | bytes 3145732
  0.6 9.3 %copy-start.3 = (f32[1,8,16,16]{3,2,1,0:T(8,128)S(1)}, f32[1,8,16,16]{3,2,1,0:T(8,128)}, u32[]{:S(2)}) copy-start(f32[1,8,16,16]{3,2,1,0:T(8,128)} %param.17) | copy-start | bytes 24580
  0.7 9.3 %copy-start.4 = (s32[1,8]{1,0:T(1,128)S(1)}, s32[1,8]{1,0:T(1,128)}, u32[]{:S(2)}) copy-start(s32[1,8]{1,0:T(1,128)} %far_index.1) | copy-start | bytes 100
  0.7 13.6 %copy-start.5 = (s32[32,8]{0,1:T(8,128)S(1)}, s32[32,8]{0,1:T(8,128)}, u32[]{:S(2)}) copy-start(s32[32,8]{0,1:T(8,128)} %param.13) | copy-start | bytes 3076
  0.7 13.6 %copy-start.6 = (s32[32]{0:T(128)S(1)}, s32[32]{0:T(128)}, u32[]{:S(2)}) copy-start(s32[32]{0:T(128)} %count.3) | copy-start | bytes 388
  3.3 6.7 %collective-permute-start.1 = (f32[32,128]{1,0:T(8,128)S(1)}, f32[32,128]{1,0:T(8,128)S(1)}, u32[]{:S(2)}, u32[]{:S(2)}) collective-permute-start(f32[32,128]{1,0:T(8,128)S(1)} %get-tuple-element.23), channel_id=1, source_target_pairs={{0,1},{1,0},{2,3},{3,2},{4,5},{5,4},{6,7},{7,6},{8,9},{9,8},{10,11... | collective-permute-start | bytes 49160 | tf_op jit(solution)/shard_map/ppermute | solution.py:335
  6.9 49.6 %collective-permute-start = (bf16[4096,128]{1,0:T(8,128)(2,1)S(1)}, bf16[4096,128]{1,0:T(8,128)(2,1)}, u32[]{:S(2)}, u32[]{:S(2)}) collective-permute-start(bf16[4096,128]{1,0:T(8,128)(2,1)S(1)} %copy-done.7), channel_id=1, source_target_pairs={{0,2},{2,4},{4,6},{6,8},{8,10},{10,12},{12,14},{14,16},{16,18},{18... | collective-permute-start | bytes 3145736 | tf_op jit(solution)/shard_map/ppermute | solution.py:307
  10.6 10.1 %collective-permute-start.2 = (f32[56,128]{1,0:T(8,128)S(1)}, f32[56,128]{1,0:T(8,128)S(1)}, u32[]{:S(2)}, u32[]{:S(2)}) collective-permute-start(f32[56,128]{1,0:T(8,128)S(1)} %get-tuple-element.25), channel_id=1, source_target_pairs={{0,2},{2,0},{4,6},{6,4},{8,10},{10,8},{12,14},{14,12},{16,18},{18,... | collective-permute-start | bytes 86024 | tf_op jit(solution)/shard_map/ppermute | solution.py:345
  12.5 10.1 %collective-permute-start.3 = (f32[56,128]{1,0:T(8,128)S(1)}, f32[56,128]{1,0:T(8,128)S(1)}, u32[]{:S(2)}, u32[]{:S(2)}) collective-permute-start(f32[56,128]{1,0:T(8,128)S(1)} %get-tuple-element.26), channel_id=1, source_target_pairs={{0,4},{2,6},{4,0},{6,2},{8,12},{10,14},{12,8},{14,10},{16,20},{18,... | collective-permute-start | bytes 86024 | tf_op jit(solution)/shard_map/ppermute | solution.py:345
  13.3 14.2 %collective-permute-start.4 = (f32[56,128]{1,0:T(8,128)S(1)}, f32[56,128]{1,0:T(8,128)S(1)}, u32[]{:S(2)}, u32[]{:S(2)}) collective-permute-start(f32[56,128]{1,0:T(8,128)S(1)} %get-tuple-element.27), channel_id=1, source_target_pairs={{0,6},{2,4},{4,2},{6,0},{8,14},{10,12},{12,10},{14,8},{16,22},{18,... | collective-permute-start | bytes 86024 | tf_op jit(solution)/shard_map/ppermute | solution.py:345
  29.8 19.7 %all-to-all-start = ((bf16[32,32,128]{2,1,0:T(8,128)(2,1)}), bf16[32,32,128]{2,1,0:T(8,128)(2,1)S(1)}, u32[]{:S(2)}, u32[]{:S(2)}) async-start(bf16[32,32,128]{2,1,0:T(8,128)(2,1)} %get-tuple-element.34), calls=%async_computation | async-start | bytes 524288 | tf_op jit(solution)/shard_map/all_to_all | solution.py:376
  39.8 26.8 %collective-permute-start.5 = (bf16[32,128,128]{2,1,0:T(8,128)(2,1)S(1)}, bf16[32,128,128]{2,1,0:T(8,128)(2,1)S(1)}, u32[]{:S(2)}, u32[]{:S(2)}) collective-permute-start(bf16[32,128,128]{2,1,0:T(8,128)(2,1)S(1)} %get-tuple-element.33), channel_id=1, source_target_pairs={{2,0},{4,2},{6,4},{8,6},{10,8},{12,10},{14,12},{16,14},{18,16},{20... | collective-permute-start | bytes 3145736 | tf_op jit(solution)/shard_map/ppermute | solution.py:360
  49.5 1.0 %copy-start.2 = (f32[2,512,128]{2,1,0:T(8,128)S(1)}, f32[2,512,128]{2,1,0:T(8,128)}, u32[]{:S(2)}) copy-start(f32[2,512,128]{2,1,0:T(8,128)} %get-tuple-element.35.couple) | copy-start | bytes 1572868
  51.0 15.6 %collective-permute-start.6 = (bf16[32,128]{1,0:T(8,128)(2,1)S(1)}, bf16[32,128]{1,0:T(8,128)(2,1)S(1)}, u32[]{:S(2)}, u32[]{:S(2)}) collective-permute-start(bf16[32,128]{1,0:T(8,128)(2,1)S(1)} %get-tuple-element.37), channel_id=1, source_target_pairs={{0,2},{2,0},{4,6},{6,4},{8,10},{10,8},{12,14},{14,12},{16,18},{18,... | collective-permute-start | bytes 24584 | tf_op jit(solution)/shard_map/ppermute | solution.py:415
  54.8 11.8 %collective-permute-start.7 = (bf16[32,128]{1,0:T(8,128)(2,1)S(1)}, bf16[32,128]{1,0:T(8,128)(2,1)S(1)}, u32[]{:S(2)}, u32[]{:S(2)}) collective-permute-start(bf16[32,128]{1,0:T(8,128)(2,1)S(1)} %get-tuple-element.38), channel_id=1, source_target_pairs={{0,4},{2,6},{4,0},{6,2},{8,12},{10,14},{12,8},{14,10},{16,20},{18,... | collective-permute-start | bytes 24584 | tf_op jit(solution)/shard_map/ppermute | solution.py:415
  54.8 11.8 %collective-permute-start.8 = (bf16[32,128]{1,0:T(8,128)(2,1)S(1)}, bf16[32,128]{1,0:T(8,128)(2,1)S(1)}, u32[]{:S(2)}, u32[]{:S(2)}) collective-permute-start(bf16[32,128]{1,0:T(8,128)(2,1)S(1)} %get-tuple-element.39), channel_id=1, source_target_pairs={{0,6},{2,4},{4,2},{6,0},{8,14},{10,12},{12,10},{14,8},{16,22},{18,... | collective-permute-start | bytes 24584 | tf_op jit(solution)/shard_map/ppermute | solution.py:415
  64.2 2.4 %copy-start = (bf16[32,16,128]{2,1,0:T(8,128)(2,1)S(1)}, bf16[32,16,128]{2,1,0:T(8,128)(2,1)}, u32[]{:S(2)}) copy-start(bf16[32,16,128]{2,1,0:T(8,128)(2,1)} %b_in.3) | copy-start | bytes 393220
  64.3 2.4 %copy-start.1 = (bf16[32,128,16]{1,2,0:T(8,128)(2,1)S(1)}, bf16[32,128,16]{1,2,0:T(8,128)(2,1)}, u32[]{:S(2)}) copy-start(bf16[32,128,16]{1,2,0:T(8,128)(2,1)} %param.16) | copy-start | bytes 393220

commit v4 on v3

--- a/solution.py
+++ b/solution.py
@@ -11,7 +11,7 @@
 MIB = 1 << 20
 QUAD = 4
 PARTS = 4
-CHUNKS = 4
+CHUNKS = 8
 UNROLL = 4
 
 
@@ -41,17 +41,23 @@
     return jnp.where(lanes(value.shape) // 32 == keep, rolled, 0.0)
 
 
-def project_kernel(feat, cot, b_in, b_out, mix, keep, give, cot_v, feat_v, b_in_v, b_out_v, mix_v, sems):
+def project_kernel(feat, cot, b_in, b_out, mix, keep, give, cot_v, feat_lo, feat_hi, b_in_v, b_out_v, mix_v, sems):
     count = feat.shape[0]
     part = count // PARTS
     loads = []
     for n in range(PARTS):
         rows = pl.ds(n * part, part)
+        feat_v = (feat_lo, feat_hi)[n // 2].at[pl.ds(n % 2 * part, part)]
         loads.append(
             [
-                pltpu.make_async_copy(src.at[rows], dst.at[rows], sems.at[n, j])
+                pltpu.make_async_copy(src.at[rows], dst, sems.at[n, j])
                 for j, (src, dst) in enumerate(
-                    ((feat, feat_v), (b_in, b_in_v), (cot, cot_v), (b_out, b_out_v))
+                    (
+                        (feat, feat_v),
+                        (b_in, b_in_v.at[rows]),
+                        (cot, cot_v.at[rows]),
+                        (b_out, b_out_v.at[rows]),
+                    )
                 )
             ]
         )
@@ -67,7 +73,7 @@
         picks = range(n * part, (n + 1) * part)
         acc_f += dot(
             jnp.concatenate([b_in_v[i] for i in picks], axis=1),
-            feat_v[n * part : (n + 1) * part].reshape(part * 128, 128),
+            (feat_lo, feat_hi)[n // 2][n % 2 * part : (n % 2 + 1) * part].reshape(part * 128, 128),
         )
         acc_b += dot(
             jnp.concatenate([b_out_v[i] for i in picks], axis=1),
@@ -145,11 +151,12 @@
     prev[...] = acc[0:32].astype(BF16)
 
 
-def forward_kernel(index, count, near, halo, feat, out, rows, near_v, out_v, sems, row_sems, out_sems):
+def forward_kernel(index, count, near, halo_lo, halo_hi, feat, out, rows, near_v, out_v, sems, row_sems, out_sems):
     base = (lax.axis_index("curve") - 1) * 32
     heads = [
         pltpu.make_async_copy(feat, rows.at[pl.ds(32, 32)], row_sems.at[0]),
-        pltpu.make_async_copy(halo, rows.at[pl.ds(0, 32)], row_sems.at[1]),
+        pltpu.make_async_copy(halo_lo, rows.at[pl.ds(0, 16)], row_sems.at[1]),
+        pltpu.make_async_copy(halo_hi, rows.at[pl.ds(16, 16)], row_sems.at[2]),
     ]
     for copy in heads:
         copy.start()
@@ -179,16 +186,8 @@
         copy.wait()
 
 
-def spread_kernel(*refs):
-    msgs, acc, (out, couple, own), total, sem = refs[:4], refs[4], refs[5:8], refs[8], refs[9]
-    saved = pltpu.make_async_copy(acc.at[pl.ds(32, 32)], own, sem)
-    saved.start()
+def fill_couple(msgs, couple, total):
     me = lax.rem(lax.axis_index("curve"), QUAD)
-    value = msgs[0][0:32, :]
-    for ref in msgs[1:]:
-        value = value + ref[0:32, :]
-    fwd = value[0:16].astype(BF16)
-    bwd = value[16:32]
     lane = lanes((24, 128))
     for os in range(4):
         total[me ^ os] = msgs[os][32:56, :]
@@ -210,6 +209,22 @@
                 hit = jnp.concatenate([hit, hit], axis=0)
                 tile = tile + jnp.where(hit, packed[a][0:16], 0.0)
             couple[p, t * 16 : (t + 1) * 16, :] = tile
+
+
+def couple_kernel(*refs):
+    fill_couple(refs[:4], refs[4], refs[5])
+
+
+def spread_kernel(*refs):
+    msgs, acc, (out, own), (total, couple, sem) = refs[:4], refs[4], refs[5:7], refs[7:]
+    saved = pltpu.make_async_copy(acc.at[pl.ds(32, 32)], own, sem)
+    saved.start()
+    fill_couple(msgs, couple, total)
+    value = msgs[0][0:32, :]
+    for ref in msgs[1:]:
+        value = value + ref[0:32, :]
+    fwd = value[0:16].astype(BF16)
+    bwd = value[16:32]
     lane16 = lanes((16, 128))
     block = jnp.concatenate(
         [jnp.where(lane16 // 32 == g, bwd, 0.0) for g in range(4)], axis=0
@@ -304,20 +319,18 @@
     index = near_index.T
     cube = (blocks, 128, 128)
 
-    halo = lax.ppermute(features, "curve", [(i, i + 1) for i in range(groups - 1)])
-
     b_out = jnp.swapaxes(basis_out, 1, 2)
     rows32 = jax.ShapeDtypeStruct((32, 128), F32)
     vmem = pl.BlockSpec(memory_space=pltpu.VMEM)
     smem = pl.BlockSpec(memory_space=pltpu.SMEM)
     raw = pl.BlockSpec(memory_space=pl.ANY)
-    keep, give, cot_v = pl.pallas_call(
+    half_cube = (blocks // 2, 128, 128)
+    keep, give, cot_v, feat_lo, feat_hi = pl.pallas_call(
         project_kernel,
-        out_shape=[rows32, rows32, pltpu.VMEM(cube, BF16)],
+        out_shape=[rows32, rows32, pltpu.VMEM(cube, BF16)] + [pltpu.VMEM(half_cube, BF16)] * 2,
         in_specs=[raw] * 5,
-        out_specs=[vmem] * 3,
+        out_specs=[vmem] * 5,
         scratch_shapes=[
-            pltpu.VMEM(cube, BF16),
             pltpu.VMEM((blocks, 16, 128), BF16),
             pltpu.VMEM((blocks, 16, 128), BF16),
             pltpu.VMEM((256, 256), F32),
@@ -333,6 +346,9 @@
         hbm(channel_mix),
     )
     got = lax.ppermute(give, "chan", [(0, 1), (1, 0)])
+    onward = [(i, i + 1) for i in range(groups - 1)]
+    halo_lo = lax.ppermute(feat_lo, "curve", onward)
+    halo_hi = lax.ppermute(feat_hi, "curve", onward)
     msgs = pl.pallas_call(
         deal_kernel,
         out_shape=[jax.ShapeDtypeStruct((56, 128), F32)] * 4,
@@ -359,39 +375,51 @@
     )(index, near_count, hbm(near_kernel), cot_v)
     arrived = lax.ppermute(prev, "curve", [(i + 1, i) for i in range(groups - 1)])
 
-    out_msg, couple, own = pl.pallas_call(
+    out_msg, own = pl.pallas_call(
         spread_kernel,
         out_shape=[
             jax.ShapeDtypeStruct((places, 32, 128), BF16),
-            pltpu.HBM((2, places * 16, 128), F32),
             pltpu.HBM(cube, F32),
         ],
         in_specs=[vmem] * 5,
-        out_specs=[vmem, vmem, raw],
-        scratch_shapes=[pltpu.VMEM((4, 24, 128), F32), pltpu.SemaphoreType.DMA],
+        out_specs=[vmem, raw],
+        scratch_shapes=[
+            pltpu.VMEM((4, 24, 128), F32),
+            pltpu.VMEM((2, places * 16, 128), F32),
+            pltpu.SemaphoreType.DMA,
+        ],
         compiler_params=params(6, None),
         name="spread",
     )(*seen, acc)
     rings = [[t * QUAD + s for t in range(places)] for s in range(QUAD)]
     in_msg = lax.all_to_all(out_msg, "curve", 0, 0, tiled=True, axis_index_groups=rings)
 
+    couple = pl.pallas_call(
+        couple_kernel,
+        out_shape=pltpu.HBM((2, places * 16, 128), F32),
+        scratch_shapes=[pltpu.VMEM((4, 24, 128), F32)],
+        compiler_params=params(6, None),
+        cost_estimate=pl.CostEstimate(flops=1 << 20, bytes_accessed=1 << 20, transcendentals=0),
+        name="couple",
+    )(*seen)
+
     near = pl.pallas_call(
         forward_kernel,
         out_shape=pltpu.HBM(cube, F32),
-        in_specs=[smem, smem, raw, raw, raw],
+        in_specs=[smem, smem, raw, raw, raw, raw],
         out_specs=raw,
         scratch_shapes=[
             pltpu.VMEM((2 * blocks + 1, 128, 128), BF16),
             pltpu.VMEM(near_kernel.shape, BF16),
             pltpu.VMEM(cube, F32),
             pltpu.SemaphoreType.DMA((CHUNKS,)),
-            pltpu.SemaphoreType.DMA((2,)),
+            pltpu.SemaphoreType.DMA((3,)),
             pltpu.SemaphoreType.DMA((CHUNKS,)),
         ],
         compiler_params=params(16, None),
         cost_estimate=pl.CostEstimate(flops=8 << 30, bytes_accessed=12 << 20, transcendentals=0),
         name="forward",
-    )(index, near_count, hbm(near_kernel), hbm(halo.reshape(cube)), hbm(features.reshape(cube)))
+    )(index, near_count, hbm(near_kernel), hbm(halo_lo), hbm(halo_hi), hbm(features.reshape(cube)))
 
     back = pl.pallas_call(
         collect_kernel,

time: 68.7 us -> 69.7 us (1.015)
  waiting for transfers between devices: 13.9 us -> 12 us
  starting transfers between devices: 28.5 us -> 29.9 us
  Pallas kernels: 24.1 us -> 25.4 us
    ppermute x1 -> x2, starting transfers between devices: 3.05 us -> 4.97 us  [the longest x1 3.05 us: layer_step(): halo_lo = lax.ppermute(feat_lo, 'curve', onward)]
    all_to_all x1, waiting for transfers between devices: 7.08 us -> 5.77 us  [layer_step(): lax.all_to_all(out_msg, 'curve', 0, 0, tiled=True, axis_index_groups=rings)]
    pallas_call x0 -> x1, Pallas kernels: none -> 1.31 us  [layer_step(): pl.pallas_call(couple_kernel, out_shape=pltpu.HBM((2, places * 16, 128),...]
  transfers between devices with their start and end apart: 10 -> 11, of which waited for: 3 -> 3; matrix products, arithmetic and copies ran while one was open for 0% -> 0% of each run, Pallas kernels for 29% -> 30%
where the time goes in v4:
time: 69.7 us; the launch traced here: 69.4 us
  starting transfers between devices  29.9 us (43%)
  Pallas kernels  25.4 us (36%)
  waiting for transfers between devices  12 us (17%)
  local copies, waits for them, and re-layouts  1.07 us (2%)
  between operations  1.01 us (1%)
    all_to_all x1, starting transfers between devices, layer_step(): lax.all_to_all(out_msg, 'curve', 0, 0, tiled=True, axis_index_groups=rings)  10 us
    pallas_call x1, Pallas kernels, layer_step(): pl.pallas_call(forward_kernel, out_shape=pltpu.HBM(cube, F32), in_specs=[...  8.28 us
    ppermute x3, waiting for transfers between devices, layer_step(): lax.ppermute(msgs[o], 'curve', [(i, i ^ o) for i in range(groups)])  6.18 us
    pallas_call x1, Pallas kernels, layer_step(): pl.pallas_call(backward_kernel, out_shape=[jax.ShapeDtypeStruct(cube, BF1...  6.13 us
    all_to_all x1, waiting for transfers between devices, layer_step(): lax.all_to_all(out_msg, 'curve', 0, 0, tiled=True, axis_index_groups=rings)  5.77 us
    ppermute x3, starting transfers between devices, layer_step(): lax.ppermute(back[o], 'curve', [(i, i ^ o) for i in range(groups)])  5.53 us
    ppermute x1, starting transfers between devices, layer_step(): got = lax.ppermute(give, 'chan', [(0, 1), (1, 0)])  3.65 us
    ppermute x3, starting transfers between devices, layer_step(): lax.ppermute(msgs[o], 'curve', [(i, i ^ o) for i in range(groups)])  3.18 us
  transfers between devices with their start and end apart: 11, of which 3 were waited for; matrix products, arithmetic and copies ran while one was open for 0% of the time, Pallas kernels for 30%

profile of v4, /device:TPU:1, one launch (start us, length us, event | category | flops | bytes accessed | tf_op | source)
XLA Modules:
  0.0 69.4 jit_solution(2629652599753038706)
XLA Ops:
  0.6 0.0 copy-start.3
  0.6 0.0 copy-start.4
  0.7 0.0 copy-start.5
  0.7 0.0 copy-start.6
  0.7 2.5 %project.1 = (f32[32,128]{1,0:T(8,128)S(1)}, f32[32,128]{1,0:T(8,128)S(1)}, bf16[32,128,128]{2,1,0:T(8,128)(2,1)S(1)}, bf16[16,128,128]{2,1,0:T(8,128)(2,1)S(1)}, bf16[16,128,128]{2,1,0:T(8,128)(2,1)S(1)}) custom-call(bf16[32,128,128]{2,1,0:T(8,128)(2,1)} %bitcast.13, bf16[32,128,128]{2,1,0:T(8,128)(2,1)} %bitcast.12, bf16[32,16,128]{2,1,0:T(8,128)(2,1)} %b_in.3, ...), custom_call_target="tpu_custom_call" | custom-call | tf_op jit(solution)/shard_map/project/pallas_call | solution.py:328
  3.2 3.6 %collective-permute-start.2 = (f32[32,128]{1,0:T(8,128)S(1)}, f32[32,128]{1,0:T(8,128)S(1)}, u32[]{:S(2)}, u32[]{:S(2)}) collective-permute-start(f32[32,128]{1,0:T(8,128)S(1)} %get-tuple-element.26), channel_id=1, source_target_pairs={{0,1},{1,0},{2,3},{3,2},{4,5},{5,4},{6,7},{7,6},{8,9},{9,8},{10,11... | collective-permute-start | bytes 49160 | tf_op jit(solution)/shard_map/ppermute | solution.py:348
  6.9 3.0 %collective-permute-start = (bf16[16,128,128]{2,1,0:T(8,128)(2,1)S(1)}, bf16[16,128,128]{2,1,0:T(8,128)(2,1)}, u32[]{:S(2)}, u32[]{:S(2)}) collective-permute-start(bf16[16,128,128]{2,1,0:T(8,128)(2,1)S(1)} %get-tuple-element.23), channel_id=1, source_target_pairs={{0,2},{2,4},{4,6},{6,8},{8,10},{10,12},{12,14},{14,16},{16,18},{18... | collective-permute-start | bytes 1572872 | tf_op jit(solution)/shard_map/ppermute | solution.py:350
  9.9 1.9 %collective-permute-start.1 = (bf16[16,128,128]{2,1,0:T(8,128)(2,1)S(1)}, bf16[16,128,128]{2,1,0:T(8,128)(2,1)}, u32[]{:S(2)}, u32[]{:S(2)}) collective-permute-start(bf16[16,128,128]{2,1,0:T(8,128)(2,1)S(1)} %get-tuple-element.24), channel_id=1, source_target_pairs={{0,2},{2,4},{4,6},{6,8},{8,10},{10,12},{12,14},{14,16},{16,18},{18... | collective-permute-start | bytes 1572872 | tf_op jit(solution)/shard_map/ppermute | solution.py:351
  11.8 0.0 collective-permute-done.2.got
  11.9 0.0 copy-done.3
  11.9 0.0 copy-done.4
  11.9 0.6 deal.1
  12.5 1.4 %collective-permute-start.3 = (f32[56,128]{1,0:T(8,128)S(1)}, f32[56,128]{1,0:T(8,128)S(1)}, u32[]{:S(2)}, u32[]{:S(2)}) collective-permute-start(f32[56,128]{1,0:T(8,128)S(1)} %get-tuple-element.28), channel_id=1, source_target_pairs={{0,2},{2,0},{4,6},{6,4},{8,10},{10,8},{12,14},{14,12},{16,18},{18,... | collective-permute-start | bytes 86024 | tf_op jit(solution)/shard_map/ppermute | solution.py:361
  13.9 1.7 %collective-permute-start.4 = (f32[56,128]{1,0:T(8,128)S(1)}, f32[56,128]{1,0:T(8,128)S(1)}, u32[]{:S(2)}, u32[]{:S(2)}) collective-permute-start(f32[56,128]{1,0:T(8,128)S(1)} %get-tuple-element.29), channel_id=1, source_target_pairs={{0,4},{2,6},{4,0},{6,2},{8,12},{10,14},{12,8},{14,10},{16,20},{18,... | collective-permute-start | bytes 86024 | tf_op jit(solution)/shard_map/ppermute | solution.py:361
  15.6 0.1 collective-permute-start.5
  15.7 0.0 copy-done.5
  15.7 0.0 copy-done.6
  15.7 6.1 %backward.1 = (bf16[32,128,128]{2,1,0:T(8,128)(2,1)S(1)}, f32[65,128,128]{2,1,0:T(8,128)S(1)}) custom-call(s32[8,32]{1,0:T(8,128)S(1)} %bitcast.10, s32[32]{0:T(128)S(1)} %copy-done.6, bf16[32,8,128,128]{3,2,1,0:T(8,128)(2,1)} %near.3, bf16[32,128,128]{2,1,0:T(8,128)(2,1)S(1)} %get-tuple-element.31.cot), custom_call_target="tpu_custom_call" | custom-call | flops 8589934592 | bytes 12582912 | tf_op jit(solution)/shard_map/backward/pallas_call | solution.py:363
  21.8 0.0 collective-permute-done.3.refs_1_
  21.9 5.6 %collective-permute-done.4.refs_2_ = f32[56,128]{1,0:T(8,128)S(1)} collective-permute-done((f32[56,128]{1,0:T(8,128)S(1)}, f32[56,128]{1,0:T(8,128)S(1)}, u32[]{:S(2)}, u32[]{:S(2)}) %collective-permute-start.4) | collective-permute-done | bytes 28704 | tf_op jit(solution)/shard_map/ppermute | solution.py:361
  27.4 0.6 collective-permute-done.5.refs_3_
  28.0 2.0 %spread.1 = (bf16[32,32,128]{2,1,0:T(8,128)(2,1)}, f32[32,128,128]{2,1,0:T(8,128)}) custom-call(f32[56,128]{1,0:T(8,128)S(1)} %get-tuple-element.27.refs_0_, f32[56,128]{1,0:T(8,128)S(1)} %collective-permute-done.3.refs_1_, f32[56,128]{1,0:T(8,128)S(1)} %collective-permute-done.4.refs_2_, f32[56,128]{1,0:T(8,128)S(1)} %collective-permute-done.5.refs_3_, ...), custom_call_target="tpu_custom_call" | custom-call | tf_op jit(solution)/shard_map/spread/pallas_call | solution.py:378
  30.1 10.0 %all-to-all-start = ((bf16[32,32,128]{2,1,0:T(8,128)(2,1)}), bf16[32,32,128]{2,1,0:T(8,128)(2,1)S(1)}, u32[]{:S(2)}, u32[]{:S(2)}) async-start(bf16[32,32,128]{2,1,0:T(8,128)(2,1)} %get-tuple-element.37), calls=%async_computation | async-start | bytes 524288 | tf_op jit(solution)/shard_map/all_to_all | solution.py:395
  40.1 2.6 %collective-permute-start.6 = (bf16[32,128,128]{2,1,0:T(8,128)(2,1)S(1)}, bf16[32,128,128]{2,1,0:T(8,128)(2,1)S(1)}, u32[]{:S(2)}, u32[]{:S(2)}) collective-permute-start(bf16[32,128,128]{2,1,0:T(8,128)(2,1)S(1)} %get-tuple-element.36), channel_id=1, source_target_pairs={{2,0},{4,2},{6,4},{8,6},{10,8},{12,10},{14,12},{16,14},{18,16},{20... | collective-permute-start | bytes 3145736 | tf_op jit(solution)/shard_map/ppermute | solution.py:376
  42.7 1.3 %couple.1 = f32[2,512,128]{2,1,0:T(8,128)} custom-call(f32[56,128]{1,0:T(8,128)S(1)} %get-tuple-element.27.refs_0_, f32[56,128]{1,0:T(8,128)S(1)} %collective-permute-done.3.refs_1_, f32[56,128]{1,0:T(8,128)S(1)} %collective-permute-done.4.refs_2_, f32[56,128]{1,0:T(8,128)S(1)} %collective-permute-done.5.refs_3_), custom_call_target="tpu_custom_call" | custom-call | flops 1048576 | bytes 1048576 | tf_op jit(solution)/shard_map/couple/pallas_call | solution.py:397
  44.0 5.8 %all-to-all-done.arrived = bf16[32,32,128]{2,1,0:T(8,128)(2,1)S(1)} async-done(((bf16[32,32,128]{2,1,0:T(8,128)(2,1)}), bf16[32,32,128]{2,1,0:T(8,128)(2,1)S(1)}, u32[]{:S(2)}, u32[]{:S(2)}) %all-to-all-start) | async-done | bytes 262176 | tf_op jit(solution)/shard_map/all_to_all | solution.py:395
  49.7 0.0 copy-start
  49.7 1.0 %copy-done = f32[2,512,128]{2,1,0:T(8,128)S(1)} copy-done((f32[2,512,128]{2,1,0:T(8,128)S(1)}, f32[2,512,128]{2,1,0:T(8,128)}, u32[]{:S(2)}) %copy-start) | copy-done | bytes 524312
  50.8 0.4 collect.1
  51.2 3.8 %collective-permute-start.7 = (bf16[32,128]{1,0:T(8,128)(2,1)S(1)}, bf16[32,128]{1,0:T(8,128)(2,1)S(1)}, u32[]{:S(2)}, u32[]{:S(2)}) collective-permute-start(bf16[32,128]{1,0:T(8,128)(2,1)S(1)} %get-tuple-element.39), channel_id=1, source_target_pairs={{0,2},{2,0},{4,6},{6,4},{8,10},{10,8},{12,14},{14,12},{16,18},{18,... | collective-permute-start | bytes 24584 | tf_op jit(solution)/shard_map/ppermute | solution.py:443
  55.0 0.0 collective-permute-start.8
  55.0 0.0 collective-permute-done.halo_lo
  55.0 1.7 %collective-permute-start.9 = (bf16[32,128]{1,0:T(8,128)(2,1)S(1)}, bf16[32,128]{1,0:T(8,128)(2,1)S(1)}, u32[]{:S(2)}, u32[]{:S(2)}) collective-permute-start(bf16[32,128]{1,0:T(8,128)(2,1)S(1)} %get-tuple-element.41), channel_id=1, source_target_pairs={{0,6},{2,4},{4,2},{6,0},{8,14},{10,12},{12,10},{14,8},{16,22},{18,... | collective-permute-start | bytes 24584 | tf_op jit(solution)/shard_map/ppermute | solution.py:443
  56.8 0.0 collective-permute-done.1.halo_hi
  56.8 8.3 %forward.1.near = f32[32,128,128]{2,1,0:T(8,128)} custom-call(s32[8,32]{1,0:T(8,128)S(1)} %bitcast.11, s32[32]{0:T(128)S(1)} %copy-done.6, bf16[32,8,128,128]{3,2,1,0:T(8,128)(2,1)} %near.3, bf16[16,128,128]{2,1,0:T(8,128)(2,1)} %collective-permute-done.halo_lo, bf16[16,128,128]{2,1,0:T(8,128)(2,1)} %collective-permute-done.1.halo_hi, ...), custom_call_target="tpu_custom_call" | custom-call | flops 8589934592 | bytes 12582912 | tf_op jit(solution)/shard_map/forward/pallas_call | solution.py:406
  65.1 0.0 copy-start.1
  65.1 0.0 copy-start.2
  65.1 2.3 %fetch.1 = (f32[32,128,128]{2,1,0:T(8,128)S(1)}, f32[32,128,128]{2,1,0:T(8,128)S(1)}) custom-call(f32[32,128,128]{2,1,0:T(8,128)} %forward.1.near, f32[32,128,128]{2,1,0:T(8,128)} %get-tuple-element.33.own), custom_call_target="tpu_custom_call" | custom-call | flops 1048576 | bytes 8388608 | tf_op jit(solution)/shard_map/fetch/pallas_call | solution.py:431
  67.4 0.0 collective-permute-done.7.m1
  67.4 0.0 collective-permute-done.8.m2
  67.4 0.0 collective-permute-done.9.m3
  67.4 0.0 collective-permute-done.6.arrived
  67.4 0.0 copy-done.1
  67.4 0.0 copy-done.2
  67.4 1.8 %finish.1 = (bf16[32,128,128]{2,1,0:T(8,128)(2,1)}, bf16[32,128,128]{2,1,0:T(8,128)(2,1)}) custom-call(f32[32,128,128]{2,1,0:T(8,128)S(1)} %get-tuple-element.34.near, f32[32,128,128]{2,1,0:T(8,128)S(1)} %get-tuple-element.35.own, bf16[32,128,128]{2,1,0:T(8,128)(2,1)S(1)} %collective-permute-done.6.arrived, bf16[32,16,128]{2,1,0:T(8,128)(2,1)S(1)} %copy-done.1, ...), custom_call_target="tpu_custom_call" | custom-call | tf_op jit(solution)/shard_map/finish/pallas_call | solution.py:445
Async XLA Ops:
  0.6 11.2 %copy-start.3 = (f32[1,8,16,16]{3,2,1,0:T(8,128)S(1)}, f32[1,8,16,16]{3,2,1,0:T(8,128)}, u32[]{:S(2)}) copy-start(f32[1,8,16,16]{3,2,1,0:T(8,128)} %param.17) | copy-start | bytes 24580
  0.6 11.2 %copy-start.4 = (s32[1,8]{1,0:T(1,128)S(1)}, s32[1,8]{1,0:T(1,128)}, u32[]{:S(2)}) copy-start(s32[1,8]{1,0:T(1,128)} %far_index.1) | copy-start | bytes 100
  0.7 15.1 %copy-start.5 = (s32[32,8]{0,1:T(8,128)S(1)}, s32[32,8]{0,1:T(8,128)}, u32[]{:S(2)}) copy-start(s32[32,8]{0,1:T(8,128)} %param.13) | copy-start | bytes 3076
  0.7 15.1 %copy-start.6 = (s32[32]{0:T(128)S(1)}, s32[32]{0:T(128)}, u32[]{:S(2)}) copy-start(s32[32]{0:T(128)} %count.3) | copy-start | bytes 388
  3.2 8.6 %collective-permute-start.2 = (f32[32,128]{1,0:T(8,128)S(1)}, f32[32,128]{1,0:T(8,128)S(1)}, u32[]{:S(2)}, u32[]{:S(2)}) collective-permute-start(f32[32,128]{1,0:T(8,128)S(1)} %get-tuple-element.26), channel_id=1, source_target_pairs={{0,1},{1,0},{2,3},{3,2},{4,5},{5,4},{6,7},{7,6},{8,9},{9,8},{10,11... | collective-permute-start | bytes 49160 | tf_op jit(solution)/shard_map/ppermute | solution.py:348
  6.9 48.2 %collective-permute-start = (bf16[16,128,128]{2,1,0:T(8,128)(2,1)S(1)}, bf16[16,128,128]{2,1,0:T(8,128)(2,1)}, u32[]{:S(2)}, u32[]{:S(2)}) collective-permute-start(bf16[16,128,128]{2,1,0:T(8,128)(2,1)S(1)} %get-tuple-element.23), channel_id=1, source_target_pairs={{0,2},{2,4},{4,6},{6,8},{8,10},{10,12},{12,14},{14,16},{16,18},{18... | collective-permute-start | bytes 1572872 | tf_op jit(solution)/shard_map/ppermute | solution.py:350
  9.9 46.9 %collective-permute-start.1 = (bf16[16,128,128]{2,1,0:T(8,128)(2,1)S(1)}, bf16[16,128,128]{2,1,0:T(8,128)(2,1)}, u32[]{:S(2)}, u32[]{:S(2)}) collective-permute-start(bf16[16,128,128]{2,1,0:T(8,128)(2,1)S(1)} %get-tuple-element.24), channel_id=1, source_target_pairs={{0,2},{2,4},{4,6},{6,8},{8,10},{10,12},{12,14},{14,16},{16,18},{18... | collective-permute-start | bytes 1572872 | tf_op jit(solution)/shard_map/ppermute | solution.py:351
  12.5 9.3 %collective-permute-start.3 = (f32[56,128]{1,0:T(8,128)S(1)}, f32[56,128]{1,0:T(8,128)S(1)}, u32[]{:S(2)}, u32[]{:S(2)}) collective-permute-start(f32[56,128]{1,0:T(8,128)S(1)} %get-tuple-element.28), channel_id=1, source_target_pairs={{0,2},{2,0},{4,6},{6,4},{8,10},{10,8},{12,14},{14,12},{16,18},{18,... | collective-permute-start | bytes 86024 | tf_op jit(solution)/shard_map/ppermute | solution.py:361
  13.9 13.5 %collective-permute-start.4 = (f32[56,128]{1,0:T(8,128)S(1)}, f32[56,128]{1,0:T(8,128)S(1)}, u32[]{:S(2)}, u32[]{:S(2)}) collective-permute-start(f32[56,128]{1,0:T(8,128)S(1)} %get-tuple-element.29), channel_id=1, source_target_pairs={{0,4},{2,6},{4,0},{6,2},{8,12},{10,14},{12,8},{14,10},{16,20},{18,... | collective-permute-start | bytes 86024 | tf_op jit(solution)/shard_map/ppermute | solution.py:361
  15.6 12.4 %collective-permute-start.5 = (f32[56,128]{1,0:T(8,128)S(1)}, f32[56,128]{1,0:T(8,128)S(1)}, u32[]{:S(2)}, u32[]{:S(2)}) collective-permute-start(f32[56,128]{1,0:T(8,128)S(1)} %get-tuple-element.30), channel_id=1, source_target_pairs={{0,6},{2,4},{4,2},{6,0},{8,14},{10,12},{12,10},{14,8},{16,22},{18,... | collective-permute-start | bytes 86024 | tf_op jit(solution)/shard_map/ppermute | solution.py:361
  30.1 19.7 %all-to-all-start = ((bf16[32,32,128]{2,1,0:T(8,128)(2,1)}), bf16[32,32,128]{2,1,0:T(8,128)(2,1)S(1)}, u32[]{:S(2)}, u32[]{:S(2)}) async-start(bf16[32,32,128]{2,1,0:T(8,128)(2,1)} %get-tuple-element.37), calls=%async_computation | async-start | bytes 524288 | tf_op jit(solution)/shard_map/all_to_all | solution.py:395
  40.1 27.3 %collective-permute-start.6 = (bf16[32,128,128]{2,1,0:T(8,128)(2,1)S(1)}, bf16[32,128,128]{2,1,0:T(8,128)(2,1)S(1)}, u32[]{:S(2)}, u32[]{:S(2)}) collective-permute-start(bf16[32,128,128]{2,1,0:T(8,128)(2,1)S(1)} %get-tuple-element.36), channel_id=1, source_target_pairs={{2,0},{4,2},{6,4},{8,6},{10,8},{12,10},{14,12},{16,14},{18,16},{20... | collective-permute-start | bytes 3145736 | tf_op jit(solution)/shard_map/ppermute | solution.py:376
  49.7 1.0 %copy-start = (f32[2,512,128]{2,1,0:T(8,128)S(1)}, f32[2,512,128]{2,1,0:T(8,128)}, u32[]{:S(2)}) copy-start(f32[2,512,128]{2,1,0:T(8,128)} %couple.1) | copy-start | bytes 1572868
  51.2 16.1 %collective-permute-start.7 = (bf16[32,128]{1,0:T(8,128)(2,1)S(1)}, bf16[32,128]{1,0:T(8,128)(2,1)S(1)}, u32[]{:S(2)}, u32[]{:S(2)}) collective-permute-start(bf16[32,128]{1,0:T(8,128)(2,1)S(1)} %get-tuple-element.39), channel_id=1, source_target_pairs={{0,2},{2,0},{4,6},{6,4},{8,10},{10,8},{12,14},{14,12},{16,18},{18,... | collective-permute-start | bytes 24584 | tf_op jit(solution)/shard_map/ppermute | solution.py:443
  55.0 12.4 %collective-permute-start.8 = (bf16[32,128]{1,0:T(8,128)(2,1)S(1)}, bf16[32,128]{1,0:T(8,128)(2,1)S(1)}, u32[]{:S(2)}, u32[]{:S(2)}) collective-permute-start(bf16[32,128]{1,0:T(8,128)(2,1)S(1)} %get-tuple-element.40), channel_id=1, source_target_pairs={{0,4},{2,6},{4,0},{6,2},{8,12},{10,14},{12,8},{14,10},{16,20},{18,... | collective-permute-start | bytes 24584 | tf_op jit(solution)/shard_map/ppermute | solution.py:443
  55.0 12.4 %collective-permute-start.9 = (bf16[32,128]{1,0:T(8,128)(2,1)S(1)}, bf16[32,128]{1,0:T(8,128)(2,1)S(1)}, u32[]{:S(2)}, u32[]{:S(2)}) collective-permute-start(bf16[32,128]{1,0:T(8,128)(2,1)S(1)} %get-tuple-element.41), channel_id=1, source_target_pairs={{0,6},{2,4},{4,2},{6,0},{8,14},{10,12},{12,10},{14,8},{16,22},{18,... | collective-permute-start | bytes 24584 | tf_op jit(solution)/shard_map/ppermute | solution.py:443
  65.1 2.4 %copy-start.1 = (bf16[32,16,128]{2,1,0:T(8,128)(2,1)S(1)}, bf16[32,16,128]{2,1,0:T(8,128)(2,1)}, u32[]{:S(2)}) copy-start(bf16[32,16,128]{2,1,0:T(8,128)(2,1)} %b_in.3) | copy-start | bytes 393220
  65.1 2.4 %copy-start.2 = (bf16[32,128,16]{1,2,0:T(8,128)(2,1)S(1)}, bf16[32,128,16]{1,2,0:T(8,128)(2,1)}, u32[]{:S(2)}) copy-start(bf16[32,128,16]{1,2,0:T(8,128)(2,1)} %param.16) | copy-start | bytes 393220

commit v5 on v3

--- a/solution.py
+++ b/solution.py
@@ -11,8 +11,8 @@
 MIB = 1 << 20
 QUAD = 4
 PARTS = 4
-CHUNKS = 4
-UNROLL = 4
+CHUNKS = 8
+AHEAD = 3
 
 
 def params(mib, semantics=("arbitrary",)):
@@ -49,9 +49,14 @@
         rows = pl.ds(n * part, part)
         loads.append(
             [
-                pltpu.make_async_copy(src.at[rows], dst.at[rows], sems.at[n, j])
+                pltpu.make_async_copy(src.at[rows], dst, sems.at[n, j])
                 for j, (src, dst) in enumerate(
-                    ((feat, feat_v), (b_in, b_in_v), (cot, cot_v), (b_out, b_out_v))
+                    (
+                        (feat, feat_v.at[rows]),
+                        (b_in, b_in_v.at[rows]),
+                        (cot, cot_v.at[rows]),
+                        (b_out, b_out_v.at[rows]),
+                    )
                 )
             ]
         )
@@ -110,39 +115,43 @@
         outs[os][48:56, :] = row.astype(F32)
 
 
-def tile_loads(near, near_v, sems):
+def tile_copies(near, near_v, sems):
     part = near.shape[0] // CHUNKS
-    copies = []
-    for n in range(CHUNKS):
-        rows = pl.ds(n * part, part)
-        copies.append(pltpu.make_async_copy(near.at[rows], near_v.at[rows], sems.at[n]))
-        copies[-1].start()
-    return copies
-
-
-def backward_kernel(index, count, near, cot, prev, acc, near_v, sems):
+    spans = [pl.ds(n * part, part) for n in range(CHUNKS)]
+    return [
+        pltpu.make_async_copy(near.at[span], near_v.at[span], sems.at[n])
+        for n, span in enumerate(spans)
+    ]
+
+
+def backward_kernel(index, count, near, cot, prev, own, acc, near_v, sems, out_sems):
     base = (lax.axis_index("curve") - 1) * 32
-    copies = tile_loads(near, near_v, sems)
+    copies = tile_copies(near, near_v, sems)[::-1]
+    for copy in copies[:AHEAD]:
+        copy.start()
     acc[...] = jnp.zeros_like(acc)
     part = near.shape[0] // CHUNKS
-    for n, copy in enumerate(copies):
-        copy.wait()
-
-        def some(step, carry):
-            for i in range(UNROLL):
-                b = n * part + step * UNROLL + i
-                cot_t = cot[b].T
-                live = count[b]
-                for k in range(0, 8, 2):
-                    pair = jnp.concatenate([near_v[b, k], near_v[b, k + 1]], axis=1)
-                    term = dot(cot_t, pair)
-                    for j in range(2):
-                        row = jnp.where(k + j < live, index[k + j, b] - base, 64)
-                        acc[row] += term[:, j * 128 : (j + 1) * 128]
-            return carry
-
-        lax.fori_loop(0, part // UNROLL, some, 0)
+    stores = []
+    for turn, copy in enumerate(copies):
+        copy.wait()
+        if turn + AHEAD < CHUNKS:
+            copies[turn + AHEAD].start()
+        n = CHUNKS - 1 - turn
+        for b in range(n * part, (n + 1) * part):
+            cot_t = cot[b].T
+            live = count[b]
+            for k in range(0, 8, 2):
+                pair = jnp.concatenate([near_v[b, k], near_v[b, k + 1]], axis=1)
+                term = dot(cot_t, pair)
+                for j in range(2):
+                    row = jnp.where(k + j < live, index[k + j, b] - base, 64)
+                    acc[row] += term[:, j * 128 : (j + 1) * 128]
+        done = acc.at[pl.ds(32 + n * part, part)]
+        stores.append(pltpu.make_async_copy(done, own.at[pl.ds(n * part, part)], out_sems.at[n]))
+        stores[-1].start()
     prev[...] = acc[0:32].astype(BF16)
+    for copy in stores:
+        copy.wait()
 
 
 def forward_kernel(index, count, near, halo, feat, out, rows, near_v, out_v, sems, row_sems, out_sems):
@@ -151,27 +160,25 @@
         pltpu.make_async_copy(feat, rows.at[pl.ds(32, 32)], row_sems.at[0]),
         pltpu.make_async_copy(halo, rows.at[pl.ds(0, 32)], row_sems.at[1]),
     ]
-    for copy in heads:
+    copies = tile_copies(near, near_v, sems)
+    for copy in heads + copies[:1]:
         copy.start()
-    copies = tile_loads(near, near_v, sems)
     rows[64] = jnp.zeros((128, 128), BF16)
     for copy in heads:
         copy.wait()
+    for copy in copies[1:AHEAD]:
+        copy.start()
     part = near.shape[0] // CHUNKS
     stores = []
     for n, copy in enumerate(copies):
         copy.wait()
-
-        def some(step, carry):
-            for i in range(UNROLL):
-                b = n * part + step * UNROLL + i
-                live = count[b]
-                picked = [rows[jnp.where(k < live, index[k, b] - base, 64)] for k in range(8)]
-                tiles = jnp.concatenate([near_v[b, k] for k in range(8)], axis=1)
-                out_v[b] = dot(tiles, jnp.concatenate(picked, axis=0))
-            return carry
-
-        lax.fori_loop(0, part // UNROLL, some, 0)
+        if n + AHEAD < CHUNKS:
+            copies[n + AHEAD].start()
+        for b in range(n * part, (n + 1) * part):
+            live = count[b]
+            picked = [rows[jnp.where(k < live, index[k, b] - base, 64)] for k in range(8)]
+            tiles = jnp.concatenate([near_v[b, k] for k in range(8)], axis=1)
+            out_v[b] = dot(tiles, jnp.concatenate(picked, axis=0))
         span = pl.ds(n * part, part)
         stores.append(pltpu.make_async_copy(out_v.at[span], out.at[span], out_sems.at[n]))
         stores[-1].start()
@@ -179,16 +186,8 @@
         copy.wait()
 
 
-def spread_kernel(*refs):
-    msgs, acc, (out, couple, own), total, sem = refs[:4], refs[4], refs[5:8], refs[8], refs[9]
-    saved = pltpu.make_async_copy(acc.at[pl.ds(32, 32)], own, sem)
-    saved.start()
+def fill_couple(msgs, couple, total):
     me = lax.rem(lax.axis_index("curve"), QUAD)
-    value = msgs[0][0:32, :]
-    for ref in msgs[1:]:
-        value = value + ref[0:32, :]
-    fwd = value[0:16].astype(BF16)
-    bwd = value[16:32]
     lane = lanes((24, 128))
     for os in range(4):
         total[me ^ os] = msgs[os][32:56, :]
@@ -210,6 +209,16 @@
                 hit = jnp.concatenate([hit, hit], axis=0)
                 tile = tile + jnp.where(hit, packed[a][0:16], 0.0)
             couple[p, t * 16 : (t + 1) * 16, :] = tile
+
+
+def spread_kernel(*refs):
+    msgs, out, (total, couple) = refs[:4], refs[4], refs[5:]
+    fill_couple(msgs, couple, total)
+    value = msgs[0][0:32, :]
+    for ref in msgs[1:]:
+        value = value + ref[0:32, :]
+    fwd = value[0:16].astype(BF16)
+    bwd = value[16:32]
     lane16 = lanes((16, 128))
     block = jnp.concatenate(
         [jnp.where(lane16 // 32 == g, bwd, 0.0) for g in range(4)], axis=0
@@ -227,11 +236,11 @@
     for t in range(32):
         out[t, 0:16, :] = fwd
         out[t, 16:32, :] = contrib[t * 16 : (t + 1) * 16]
-    saved.wait()
-
-
-def collect_kernel(arrived, couple, *refs):
-    outs, (picked, summed) = refs[:4], refs[4:]
+
+
+def collect_kernel(arrived, *refs):
+    msgs, outs, (picked, groups, couple) = refs[:4], refs[4:8], refs[8:]
+    fill_couple(msgs, couple, groups)
     me = lax.rem(lax.axis_index("curve"), QUAD)
     total = arrived[0, 16:32, :].astype(F32)
     for t in range(1, 32):
@@ -304,8 +313,6 @@
     index = near_index.T
     cube = (blocks, 128, 128)
 
-    halo = lax.ppermute(features, "curve", [(i, i + 1) for i in range(groups - 1)])
-
     b_out = jnp.swapaxes(basis_out, 1, 2)
     rows32 = jax.ShapeDtypeStruct((32, 128), F32)
     vmem = pl.BlockSpec(memory_space=pltpu.VMEM)
@@ -333,6 +340,7 @@
         hbm(channel_mix),
     )
     got = lax.ppermute(give, "chan", [(0, 1), (1, 0)])
+    halo = lax.ppermute(features, "curve", [(i, i + 1) for i in range(groups - 1)])
     msgs = pl.pallas_call(
         deal_kernel,
         out_shape=[jax.ShapeDtypeStruct((56, 128), F32)] * 4,
@@ -344,34 +352,33 @@
     for o in range(1, 4):
         seen.append(lax.ppermute(msgs[o], "curve", [(i, i ^ o) for i in range(groups)]))
 
-    prev, acc = pl.pallas_call(
+    prev, own = pl.pallas_call(
         backward_kernel,
-        out_shape=[
-            jax.ShapeDtypeStruct(cube, BF16),
+        out_shape=[jax.ShapeDtypeStruct(cube, BF16), pltpu.HBM(cube, F32)],
+        in_specs=[smem, smem, raw, vmem],
+        out_specs=[vmem, raw],
+        scratch_shapes=[
             pltpu.VMEM((2 * blocks + 1, 128, 128), F32),
-        ],
-        in_specs=[smem, smem, raw, vmem],
-        out_specs=[vmem, vmem],
-        scratch_shapes=[pltpu.VMEM(near_kernel.shape, BF16), pltpu.SemaphoreType.DMA((CHUNKS,))],
+            pltpu.VMEM(near_kernel.shape, BF16),
+            pltpu.SemaphoreType.DMA((CHUNKS,)),
+            pltpu.SemaphoreType.DMA((CHUNKS,)),
+        ],
         compiler_params=params(16, None),
         cost_estimate=pl.CostEstimate(flops=8 << 30, bytes_accessed=12 << 20, transcendentals=0),
         name="backward",
     )(index, near_count, hbm(near_kernel), cot_v)
     arrived = lax.ppermute(prev, "curve", [(i + 1, i) for i in range(groups - 1)])
 
-    out_msg, couple, own = pl.pallas_call(
+    out_msg = pl.pallas_call(
         spread_kernel,
-        out_shape=[
-            jax.ShapeDtypeStruct((places, 32, 128), BF16),
-            pltpu.HBM((2, places * 16, 128), F32),
-            pltpu.HBM(cube, F32),
-        ],
-        in_specs=[vmem] * 5,
-        out_specs=[vmem, vmem, raw],
-        scratch_shapes=[pltpu.VMEM((4, 24, 128), F32), pltpu.SemaphoreType.DMA],
+        out_shape=jax.ShapeDtypeStruct((places, 32, 128), BF16),
+        scratch_shapes=[
+            pltpu.VMEM((4, 24, 128), F32),
+            pltpu.VMEM((2, places * 16, 128), F32),
+        ],
         compiler_params=params(6, None),
         name="spread",
-    )(*seen, acc)
+    )(*seen)
     rings = [[t * QUAD + s for t in range(places)] for s in range(QUAD)]
     in_msg = lax.all_to_all(out_msg, "curve", 0, 0, tiled=True, axis_index_groups=rings)
 
@@ -396,10 +403,14 @@
     back = pl.pallas_call(
         collect_kernel,
         out_shape=[jax.ShapeDtypeStruct((32, 128), BF16)] * 4,
-        scratch_shapes=[pltpu.VMEM((256, 128), F32), pltpu.VMEM((16, 128), F32)],
+        scratch_shapes=[
+            pltpu.VMEM((256, 128), F32),
+            pltpu.VMEM((4, 24, 128), F32),
+            pltpu.VMEM((2, places * 16, 128), F32),
+        ],
         compiler_params=params(6, None),
         name="collect",
-    )(in_msg, couple)
+    )(in_msg, *seen)
     near_back, own_back = pl.pallas_call(
         fetch_kernel,
         out_shape=[pltpu.VMEM(cube, F32)] * 2,

time: 68.7 us -> 56.1 us (0.82)
  the two profiles are of different devices: /device:TPU:1 before, /device:TPU:7 now
where the time goes in v5:
time: 56.1 us; the launch traced here: 55.8 us
  Pallas kernels  24.1 us (43%)
  starting transfers between devices  23.1 us (41%)
  waiting for transfers between devices  7.55 us (13%)
  between operations  1.03 us (2%)
    all_to_all x1, starting transfers between devices, layer_step(): lax.all_to_all(out_msg, 'curve', 0, 0, tiled=True, axis_index_groups=rings)  10.3 us
    pallas_call x1, Pallas kernels, layer_step(): pl.pallas_call(forward_kernel, out_shape=pltpu.HBM(cube, F32), in_specs=[...  7.51 us
    pallas_call x1, Pallas kernels, layer_step(): pl.pallas_call(backward_kernel, out_shape=[jax.ShapeDtypeStruct(cube, BF1...  6.87 us
    all_to_all x1, waiting for transfers between devices, layer_step(): lax.all_to_all(out_msg, 'curve', 0, 0, tiled=True, axis_index_groups=rings)  4.56 us
    ppermute x1, starting transfers between devices, layer_step(): lax.ppermute(features, 'curve', [(i, i + 1) for i in range(groups - 1)])  3.82 us
    ppermute x3, starting transfers between devices, layer_step(): lax.ppermute(msgs[o], 'curve', [(i, i ^ o) for i in range(groups)])  3.64 us
    ppermute x1, waiting for transfers between devices, layer_step(): got = lax.ppermute(give, 'chan', [(0, 1), (1, 0)])  2.97 us
    pallas_call x1, Pallas kernels, layer_step(): pl.pallas_call(project_kernel, out_shape=[rows32, rows32, pltpu.VMEM(cube...  2.56 us
  transfers between devices with their start and end apart: 10, of which 2 were waited for; matrix products, arithmetic and copies ran while one was open for 0% of the time, Pallas kernels for 34%

profile of v5, /device:TPU:7, one launch (start us, length us, event | category | flops | bytes accessed | tf_op | source)
XLA Modules:
  0.0 55.8 jit_solution(9819028598726216306)
XLA Ops:
  0.6 0.0 copy-start.6
  0.6 0.0 copy-start.3
  0.7 0.0 copy-start.2
  0.7 0.0 copy-start.5
  0.7 0.0 copy-start.4
  0.7 2.6 %project.1 = (f32[32,128]{1,0:T(8,128)S(1)}, f32[32,128]{1,0:T(8,128)S(1)}, bf16[32,128,128]{2,1,0:T(8,128)(2,1)S(1)}) custom-call(bf16[32,128,128]{2,1,0:T(8,128)(2,1)} %bitcast.14, bf16[32,128,128]{2,1,0:T(8,128)(2,1)} %bitcast.13, bf16[32,16,128]{2,1,0:T(8,128)(2,1)} %b_in.3, bf16[32,16,128]{2,1,0:T(8,128)(2,1)} %bitcast.8, f32[256,256]{1,0:T(8,128)} %mix.1), custom_call_target="tpu_custom_call" | custom-call | tf_op jit(solution)/shard_map/project/pallas_call | solution.py:321
  3.2 1.2 %collective-permute-start.2 = (f32[32,128]{1,0:T(8,128)S(1)}, f32[32,128]{1,0:T(8,128)S(1)}, u32[]{:S(2)}, u32[]{:S(2)}) collective-permute-start(f32[32,128]{1,0:T(8,128)S(1)} %get-tuple-element.25), channel_id=1, source_target_pairs={{0,1},{1,0},{2,3},{3,2},{4,5},{5,4},{6,7},{7,6},{8,9},{9,8},{10,11... | collective-permute-start | bytes 49160 | tf_op jit(solution)/shard_map/ppermute | solution.py:342
  4.5 3.0 %collective-permute-done.2.got = f32[32,128]{1,0:T(8,128)S(1)} collective-permute-done((f32[32,128]{1,0:T(8,128)S(1)}, f32[32,128]{1,0:T(8,128)S(1)}, u32[]{:S(2)}, u32[]{:S(2)}) %collective-permute-start.2) | collective-permute-done | bytes 16416 | tf_op jit(solution)/shard_map/ppermute | solution.py:342
  7.4 0.0 copy-done.3
  7.4 0.0 copy-done.2
  7.4 0.6 %deal.1 = (f32[56,128]{1,0:T(8,128)S(1)}, f32[56,128]{1,0:T(8,128)S(1)}, f32[56,128]{1,0:T(8,128)S(1)}, f32[56,128]{1,0:T(8,128)S(1)}) custom-call(s32[1,8]{1,0:T(1,128)S(1)} %copy-done.3, f32[128,16]{1,0:T(8,128)S(1)} %bitcast.10, f32[32,128]{1,0:T(8,128)S(1)} %get-tuple-element.24.keep, f32[32,128]{1,0:T(8,128)S(1)} %collective-permute-done.2.got), custom_call_target="tpu_custom_call" | custom-call | tf_op jit(solution)/shard_map/deal/pallas_call | solution.py:344
  8.1 1.9 %collective-permute-start.3 = (f32[56,128]{1,0:T(8,128)S(1)}, f32[56,128]{1,0:T(8,128)S(1)}, u32[]{:S(2)}, u32[]{:S(2)}) collective-permute-start(f32[56,128]{1,0:T(8,128)S(1)} %get-tuple-element.27), channel_id=1, source_target_pairs={{0,2},{2,0},{4,6},{6,4},{8,10},{10,8},{12,14},{14,12},{16,18},{18,... | collective-permute-start | bytes 86024 | tf_op jit(solution)/shard_map/ppermute | solution.py:353
  10.0 0.5 collective-permute-start.4
  10.5 1.2 %collective-permute-start.5 = (f32[56,128]{1,0:T(8,128)S(1)}, f32[56,128]{1,0:T(8,128)S(1)}, u32[]{:S(2)}, u32[]{:S(2)}) collective-permute-start(f32[56,128]{1,0:T(8,128)S(1)} %get-tuple-element.29), channel_id=1, source_target_pairs={{0,6},{2,4},{4,2},{6,0},{8,14},{10,12},{12,10},{14,8},{16,22},{18,... | collective-permute-start | bytes 86024 | tf_op jit(solution)/shard_map/ppermute | solution.py:353
  11.7 0.0 copy-done.6
  11.7 3.8 %collective-permute-start = (bf16[4096,128]{1,0:T(8,128)(2,1)S(1)}, bf16[4096,128]{1,0:T(8,128)(2,1)}, u32[]{:S(2)}, u32[]{:S(2)}) collective-permute-start(bf16[4096,128]{1,0:T(8,128)(2,1)S(1)} %copy-done.6), channel_id=1, source_target_pairs={{0,2},{2,4},{4,6},{6,8},{8,10},{10,12},{12,14},{14,16},{16,18},{18... | collective-permute-start | bytes 3145736 | tf_op jit(solution)/shard_map/ppermute | solution.py:343
  15.6 0.0 collective-permute-done.3.refs_1_
  15.6 0.0 collective-permute-done.4.refs_2_
  15.6 0.0 collective-permute-done.5.refs_3_
  15.6 1.6 %spread.1 = bf16[32,32,128]{2,1,0:T(8,128)(2,1)} custom-call(f32[56,128]{1,0:T(8,128)S(1)} %get-tuple-element.26.refs_0_, f32[56,128]{1,0:T(8,128)S(1)} %collective-permute-done.3.refs_1_, f32[56,128]{1,0:T(8,128)S(1)} %collective-permute-done.4.refs_2_, f32[56,128]{1,0:T(8,128)S(1)} %collective-permute-done.5.refs_3_), custom_call_target="tpu_custom_call" | custom-call | tf_op jit(solution)/shard_map/spread/pallas_call | solution.py:372
  17.2 10.3 %all-to-all-start = ((bf16[32,32,128]{2,1,0:T(8,128)(2,1)}), bf16[32,32,128]{2,1,0:T(8,128)(2,1)S(1)}, u32[]{:S(2)}, u32[]{:S(2)}) async-start(bf16[32,32,128]{2,1,0:T(8,128)(2,1)} %spread.1), calls=%async_computation | async-start | bytes 524288 | tf_op jit(solution)/shard_map/all_to_all | solution.py:383
  27.5 0.0 copy-done.5
  27.5 0.0 copy-done.4
  27.5 6.9 %backward.1 = (bf16[32,128,128]{2,1,0:T(8,128)(2,1)S(1)}, f32[32,128,128]{2,1,0:T(8,128)}) custom-call(s32[8,32]{1,0:T(8,128)S(1)} %bitcast.11, s32[32]{0:T(128)S(1)} %copy-done.5, bf16[32,8,128,128]{3,2,1,0:T(8,128)(2,1)} %near.3, bf16[32,128,128]{2,1,0:T(8,128)(2,1)S(1)} %get-tuple-element.19.cot), custom_call_target="tpu_custom_call" | custom-call | flops 8589934592 | bytes 12582912 | tf_op jit(solution)/shard_map/backward/pallas_call | solution.py:355
  34.4 1.9 %collective-permute-start.1 = (bf16[32,128,128]{2,1,0:T(8,128)(2,1)S(1)}, bf16[32,128,128]{2,1,0:T(8,128)(2,1)S(1)}, u32[]{:S(2)}, u32[]{:S(2)}) collective-permute-start(bf16[32,128,128]{2,1,0:T(8,128)(2,1)S(1)} %get-tuple-element.23), channel_id=1, source_target_pairs={{2,0},{4,2},{6,4},{8,6},{10,8},{12,10},{14,12},{16,14},{18,16},{20... | collective-permute-start | bytes 3145736 | tf_op jit(solution)/shard_map/ppermute | solution.py:370
  36.3 4.6 %all-to-all-done.arrived = bf16[32,32,128]{2,1,0:T(8,128)(2,1)S(1)} async-done(((bf16[32,32,128]{2,1,0:T(8,128)(2,1)}), bf16[32,32,128]{2,1,0:T(8,128)(2,1)S(1)}, u32[]{:S(2)}, u32[]{:S(2)}) %all-to-all-start) | async-done | bytes 262176 | tf_op jit(solution)/shard_map/all_to_all | solution.py:383
  40.9 0.9 %collect.1 = (bf16[32,128]{1,0:T(8,128)(2,1)S(1)}, bf16[32,128]{1,0:T(8,128)(2,1)S(1)}, bf16[32,128]{1,0:T(8,128)(2,1)S(1)}, bf16[32,128]{1,0:T(8,128)(2,1)S(1)}) custom-call(bf16[32,32,128]{2,1,0:T(8,128)(2,1)S(1)} %all-to-all-done.arrived, f32[56,128]{1,0:T(8,128)S(1)} %get-tuple-element.26.refs_0_, f32[56,128]{1,0:T(8,128)S(1)} %collective-permute-done.3.refs_1_, ...), custom_call_target="tpu_custom_call" | custom-call | tf_op jit(solution)/shard_map/collect/pallas_call | solution.py:403
  41.8 0.1 collective-permute-start.6
  41.9 0.1 collective-permute-start.7
  42.0 2.0 %collective-permute-start.8 = (bf16[32,128]{1,0:T(8,128)(2,1)S(1)}, bf16[32,128]{1,0:T(8,128)(2,1)S(1)}, u32[]{:S(2)}, u32[]{:S(2)}) collective-permute-start(bf16[32,128]{1,0:T(8,128)(2,1)S(1)} %get-tuple-element.33), channel_id=1, source_target_pairs={{0,6},{2,4},{4,2},{6,0},{8,14},{10,12},{12,10},{14,8},{16,22},{18,... | collective-permute-start | bytes 24584 | tf_op jit(solution)/shard_map/ppermute | solution.py:426
  44.0 0.0 collective-permute-done
  44.0 7.5 %forward.1.near = f32[32,128,128]{2,1,0:T(8,128)} custom-call(s32[8,32]{1,0:T(8,128)S(1)} %bitcast.12, s32[32]{0:T(128)S(1)} %copy-done.5, bf16[32,8,128,128]{3,2,1,0:T(8,128)(2,1)} %near.3, bf16[32,128,128]{2,1,0:T(8,128)(2,1)} %bitcast.1.halo, bf16[32,128,128]{2,1,0:T(8,128)(2,1)} %bitcast.15), custom_call_target="tpu_custom_call" | custom-call | flops 8589934592 | bytes 12582912 | tf_op jit(solution)/shard_map/forward/pallas_call | solution.py:385
  51.5 0.0 copy-start
  51.5 0.0 copy-start.1
  51.5 2.3 %fetch.1 = (f32[32,128,128]{2,1,0:T(8,128)S(1)}, f32[32,128,128]{2,1,0:T(8,128)S(1)}) custom-call(f32[32,128,128]{2,1,0:T(8,128)} %forward.1.near, f32[32,128,128]{2,1,0:T(8,128)} %get-tuple-element.20.own), custom_call_target="tpu_custom_call" | custom-call | flops 1048576 | bytes 8388608 | tf_op jit(solution)/shard_map/fetch/pallas_call | solution.py:414
  53.8 0.0 collective-permute-done.6.m1
  53.8 0.0 collective-permute-done.7.m2
  53.9 0.0 collective-permute-done.8.m3
  53.9 0.0 collective-permute-done.1.arrived
  53.9 0.0 copy-done
  53.9 0.0 copy-done.1
  53.9 1.8 %finish.1 = (bf16[32,128,128]{2,1,0:T(8,128)(2,1)}, bf16[32,128,128]{2,1,0:T(8,128)(2,1)}) custom-call(f32[32,128,128]{2,1,0:T(8,128)S(1)} %get-tuple-element.21.near, f32[32,128,128]{2,1,0:T(8,128)S(1)} %get-tuple-element.22.own, bf16[32,128,128]{2,1,0:T(8,128)(2,1)S(1)} %collective-permute-done.1.arrived, bf16[32,16,128]{2,1,0:T(8,128)(2,1)S(1)} %copy-done, ...), custom_call_target="tpu_custom_call" | custom-call | tf_op jit(solution)/shard_map/finish/pallas_call | solution.py:428
Async XLA Ops:
  0.6 11.1 %copy-start.6 = (bf16[4096,128]{1,0:T(8,128)(2,1)S(1)}, bf16[4096,128]{1,0:T(8,128)(2,1)}, u32[]{:S(2)}) copy-start(bf16[4096,128]{1,0:T(8,128)(2,1)} %param.10) | copy-start | bytes 3145732
  0.6 6.8 %copy-start.3 = (s32[1,8]{1,0:T(1,128)S(1)}, s32[1,8]{1,0:T(1,128)}, u32[]{:S(2)}) copy-start(s32[1,8]{1,0:T(1,128)} %far_index.1) | copy-start | bytes 100
  0.7 6.8 %copy-start.2 = (f32[1,8,16,16]{3,2,1,0:T(8,128)S(1)}, f32[1,8,16,16]{3,2,1,0:T(8,128)}, u32[]{:S(2)}) copy-start(f32[1,8,16,16]{3,2,1,0:T(8,128)} %param.17) | copy-start | bytes 24580
  0.7 26.8 %copy-start.5 = (s32[32]{0:T(128)S(1)}, s32[32]{0:T(128)}, u32[]{:S(2)}) copy-start(s32[32]{0:T(128)} %count.3) | copy-start | bytes 388
  0.7 26.8 %copy-start.4 = (s32[32,8]{0,1:T(8,128)S(1)}, s32[32,8]{0,1:T(8,128)}, u32[]{:S(2)}) copy-start(s32[32,8]{0,1:T(8,128)} %param.13) | copy-start | bytes 3076
  3.2 4.2 %collective-permute-start.2 = (f32[32,128]{1,0:T(8,128)S(1)}, f32[32,128]{1,0:T(8,128)S(1)}, u32[]{:S(2)}, u32[]{:S(2)}) collective-permute-start(f32[32,128]{1,0:T(8,128)S(1)} %get-tuple-element.25), channel_id=1, source_target_pairs={{0,1},{1,0},{2,3},{3,2},{4,5},{5,4},{6,7},{7,6},{8,9},{9,8},{10,11... | collective-permute-start | bytes 49160 | tf_op jit(solution)/shard_map/ppermute | solution.py:342
  8.1 7.5 %collective-permute-start.3 = (f32[56,128]{1,0:T(8,128)S(1)}, f32[56,128]{1,0:T(8,128)S(1)}, u32[]{:S(2)}, u32[]{:S(2)}) collective-permute-start(f32[56,128]{1,0:T(8,128)S(1)} %get-tuple-element.27), channel_id=1, source_target_pairs={{0,2},{2,0},{4,6},{6,4},{8,10},{10,8},{12,14},{14,12},{16,18},{18,... | collective-permute-start | bytes 86024 | tf_op jit(solution)/shard_map/ppermute | solution.py:353
  10.0 5.6 %collective-permute-start.4 = (f32[56,128]{1,0:T(8,128)S(1)}, f32[56,128]{1,0:T(8,128)S(1)}, u32[]{:S(2)}, u32[]{:S(2)}) collective-permute-start(f32[56,128]{1,0:T(8,128)S(1)} %get-tuple-element.28), channel_id=1, source_target_pairs={{0,4},{2,6},{4,0},{6,2},{8,12},{10,14},{12,8},{14,10},{16,20},{18,... | collective-permute-start | bytes 86024 | tf_op jit(solution)/shard_map/ppermute | solution.py:353
  10.5 5.0 %collective-permute-start.5 = (f32[56,128]{1,0:T(8,128)S(1)}, f32[56,128]{1,0:T(8,128)S(1)}, u32[]{:S(2)}, u32[]{:S(2)}) collective-permute-start(f32[56,128]{1,0:T(8,128)S(1)} %get-tuple-element.29), channel_id=1, source_target_pairs={{0,6},{2,4},{4,2},{6,0},{8,14},{10,12},{12,10},{14,8},{16,22},{18,... | collective-permute-start | bytes 86024 | tf_op jit(solution)/shard_map/ppermute | solution.py:353
  11.7 32.3 %collective-permute-start = (bf16[4096,128]{1,0:T(8,128)(2,1)S(1)}, bf16[4096,128]{1,0:T(8,128)(2,1)}, u32[]{:S(2)}, u32[]{:S(2)}) collective-permute-start(bf16[4096,128]{1,0:T(8,128)(2,1)S(1)} %copy-done.6), channel_id=1, source_target_pairs={{0,2},{2,4},{4,6},{6,8},{8,10},{10,12},{12,14},{14,16},{16,18},{18... | collective-permute-start | bytes 3145736 | tf_op jit(solution)/shard_map/ppermute | solution.py:343
  17.2 23.7 %all-to-all-start = ((bf16[32,32,128]{2,1,0:T(8,128)(2,1)}), bf16[32,32,128]{2,1,0:T(8,128)(2,1)S(1)}, u32[]{:S(2)}, u32[]{:S(2)}) async-start(bf16[32,32,128]{2,1,0:T(8,128)(2,1)} %spread.1), calls=%async_computation | async-start | bytes 524288 | tf_op jit(solution)/shard_map/all_to_all | solution.py:383
  34.4 19.5 %collective-permute-start.1 = (bf16[32,128,128]{2,1,0:T(8,128)(2,1)S(1)}, bf16[32,128,128]{2,1,0:T(8,128)(2,1)S(1)}, u32[]{:S(2)}, u32[]{:S(2)}) collective-permute-start(bf16[32,128,128]{2,1,0:T(8,128)(2,1)S(1)} %get-tuple-element.23), channel_id=1, source_target_pairs={{2,0},{4,2},{6,4},{8,6},{10,8},{12,10},{14,12},{16,14},{18,16},{20... | collective-permute-start | bytes 3145736 | tf_op jit(solution)/shard_map/ppermute | solution.py:370
  41.8 12.1 %collective-permute-start.6 = (bf16[32,128]{1,0:T(8,128)(2,1)S(1)}, bf16[32,128]{1,0:T(8,128)(2,1)S(1)}, u32[]{:S(2)}, u32[]{:S(2)}) collective-permute-start(bf16[32,128]{1,0:T(8,128)(2,1)S(1)} %get-tuple-element.31), channel_id=1, source_target_pairs={{0,2},{2,0},{4,6},{6,4},{8,10},{10,8},{12,14},{14,12},{16,18},{18,... | collective-permute-start | bytes 24584 | tf_op jit(solution)/shard_map/ppermute | solution.py:426
  41.9 12.0 %collective-permute-start.7 = (bf16[32,128]{1,0:T(8,128)(2,1)S(1)}, bf16[32,128]{1,0:T(8,128)(2,1)S(1)}, u32[]{:S(2)}, u32[]{:S(2)}) collective-permute-start(bf16[32,128]{1,0:T(8,128)(2,1)S(1)} %get-tuple-element.32), channel_id=1, source_target_pairs={{0,4},{2,6},{4,0},{6,2},{8,12},{10,14},{12,8},{14,10},{16,20},{18,... | collective-permute-start | bytes 24584 | tf_op jit(solution)/shard_map/ppermute | solution.py:426
  42.0 11.9 %collective-permute-start.8 = (bf16[32,128]{1,0:T(8,128)(2,1)S(1)}, bf16[32,128]{1,0:T(8,128)(2,1)S(1)}, u32[]{:S(2)}, u32[]{:S(2)}) collective-permute-start(bf16[32,128]{1,0:T(8,128)(2,1)S(1)} %get-tuple-element.33), channel_id=1, source_target_pairs={{0,6},{2,4},{4,2},{6,0},{8,14},{10,12},{12,10},{14,8},{16,22},{18,... | collective-permute-start | bytes 24584 | tf_op jit(solution)/shard_map/ppermute | solution.py:426
  51.5 2.4 %copy-start = (bf16[32,16,128]{2,1,0:T(8,128)(2,1)S(1)}, bf16[32,16,128]{2,1,0:T(8,128)(2,1)}, u32[]{:S(2)}) copy-start(bf16[32,16,128]{2,1,0:T(8,128)(2,1)} %b_in.3) | copy-start | bytes 393220
  51.5 2.4 %copy-start.1 = (bf16[32,128,16]{1,2,0:T(8,128)(2,1)S(1)}, bf16[32,128,16]{1,2,0:T(8,128)(2,1)}, u32[]{:S(2)}) copy-start(bf16[32,128,16]{1,2,0:T(8,128)(2,1)} %param.16) | copy-start | bytes 393220

commit v6 on v5

--- a/solution.py
+++ b/solution.py
@@ -11,6 +11,7 @@
 MIB = 1 << 20
 QUAD = 4
 PARTS = 4
+UNROLL = 4
 CHUNKS = 8
 AHEAD = 3
 
@@ -124,28 +125,27 @@
     ]
 
 
-def backward_kernel(index, count, near, cot, prev, own, acc, near_v, sems, out_sems):
+def backward_kernel(index, count, near, cot, prev, own, acc, out_sems):
     base = (lax.axis_index("curve") - 1) * 32
-    copies = tile_copies(near, near_v, sems)[::-1]
-    for copy in copies[:AHEAD]:
-        copy.start()
     acc[...] = jnp.zeros_like(acc)
-    part = near.shape[0] // CHUNKS
+    part = near.shape[0] // PARTS
     stores = []
-    for turn, copy in enumerate(copies):
-        copy.wait()
-        if turn + AHEAD < CHUNKS:
-            copies[turn + AHEAD].start()
-        n = CHUNKS - 1 - turn
-        for b in range(n * part, (n + 1) * part):
-            cot_t = cot[b].T
-            live = count[b]
-            for k in range(0, 8, 2):
-                pair = jnp.concatenate([near_v[b, k], near_v[b, k + 1]], axis=1)
-                term = dot(cot_t, pair)
-                for j in range(2):
-                    row = jnp.where(k + j < live, index[k + j, b] - base, 64)
-                    acc[row] += term[:, j * 128 : (j + 1) * 128]
+    for n in reversed(range(PARTS)):
+
+        def some(step, carry):
+            for i in range(UNROLL):
+                b = (n + 1) * part - 1 - (step * UNROLL + i)
+                cot_t = cot[b].T
+                live = count[b]
+                for k in range(0, 8, 2):
+                    pair = jnp.concatenate([near[b, k], near[b, k + 1]], axis=1)
+                    term = dot(cot_t, pair)
+                    for j in range(2):
+                        row = jnp.where(k + j < live, index[k + j, b] - base, 64)
+                        acc[row] += term[:, j * 128 : (j + 1) * 128]
+            return carry
+
+        lax.fori_loop(0, part // UNROLL, some, 0)
         done = acc.at[pl.ds(32 + n * part, part)]
         stores.append(pltpu.make_async_copy(done, own.at[pl.ds(n * part, part)], out_sems.at[n]))
         stores[-1].start()
@@ -331,6 +331,7 @@
             pltpu.SemaphoreType.DMA((PARTS + 1, 4)),
         ],
         compiler_params=params(14, None),
+        cost_estimate=pl.CostEstimate(flops=8 << 30, bytes_accessed=3 << 20, transcendentals=0),
         name="project",
     )(
         hbm(features.reshape(cube)),
@@ -355,18 +356,16 @@
     prev, own = pl.pallas_call(
         backward_kernel,
         out_shape=[jax.ShapeDtypeStruct(cube, BF16), pltpu.HBM(cube, F32)],
-        in_specs=[smem, smem, raw, vmem],
+        in_specs=[smem, smem, vmem, vmem],
         out_specs=[vmem, raw],
         scratch_shapes=[
             pltpu.VMEM((2 * blocks + 1, 128, 128), F32),
-            pltpu.VMEM(near_kernel.shape, BF16),
-            pltpu.SemaphoreType.DMA((CHUNKS,)),
-            pltpu.SemaphoreType.DMA((CHUNKS,)),
+            pltpu.SemaphoreType.DMA((PARTS,)),
         ],
         compiler_params=params(16, None),
         cost_estimate=pl.CostEstimate(flops=8 << 30, bytes_accessed=12 << 20, transcendentals=0),
         name="backward",
-    )(index, near_count, hbm(near_kernel), cot_v)
+    )(index, near_count, near_kernel, cot_v)
     arrived = lax.ppermute(prev, "curve", [(i + 1, i) for i in range(groups - 1)])
 
     out_msg = pl.pallas_call(

time: 56.1 us -> 57 us (1.016)
  the two profiles are of different devices: /device:TPU:7 before, /device:TPU:25 now
where the time goes in v6:
time: 57 us; the launch traced here: 56.7 us
  starting transfers between devices  27.8 us (49%)
  Pallas kernels  23.1 us (41%)
  local copies, waits for them, and re-layouts  3.41 us (6%)
  waiting for transfers between devices  1.37 us (2%)
  between operations  1.03 us (2%)
    all_to_all x1, starting transfers between devices, layer_step(): lax.all_to_all(out_msg, 'curve', 0, 0, tiled=True, axis_index_groups=rings)  11 us
    pallas_call x1, Pallas kernels, layer_step(): pl.pallas_call(forward_kernel, out_shape=pltpu.HBM(cube, F32), in_specs=[...  7.52 us
    pallas_call x1, Pallas kernels, layer_step(): pl.pallas_call(backward_kernel, out_shape=[jax.ShapeDtypeStruct(cube, BF1...  5.82 us
    ppermute x3, starting transfers between devices, layer_step(): lax.ppermute(back[o], 'curve', [(i, i ^ o) for i in range(groups)])  4.77 us
    ppermute x3, starting transfers between devices, layer_step(): lax.ppermute(msgs[o], 'curve', [(i, i ^ o) for i in range(groups)])  3.64 us
    unnamed x16, local copies, waits for them, and re-layouts  3.41 us
    ppermute x1, starting transfers between devices, layer_step(): lax.ppermute(features, 'curve', [(i, i + 1) for i in range(groups - 1)])  3.12 us
    ppermute x1, starting transfers between devices, layer_step(): got = lax.ppermute(give, 'chan', [(0, 1), (1, 0)])  2.83 us
  transfers between devices with their start and end apart: 10, of which 1 were waited for; matrix products, arithmetic and copies ran while one was open for 0% of the time, Pallas kernels for 32%

profile of v6, /device:TPU:25, one launch (start us, length us, event | category | flops | bytes accessed | tf_op | source)
XLA Modules:
  0.0 56.7 jit_solution(18386441258839535747)
XLA Ops:
  0.6 0.0 copy-start.2
  0.6 0.0 copy-start.3
  0.7 0.0 copy-start.7
  0.7 0.0 copy-start.5
  0.7 0.0 copy-start.6
  0.7 2.6 %project.1 = (f32[32,128]{1,0:T(8,128)S(1)}, f32[32,128]{1,0:T(8,128)S(1)}, bf16[32,128,128]{2,1,0:T(8,128)(2,1)S(1)}) custom-call(bf16[32,128,128]{2,1,0:T(8,128)(2,1)} %bitcast.14, bf16[32,128,128]{2,1,0:T(8,128)(2,1)} %bitcast.13, bf16[32,16,128]{2,1,0:T(8,128)(2,1)} %b_in.3, bf16[32,16,128]{2,1,0:T(8,128)(2,1)} %bitcast.8, f32[256,256]{1,0:T(8,128)} %mix.1), custom_call_target="tpu_custom_call" | custom-call | flops 8589934592 | bytes 3145728 | tf_op jit(solution)/shard_map/project/pallas_call | solution.py:321
  3.3 2.8 %collective-permute-start.2 = (f32[32,128]{1,0:T(8,128)S(1)}, f32[32,128]{1,0:T(8,128)S(1)}, u32[]{:S(2)}, u32[]{:S(2)}) collective-permute-start(f32[32,128]{1,0:T(8,128)S(1)} %get-tuple-element.25), channel_id=1, source_target_pairs={{0,1},{1,0},{2,3},{3,2},{4,5},{5,4},{6,7},{7,6},{8,9},{9,8},{10,11... | collective-permute-start | bytes 49160 | tf_op jit(solution)/shard_map/ppermute | solution.py:343
  6.1 1.4 %collective-permute-done.2.got = f32[32,128]{1,0:T(8,128)S(1)} collective-permute-done((f32[32,128]{1,0:T(8,128)S(1)}, f32[32,128]{1,0:T(8,128)S(1)}, u32[]{:S(2)}, u32[]{:S(2)}) %collective-permute-start.2) | collective-permute-done | bytes 16416 | tf_op jit(solution)/shard_map/ppermute | solution.py:343
  7.4 0.0 copy-done.2
  7.4 0.0 copy-done.3
  7.4 0.6 %deal.1 = (f32[56,128]{1,0:T(8,128)S(1)}, f32[56,128]{1,0:T(8,128)S(1)}, f32[56,128]{1,0:T(8,128)S(1)}, f32[56,128]{1,0:T(8,128)S(1)}) custom-call(s32[1,8]{1,0:T(1,128)S(1)} %copy-done.3, f32[128,16]{1,0:T(8,128)S(1)} %bitcast.10, f32[32,128]{1,0:T(8,128)S(1)} %get-tuple-element.24.keep, f32[32,128]{1,0:T(8,128)S(1)} %collective-permute-done.2.got), custom_call_target="tpu_custom_call" | custom-call | tf_op jit(solution)/shard_map/deal/pallas_call | solution.py:345
  8.1 1.9 %collective-permute-start.3 = (f32[56,128]{1,0:T(8,128)S(1)}, f32[56,128]{1,0:T(8,128)S(1)}, u32[]{:S(2)}, u32[]{:S(2)}) collective-permute-start(f32[56,128]{1,0:T(8,128)S(1)} %get-tuple-element.27), channel_id=1, source_target_pairs={{0,2},{2,0},{4,6},{6,4},{8,10},{10,8},{12,14},{14,12},{16,18},{18,... | collective-permute-start | bytes 86024 | tf_op jit(solution)/shard_map/ppermute | solution.py:354
  10.0 1.2 %collective-permute-start.4 = (f32[56,128]{1,0:T(8,128)S(1)}, f32[56,128]{1,0:T(8,128)S(1)}, u32[]{:S(2)}, u32[]{:S(2)}) collective-permute-start(f32[56,128]{1,0:T(8,128)S(1)} %get-tuple-element.28), channel_id=1, source_target_pairs={{0,4},{2,6},{4,0},{6,2},{8,12},{10,14},{12,8},{14,10},{16,20},{18,... | collective-permute-start | bytes 86024 | tf_op jit(solution)/shard_map/ppermute | solution.py:354
  11.2 0.5 collective-permute-start.5
  11.7 0.0 copy-done.7
  11.7 3.1 %collective-permute-start = (bf16[4096,128]{1,0:T(8,128)(2,1)S(1)}, bf16[4096,128]{1,0:T(8,128)(2,1)}, u32[]{:S(2)}, u32[]{:S(2)}) collective-permute-start(bf16[4096,128]{1,0:T(8,128)(2,1)S(1)} %copy-done.7), channel_id=1, source_target_pairs={{0,2},{2,4},{4,6},{6,8},{8,10},{10,12},{12,14},{14,16},{16,18},{18... | collective-permute-start | bytes 3145736 | tf_op jit(solution)/shard_map/ppermute | solution.py:344
  14.9 0.0 collective-permute-done.3.refs_1_
  14.9 0.0 collective-permute-done.4.refs_2_
  14.9 0.0 collective-permute-done.5.refs_3_
  14.9 1.6 %spread.1 = bf16[32,32,128]{2,1,0:T(8,128)(2,1)} custom-call(f32[56,128]{1,0:T(8,128)S(1)} %get-tuple-element.26.refs_0_, f32[56,128]{1,0:T(8,128)S(1)} %collective-permute-done.3.refs_1_, f32[56,128]{1,0:T(8,128)S(1)} %collective-permute-done.4.refs_2_, f32[56,128]{1,0:T(8,128)S(1)} %collective-permute-done.5.refs_3_), custom_call_target="tpu_custom_call" | custom-call | tf_op jit(solution)/shard_map/spread/pallas_call | solution.py:371
  16.5 11.0 %all-to-all-start = ((bf16[32,32,128]{2,1,0:T(8,128)(2,1)}), bf16[32,32,128]{2,1,0:T(8,128)(2,1)S(1)}, u32[]{:S(2)}, u32[]{:S(2)}) async-start(bf16[32,32,128]{2,1,0:T(8,128)(2,1)} %spread.1), calls=%async_computation | async-start | bytes 524288 | tf_op jit(solution)/shard_map/all_to_all | solution.py:382
  27.4 0.0 copy-done.5
  27.4 0.0 copy-done.6
  27.5 0.0 copy-start.4
  27.5 3.4 %copy-done.4 = bf16[32,8,128,128]{3,2,1,0:T(8,128)(2,1)S(1)} copy-done((bf16[32,8,128,128]{3,2,1,0:T(8,128)(2,1)S(1)}, bf16[32,8,128,128]{3,2,1,0:T(8,128)(2,1)}, u32[]{:S(2)}) %copy-start.4) | copy-done | bytes 8388632
  30.8 5.8 %backward.1 = (bf16[32,128,128]{2,1,0:T(8,128)(2,1)S(1)}, f32[32,128,128]{2,1,0:T(8,128)}) custom-call(s32[8,32]{1,0:T(8,128)S(1)} %bitcast.11, s32[32]{0:T(128)S(1)} %copy-done.6, bf16[32,8,128,128]{3,2,1,0:T(8,128)(2,1)S(1)} %copy-done.4, bf16[32,128,128]{2,1,0:T(8,128)(2,1)S(1)} %get-tuple-element.19.cot), custom_call_target="tpu_custom_call" | custom-call | flops 8589934592 | bytes 12582912 | tf_op jit(solution)/shard_map/backward/pallas_call | solution.py:356
  36.7 2.4 %collective-permute-start.1 = (bf16[32,128,128]{2,1,0:T(8,128)(2,1)S(1)}, bf16[32,128,128]{2,1,0:T(8,128)(2,1)S(1)}, u32[]{:S(2)}, u32[]{:S(2)}) collective-permute-start(bf16[32,128,128]{2,1,0:T(8,128)(2,1)S(1)} %get-tuple-element.23), channel_id=1, source_target_pairs={{2,0},{4,2},{6,4},{8,6},{10,8},{12,10},{14,12},{16,14},{18,16},{20... | collective-permute-start | bytes 3145736 | tf_op jit(solution)/shard_map/ppermute | solution.py:369
  39.1 0.0 all-to-all-done.arrived
  39.1 0.9 %collect.1 = (bf16[32,128]{1,0:T(8,128)(2,1)S(1)}, bf16[32,128]{1,0:T(8,128)(2,1)S(1)}, bf16[32,128]{1,0:T(8,128)(2,1)S(1)}, bf16[32,128]{1,0:T(8,128)(2,1)S(1)}) custom-call(bf16[32,32,128]{2,1,0:T(8,128)(2,1)S(1)} %all-to-all-done.arrived, f32[56,128]{1,0:T(8,128)S(1)} %get-tuple-element.26.refs_0_, f32[56,128]{1,0:T(8,128)S(1)} %collective-permute-done.3.refs_1_, ...), custom_call_target="tpu_custom_call" | custom-call | tf_op jit(solution)/shard_map/collect/pallas_call | solution.py:402
  40.1 3.0 %collective-permute-start.6 = (bf16[32,128]{1,0:T(8,128)(2,1)S(1)}, bf16[32,128]{1,0:T(8,128)(2,1)S(1)}, u32[]{:S(2)}, u32[]{:S(2)}) collective-permute-start(bf16[32,128]{1,0:T(8,128)(2,1)S(1)} %get-tuple-element.31), channel_id=1, source_target_pairs={{0,2},{2,0},{4,6},{6,4},{8,10},{10,8},{12,14},{14,12},{16,18},{18,... | collective-permute-start | bytes 24584 | tf_op jit(solution)/shard_map/ppermute | solution.py:425
  43.1 0.0 collective-permute-start.7
  43.1 1.7 %collective-permute-start.8 = (bf16[32,128]{1,0:T(8,128)(2,1)S(1)}, bf16[32,128]{1,0:T(8,128)(2,1)S(1)}, u32[]{:S(2)}, u32[]{:S(2)}) collective-permute-start(bf16[32,128]{1,0:T(8,128)(2,1)S(1)} %get-tuple-element.33), channel_id=1, source_target_pairs={{0,6},{2,4},{4,2},{6,0},{8,14},{10,12},{12,10},{14,8},{16,22},{18,... | collective-permute-start | bytes 24584 | tf_op jit(solution)/shard_map/ppermute | solution.py:425
  44.8 0.0 collective-permute-done
  44.8 7.5 %forward.1.near = f32[32,128,128]{2,1,0:T(8,128)} custom-call(s32[8,32]{1,0:T(8,128)S(1)} %bitcast.12, s32[32]{0:T(128)S(1)} %copy-done.6, bf16[32,8,128,128]{3,2,1,0:T(8,128)(2,1)} %near.3, bf16[32,128,128]{2,1,0:T(8,128)(2,1)} %bitcast.1.halo, bf16[32,128,128]{2,1,0:T(8,128)(2,1)} %bitcast.15), custom_call_target="tpu_custom_call" | custom-call | flops 8589934592 | bytes 12582912 | tf_op jit(solution)/shard_map/forward/pallas_call | solution.py:384
  52.4 0.0 copy-start
  52.4 0.0 copy-start.1
  52.4 2.3 %fetch.1 = (f32[32,128,128]{2,1,0:T(8,128)S(1)}, f32[32,128,128]{2,1,0:T(8,128)S(1)}) custom-call(f32[32,128,128]{2,1,0:T(8,128)} %forward.1.near, f32[32,128,128]{2,1,0:T(8,128)} %get-tuple-element.20.own), custom_call_target="tpu_custom_call" | custom-call | flops 1048576 | bytes 8388608 | tf_op jit(solution)/shard_map/fetch/pallas_call | solution.py:413
  54.7 0.0 collective-permute-done.6.m1
  54.7 0.0 collective-permute-done.7.m2
  54.7 0.0 collective-permute-done.8.m3
  54.7 0.0 collective-permute-done.1.arrived
  54.7 0.0 copy-done
  54.7 0.0 copy-done.1
  54.7 1.8 %finish.1 = (bf16[32,128,128]{2,1,0:T(8,128)(2,1)}, bf16[32,128,128]{2,1,0:T(8,128)(2,1)}) custom-call(f32[32,128,128]{2,1,0:T(8,128)S(1)} %get-tuple-element.21.near, f32[32,128,128]{2,1,0:T(8,128)S(1)} %get-tuple-element.22.own, bf16[32,128,128]{2,1,0:T(8,128)(2,1)S(1)} %collective-permute-done.1.arrived, bf16[32,16,128]{2,1,0:T(8,128)(2,1)S(1)} %copy-done, ...), custom_call_target="tpu_custom_call" | custom-call | tf_op jit(solution)/shard_map/finish/pallas_call | solution.py:427
Async XLA Ops:
  0.6 6.8 %copy-start.2 = (f32[1,8,16,16]{3,2,1,0:T(8,128)S(1)}, f32[1,8,16,16]{3,2,1,0:T(8,128)}, u32[]{:S(2)}) copy-start(f32[1,8,16,16]{3,2,1,0:T(8,128)} %param.17) | copy-start | bytes 24580
  0.6 6.8 %copy-start.3 = (s32[1,8]{1,0:T(1,128)S(1)}, s32[1,8]{1,0:T(1,128)}, u32[]{:S(2)}) copy-start(s32[1,8]{1,0:T(1,128)} %far_index.1) | copy-start | bytes 100
  0.7 11.1 %copy-start.7 = (bf16[4096,128]{1,0:T(8,128)(2,1)S(1)}, bf16[4096,128]{1,0:T(8,128)(2,1)}, u32[]{:S(2)}) copy-start(bf16[4096,128]{1,0:T(8,128)(2,1)} %param.10) | copy-start | bytes 3145732
  0.7 26.8 %copy-start.5 = (s32[32,8]{0,1:T(8,128)S(1)}, s32[32,8]{0,1:T(8,128)}, u32[]{:S(2)}) copy-start(s32[32,8]{0,1:T(8,128)} %param.13) | copy-start | bytes 3076
  0.7 26.8 %copy-start.6 = (s32[32]{0:T(128)S(1)}, s32[32]{0:T(128)}, u32[]{:S(2)}) copy-start(s32[32]{0:T(128)} %count.3) | copy-start | bytes 388
  3.3 4.2 %collective-permute-start.2 = (f32[32,128]{1,0:T(8,128)S(1)}, f32[32,128]{1,0:T(8,128)S(1)}, u32[]{:S(2)}, u32[]{:S(2)}) collective-permute-start(f32[32,128]{1,0:T(8,128)S(1)} %get-tuple-element.25), channel_id=1, source_target_pairs={{0,1},{1,0},{2,3},{3,2},{4,5},{5,4},{6,7},{7,6},{8,9},{9,8},{10,11... | collective-permute-start | bytes 49160 | tf_op jit(solution)/shard_map/ppermute | solution.py:343
  8.1 6.8 %collective-permute-start.3 = (f32[56,128]{1,0:T(8,128)S(1)}, f32[56,128]{1,0:T(8,128)S(1)}, u32[]{:S(2)}, u32[]{:S(2)}) collective-permute-start(f32[56,128]{1,0:T(8,128)S(1)} %get-tuple-element.27), channel_id=1, source_target_pairs={{0,2},{2,0},{4,6},{6,4},{8,10},{10,8},{12,14},{14,12},{16,18},{18,... | collective-permute-start | bytes 86024 | tf_op jit(solution)/shard_map/ppermute | solution.py:354
  10.0 4.9 %collective-permute-start.4 = (f32[56,128]{1,0:T(8,128)S(1)}, f32[56,128]{1,0:T(8,128)S(1)}, u32[]{:S(2)}, u32[]{:S(2)}) collective-permute-start(f32[56,128]{1,0:T(8,128)S(1)} %get-tuple-element.28), channel_id=1, source_target_pairs={{0,4},{2,6},{4,0},{6,2},{8,12},{10,14},{12,8},{14,10},{16,20},{18,... | collective-permute-start | bytes 86024 | tf_op jit(solution)/shard_map/ppermute | solution.py:354
  11.2 3.7 %collective-permute-start.5 = (f32[56,128]{1,0:T(8,128)S(1)}, f32[56,128]{1,0:T(8,128)S(1)}, u32[]{:S(2)}, u32[]{:S(2)}) collective-permute-start(f32[56,128]{1,0:T(8,128)S(1)} %get-tuple-element.29), channel_id=1, source_target_pairs={{0,6},{2,4},{4,2},{6,0},{8,14},{10,12},{12,10},{14,8},{16,22},{18,... | collective-permute-start | bytes 86024 | tf_op jit(solution)/shard_map/ppermute | solution.py:354
  11.7 33.1 %collective-permute-start = (bf16[4096,128]{1,0:T(8,128)(2,1)S(1)}, bf16[4096,128]{1,0:T(8,128)(2,1)}, u32[]{:S(2)}, u32[]{:S(2)}) collective-permute-start(bf16[4096,128]{1,0:T(8,128)(2,1)S(1)} %copy-done.7), channel_id=1, source_target_pairs={{0,2},{2,4},{4,6},{6,8},{8,10},{10,12},{12,14},{14,16},{16,18},{18... | collective-permute-start | bytes 3145736 | tf_op jit(solution)/shard_map/ppermute | solution.py:344
  16.5 22.7 %all-to-all-start = ((bf16[32,32,128]{2,1,0:T(8,128)(2,1)}), bf16[32,32,128]{2,1,0:T(8,128)(2,1)S(1)}, u32[]{:S(2)}, u32[]{:S(2)}) async-start(bf16[32,32,128]{2,1,0:T(8,128)(2,1)} %spread.1), calls=%async_computation | async-start | bytes 524288 | tf_op jit(solution)/shard_map/all_to_all | solution.py:382
  27.5 3.4 %copy-start.4 = (bf16[32,8,128,128]{3,2,1,0:T(8,128)(2,1)S(1)}, bf16[32,8,128,128]{3,2,1,0:T(8,128)(2,1)}, u32[]{:S(2)}) copy-start(bf16[32,8,128,128]{3,2,1,0:T(8,128)(2,1)} %near.3) | copy-start | bytes 25165828
  36.7 18.0 %collective-permute-start.1 = (bf16[32,128,128]{2,1,0:T(8,128)(2,1)S(1)}, bf16[32,128,128]{2,1,0:T(8,128)(2,1)S(1)}, u32[]{:S(2)}, u32[]{:S(2)}) collective-permute-start(bf16[32,128,128]{2,1,0:T(8,128)(2,1)S(1)} %get-tuple-element.23), channel_id=1, source_target_pairs={{2,0},{4,2},{6,4},{8,6},{10,8},{12,10},{14,12},{16,14},{18,16},{20... | collective-permute-start | bytes 3145736 | tf_op jit(solution)/shard_map/ppermute | solution.py:369
  40.1 14.6 %collective-permute-start.6 = (bf16[32,128]{1,0:T(8,128)(2,1)S(1)}, bf16[32,128]{1,0:T(8,128)(2,1)S(1)}, u32[]{:S(2)}, u32[]{:S(2)}) collective-permute-start(bf16[32,128]{1,0:T(8,128)(2,1)S(1)} %get-tuple-element.31), channel_id=1, source_target_pairs={{0,2},{2,0},{4,6},{6,4},{8,10},{10,8},{12,14},{14,12},{16,18},{18,... | collective-permute-start | bytes 24584 | tf_op jit(solution)/shard_map/ppermute | solution.py:425
  43.1 11.6 %collective-permute-start.7 = (bf16[32,128]{1,0:T(8,128)(2,1)S(1)}, bf16[32,128]{1,0:T(8,128)(2,1)S(1)}, u32[]{:S(2)}, u32[]{:S(2)}) collective-permute-start(bf16[32,128]{1,0:T(8,128)(2,1)S(1)} %get-tuple-element.32), channel_id=1, source_target_pairs={{0,4},{2,6},{4,0},{6,2},{8,12},{10,14},{12,8},{14,10},{16,20},{18,... | collective-permute-start | bytes 24584 | tf_op jit(solution)/shard_map/ppermute | solution.py:425
  43.1 11.6 %collective-permute-start.8 = (bf16[32,128]{1,0:T(8,128)(2,1)S(1)}, bf16[32,128]{1,0:T(8,128)(2,1)S(1)}, u32[]{:S(2)}, u32[]{:S(2)}) collective-permute-start(bf16[32,128]{1,0:T(8,128)(2,1)S(1)} %get-tuple-element.33), channel_id=1, source_target_pairs={{0,6},{2,4},{4,2},{6,0},{8,14},{10,12},{12,10},{14,8},{16,22},{18,... | collective-permute-start | bytes 24584 | tf_op jit(solution)/shard_map/ppermute | solution.py:425
  52.4 2.4 %copy-start = (bf16[32,16,128]{2,1,0:T(8,128)(2,1)S(1)}, bf16[32,16,128]{2,1,0:T(8,128)(2,1)}, u32[]{:S(2)}) copy-start(bf16[32,16,128]{2,1,0:T(8,128)(2,1)} %b_in.3) | copy-start | bytes 393220
  52.4 2.4 %copy-start.1 = (bf16[32,128,16]{1,2,0:T(8,128)(2,1)S(1)}, bf16[32,128,16]{1,2,0:T(8,128)(2,1)}, u32[]{:S(2)}) copy-start(bf16[32,128,16]{1,2,0:T(8,128)(2,1)} %param.16) | copy-start | bytes 393220

commit v7 on v6

--- a/solution.py
+++ b/solution.py
@@ -12,7 +12,7 @@
 QUAD = 4
 PARTS = 4
 UNROLL = 4
-CHUNKS = 8
+CHUNKS = (2, 6, 8, 8, 8)
 AHEAD = 3
 
 
@@ -117,12 +117,13 @@
 
 
 def tile_copies(near, near_v, sems):
-    part = near.shape[0] // CHUNKS
-    spans = [pl.ds(n * part, part) for n in range(CHUNKS)]
-    return [
-        pltpu.make_async_copy(near.at[span], near_v.at[span], sems.at[n])
-        for n, span in enumerate(spans)
-    ]
+    copies = []
+    first = 0
+    for n, size in enumerate(CHUNKS):
+        span = pl.ds(first, size)
+        copies.append(pltpu.make_async_copy(near.at[span], near_v.at[span], sems.at[n]))
+        first += size
+    return copies
 
 
 def backward_kernel(index, count, near, cot, prev, own, acc, out_sems):
@@ -168,20 +169,21 @@
         copy.wait()
     for copy in copies[1:AHEAD]:
         copy.start()
-    part = near.shape[0] // CHUNKS
+    first = 0
     stores = []
     for n, copy in enumerate(copies):
         copy.wait()
-        if n + AHEAD < CHUNKS:
+        if n + AHEAD < len(CHUNKS):
             copies[n + AHEAD].start()
-        for b in range(n * part, (n + 1) * part):
+        for b in range(first, first + CHUNKS[n]):
             live = count[b]
             picked = [rows[jnp.where(k < live, index[k, b] - base, 64)] for k in range(8)]
             tiles = jnp.concatenate([near_v[b, k] for k in range(8)], axis=1)
             out_v[b] = dot(tiles, jnp.concatenate(picked, axis=0))
-        span = pl.ds(n * part, part)
+        span = pl.ds(first, CHUNKS[n])
         stores.append(pltpu.make_async_copy(out_v.at[span], out.at[span], out_sems.at[n]))
         stores[-1].start()
+        first += CHUNKS[n]
     for copy in stores:
         copy.wait()
 
@@ -212,7 +214,7 @@
 
 
 def spread_kernel(*refs):
-    msgs, out, (total, couple) = refs[:4], refs[4], refs[5:]
+    msgs, out, (total, couple, held, sems) = refs[:4], refs[4], refs[5:]
     fill_couple(msgs, couple, total)
     value = msgs[0][0:32, :]
     for ref in msgs[1:]:
@@ -223,19 +225,29 @@
     block = jnp.concatenate(
         [jnp.where(lane16 // 32 == g, bwd, 0.0) for g in range(4)], axis=0
     )
-    contrib = jnp.zeros((512, 128), F32)
+    sides = []
     for p in range(2):
         rhs = jnp.concatenate(
             [block if d == 0 else pltpu.roll(block, 32 * d, 1) for d in (2 * p, 2 * p + 1)],
             axis=0,
         )
-        r_hi, r_lo = split(rhs)
-        k_hi, k_lo = split(couple[p])
-        contrib = contrib + (dot(k_hi, r_lo) + dot(k_lo, r_hi)) + dot(k_hi, r_hi)
-    contrib = contrib.astype(BF16)
-    for t in range(32):
-        out[t, 0:16, :] = fwd
-        out[t, 16:32, :] = contrib[t * 16 : (t + 1) * 16]
+        sides.append(split(rhs))
+    copies = []
+    for n in range(PARTS):
+        contrib = jnp.zeros((128, 128), F32)
+        for p in range(2):
+            r_hi, r_lo = sides[p]
+            k_hi, k_lo = split(couple[p, n * 128 : (n + 1) * 128, :])
+            contrib = contrib + (dot(k_hi, r_lo) + dot(k_lo, r_hi)) + dot(k_hi, r_hi)
+        contrib = contrib.astype(BF16)
+        for i in range(8):
+            held[n * 8 + i, 0:16, :] = fwd
+            held[n * 8 + i, 16:32, :] = contrib[i * 16 : (i + 1) * 16]
+        span = pl.ds(n * 8, 8)
+        copies.append(pltpu.make_async_copy(held.at[span], out.at[span], sems.at[n]))
+        copies[-1].start()
+    for copy in copies:
+        copy.wait()
 
 
 def collect_kernel(arrived, *refs):
@@ -370,10 +382,13 @@
 
     out_msg = pl.pallas_call(
         spread_kernel,
-        out_shape=jax.ShapeDtypeStruct((places, 32, 128), BF16),
+        out_shape=pltpu.HBM((places, 32, 128), BF16),
+        out_specs=raw,
         scratch_shapes=[
             pltpu.VMEM((4, 24, 128), F32),
             pltpu.VMEM((2, places * 16, 128), F32),
+            pltpu.VMEM((places, 32, 128), BF16),
+            pltpu.SemaphoreType.DMA((PARTS,)),
         ],
         compiler_params=params(6, None),
         name="spread",
@@ -390,9 +405,9 @@
             pltpu.VMEM((2 * blocks + 1, 128, 128), BF16),
             pltpu.VMEM(near_kernel.shape, BF16),
             pltpu.VMEM(cube, F32),
-            pltpu.SemaphoreType.DMA((CHUNKS,)),
+            pltpu.SemaphoreType.DMA((len(CHUNKS),)),
             pltpu.SemaphoreType.DMA((2,)),
-            pltpu.SemaphoreType.DMA((CHUNKS,)),
+            pltpu.SemaphoreType.DMA((len(CHUNKS),)),
         ],
         compiler_params=params(16, None),
         cost_estimate=pl.CostEstimate(flops=8 << 30, bytes_accessed=12 << 20, transcendentals=0),

time: 57 us -> 57 us (level)
  the two profiles are of different devices: /device:TPU:25 before, /device:TPU:29 now
where the time goes in v7:
time: 57 us; the launch traced here: 56.7 us
  starting transfers between devices  25.3 us (44%)
  Pallas kernels  23.1 us (41%)
  waiting for transfers between devices  3.89 us (7%)
  local copies, waits for them, and re-layouts  3.41 us (6%)
  between operations  1.04 us (2%)
    all_to_all x1, starting transfers between devices, layer_step(): lax.all_to_all(out_msg, 'curve', 0, 0, tiled=True, axis_index_groups=rings)  11 us
    pallas_call x1, Pallas kernels, layer_step(): pl.pallas_call(forward_kernel, out_shape=pltpu.HBM(cube, F32), in_specs=[...  7.51 us
    pallas_call x1, Pallas kernels, layer_step(): pl.pallas_call(backward_kernel, out_shape=[jax.ShapeDtypeStruct(cube, BF1...  5.84 us
    ppermute x3, starting transfers between devices, layer_step(): lax.ppermute(back[o], 'curve', [(i, i ^ o) for i in range(groups)])  5.08 us
    ppermute x1, waiting for transfers between devices, layer_step(): got = lax.ppermute(give, 'chan', [(0, 1), (1, 0)])  3.87 us
    ppermute x3, starting transfers between devices, layer_step(): lax.ppermute(msgs[o], 'curve', [(i, i ^ o) for i in range(groups)])  3.64 us
    unnamed x16, local copies, waits for them, and re-layouts  3.41 us
    ppermute x1, starting transfers between devices, layer_step(): lax.ppermute(features, 'curve', [(i, i + 1) for i in range(groups - 1)])  2.83 us
  transfers between devices with their start and end apart: 10, of which 1 were waited for; matrix products, arithmetic and copies ran while one was open for 0% of the time, Pallas kernels for 32%

profile of v7, /device:TPU:29, one launch (start us, length us, event | category | flops | bytes accessed | tf_op | source)
XLA Modules:
  0.0 56.7 jit_solution(14124115892785046529)
XLA Ops:
  0.6 0.0 copy-start.2
  0.6 0.0 copy-start.3
  0.7 0.0 copy-start.7
  0.7 0.0 copy-start.5
  0.7 0.0 copy-start.6
  0.7 2.6 %project.1 = (f32[32,128]{1,0:T(8,128)S(1)}, f32[32,128]{1,0:T(8,128)S(1)}, bf16[32,128,128]{2,1,0:T(8,128)(2,1)S(1)}) custom-call(bf16[32,128,128]{2,1,0:T(8,128)(2,1)} %bitcast.14, bf16[32,128,128]{2,1,0:T(8,128)(2,1)} %bitcast.13, bf16[32,16,128]{2,1,0:T(8,128)(2,1)} %b_in.3, bf16[32,16,128]{2,1,0:T(8,128)(2,1)} %bitcast.8, f32[256,256]{1,0:T(8,128)} %mix.1), custom_call_target="tpu_custom_call" | custom-call | flops 8589934592 | bytes 3145728 | tf_op jit(solution)/shard_map/project/pallas_call | solution.py:333
  3.3 0.3 collective-permute-start.2
  3.6 3.9 %collective-permute-done.2.got = f32[32,128]{1,0:T(8,128)S(1)} collective-permute-done((f32[32,128]{1,0:T(8,128)S(1)}, f32[32,128]{1,0:T(8,128)S(1)}, u32[]{:S(2)}, u32[]{:S(2)}) %collective-permute-start.2) | collective-permute-done | bytes 16416 | tf_op jit(solution)/shard_map/ppermute | solution.py:355
  7.4 0.0 copy-done.2
  7.4 0.0 copy-done.3
  7.4 0.6 %deal.1 = (f32[56,128]{1,0:T(8,128)S(1)}, f32[56,128]{1,0:T(8,128)S(1)}, f32[56,128]{1,0:T(8,128)S(1)}, f32[56,128]{1,0:T(8,128)S(1)}) custom-call(s32[1,8]{1,0:T(1,128)S(1)} %copy-done.3, f32[128,16]{1,0:T(8,128)S(1)} %bitcast.10, f32[32,128]{1,0:T(8,128)S(1)} %get-tuple-element.24.keep, f32[32,128]{1,0:T(8,128)S(1)} %collective-permute-done.2.got), custom_call_target="tpu_custom_call" | custom-call | tf_op jit(solution)/shard_map/deal/pallas_call | solution.py:357
  8.1 1.9 %collective-permute-start.3 = (f32[56,128]{1,0:T(8,128)S(1)}, f32[56,128]{1,0:T(8,128)S(1)}, u32[]{:S(2)}, u32[]{:S(2)}) collective-permute-start(f32[56,128]{1,0:T(8,128)S(1)} %get-tuple-element.27), channel_id=1, source_target_pairs={{0,2},{2,0},{4,6},{6,4},{8,10},{10,8},{12,14},{14,12},{16,18},{18,... | collective-permute-start | bytes 86024 | tf_op jit(solution)/shard_map/ppermute | solution.py:366
  10.0 0.9 %collective-permute-start.4 = (f32[56,128]{1,0:T(8,128)S(1)}, f32[56,128]{1,0:T(8,128)S(1)}, u32[]{:S(2)}, u32[]{:S(2)}) collective-permute-start(f32[56,128]{1,0:T(8,128)S(1)} %get-tuple-element.28), channel_id=1, source_target_pairs={{0,4},{2,6},{4,0},{6,2},{8,12},{10,14},{12,8},{14,10},{16,20},{18,... | collective-permute-start | bytes 86024 | tf_op jit(solution)/shard_map/ppermute | solution.py:366
  10.9 0.8 %collective-permute-start.5 = (f32[56,128]{1,0:T(8,128)S(1)}, f32[56,128]{1,0:T(8,128)S(1)}, u32[]{:S(2)}, u32[]{:S(2)}) collective-permute-start(f32[56,128]{1,0:T(8,128)S(1)} %get-tuple-element.29), channel_id=1, source_target_pairs={{0,6},{2,4},{4,2},{6,0},{8,14},{10,12},{12,10},{14,8},{16,22},{18,... | collective-permute-start | bytes 86024 | tf_op jit(solution)/shard_map/ppermute | solution.py:366
  11.7 0.0 copy-done.7
  11.7 2.8 %collective-permute-start = (bf16[4096,128]{1,0:T(8,128)(2,1)S(1)}, bf16[4096,128]{1,0:T(8,128)(2,1)}, u32[]{:S(2)}, u32[]{:S(2)}) collective-permute-start(bf16[4096,128]{1,0:T(8,128)(2,1)S(1)} %copy-done.7), channel_id=1, source_target_pairs={{0,2},{2,4},{4,6},{6,8},{8,10},{10,12},{12,14},{14,16},{16,18},{18... | collective-permute-start | bytes 3145736 | tf_op jit(solution)/shard_map/ppermute | solution.py:356
  14.6 0.0 collective-permute-done.3.refs_1_
  14.6 0.0 collective-permute-done.4.refs_2_
  14.6 0.0 collective-permute-done.5.refs_3_
  14.6 1.5 %spread.1 = bf16[32,32,128]{2,1,0:T(8,128)(2,1)} custom-call(f32[56,128]{1,0:T(8,128)S(1)} %get-tuple-element.26.refs_0_, f32[56,128]{1,0:T(8,128)S(1)} %collective-permute-done.3.refs_1_, f32[56,128]{1,0:T(8,128)S(1)} %collective-permute-done.4.refs_2_, f32[56,128]{1,0:T(8,128)S(1)} %collective-permute-done.5.refs_3_), custom_call_target="tpu_custom_call" | custom-call | tf_op jit(solution)/shard_map/spread/pallas_call | solution.py:383
  16.1 11.0 %all-to-all-start = ((bf16[32,32,128]{2,1,0:T(8,128)(2,1)}), bf16[32,32,128]{2,1,0:T(8,128)(2,1)S(1)}, u32[]{:S(2)}, u32[]{:S(2)}) async-start(bf16[32,32,128]{2,1,0:T(8,128)(2,1)} %spread.1), calls=%async_computation | async-start | bytes 524288 | tf_op jit(solution)/shard_map/all_to_all | solution.py:397
  27.1 0.0 copy-done.5
  27.1 0.0 copy-done.6
  27.1 0.0 copy-start.4
  27.1 3.4 %copy-done.4 = bf16[32,8,128,128]{3,2,1,0:T(8,128)(2,1)S(1)} copy-done((bf16[32,8,128,128]{3,2,1,0:T(8,128)(2,1)S(1)}, bf16[32,8,128,128]{3,2,1,0:T(8,128)(2,1)}, u32[]{:S(2)}) %copy-start.4) | copy-done | bytes 8388632
  30.5 5.8 %backward.1 = (bf16[32,128,128]{2,1,0:T(8,128)(2,1)S(1)}, f32[32,128,128]{2,1,0:T(8,128)}) custom-call(s32[8,32]{1,0:T(8,128)S(1)} %bitcast.11, s32[32]{0:T(128)S(1)} %copy-done.6, bf16[32,8,128,128]{3,2,1,0:T(8,128)(2,1)S(1)} %copy-done.4, bf16[32,128,128]{2,1,0:T(8,128)(2,1)S(1)} %get-tuple-element.19.cot), custom_call_target="tpu_custom_call" | custom-call | flops 8589934592 | bytes 12582912 | tf_op jit(solution)/shard_map/backward/pallas_call | solution.py:368
  36.4 2.4 %collective-permute-start.1 = (bf16[32,128,128]{2,1,0:T(8,128)(2,1)S(1)}, bf16[32,128,128]{2,1,0:T(8,128)(2,1)S(1)}, u32[]{:S(2)}, u32[]{:S(2)}) collective-permute-start(bf16[32,128,128]{2,1,0:T(8,128)(2,1)S(1)} %get-tuple-element.23), channel_id=1, source_target_pairs={{2,0},{4,2},{6,4},{8,6},{10,8},{12,10},{14,12},{16,14},{18,16},{20... | collective-permute-start | bytes 3145736 | tf_op jit(solution)/shard_map/ppermute | solution.py:381
  38.8 0.0 all-to-all-done.arrived
  38.8 0.9 %collect.1 = (bf16[32,128]{1,0:T(8,128)(2,1)S(1)}, bf16[32,128]{1,0:T(8,128)(2,1)S(1)}, bf16[32,128]{1,0:T(8,128)(2,1)S(1)}, bf16[32,128]{1,0:T(8,128)(2,1)S(1)}) custom-call(bf16[32,32,128]{2,1,0:T(8,128)(2,1)S(1)} %all-to-all-done.arrived, f32[56,128]{1,0:T(8,128)S(1)} %get-tuple-element.26.refs_0_, f32[56,128]{1,0:T(8,128)S(1)} %collective-permute-done.3.refs_1_, ...), custom_call_target="tpu_custom_call" | custom-call | tf_op jit(solution)/shard_map/collect/pallas_call | solution.py:417
  39.7 3.3 %collective-permute-start.6 = (bf16[32,128]{1,0:T(8,128)(2,1)S(1)}, bf16[32,128]{1,0:T(8,128)(2,1)S(1)}, u32[]{:S(2)}, u32[]{:S(2)}) collective-permute-start(bf16[32,128]{1,0:T(8,128)(2,1)S(1)} %get-tuple-element.31), channel_id=1, source_target_pairs={{0,2},{2,0},{4,6},{6,4},{8,10},{10,8},{12,14},{14,12},{16,18},{18,... | collective-permute-start | bytes 24584 | tf_op jit(solution)/shard_map/ppermute | solution.py:440
  43.1 0.0 collective-permute-start.7
  43.1 1.7 %collective-permute-start.8 = (bf16[32,128]{1,0:T(8,128)(2,1)S(1)}, bf16[32,128]{1,0:T(8,128)(2,1)S(1)}, u32[]{:S(2)}, u32[]{:S(2)}) collective-permute-start(bf16[32,128]{1,0:T(8,128)(2,1)S(1)} %get-tuple-element.33), channel_id=1, source_target_pairs={{0,6},{2,4},{4,2},{6,0},{8,14},{10,12},{12,10},{14,8},{16,22},{18,... | collective-permute-start | bytes 24584 | tf_op jit(solution)/shard_map/ppermute | solution.py:440
  44.8 0.0 collective-permute-done
  44.8 7.5 %forward.1.near = f32[32,128,128]{2,1,0:T(8,128)} custom-call(s32[8,32]{1,0:T(8,128)S(1)} %bitcast.12, s32[32]{0:T(128)S(1)} %copy-done.6, bf16[32,8,128,128]{3,2,1,0:T(8,128)(2,1)} %near.3, bf16[32,128,128]{2,1,0:T(8,128)(2,1)} %bitcast.1.halo, bf16[32,128,128]{2,1,0:T(8,128)(2,1)} %bitcast.15), custom_call_target="tpu_custom_call" | custom-call | flops 8589934592 | bytes 12582912 | tf_op jit(solution)/shard_map/forward/pallas_call | solution.py:399
  52.3 0.0 copy-start
  52.4 0.0 copy-start.1
  52.4 2.3 %fetch.1 = (f32[32,128,128]{2,1,0:T(8,128)S(1)}, f32[32,128,128]{2,1,0:T(8,128)S(1)}) custom-call(f32[32,128,128]{2,1,0:T(8,128)} %forward.1.near, f32[32,128,128]{2,1,0:T(8,128)} %get-tuple-element.20.own), custom_call_target="tpu_custom_call" | custom-call | flops 1048576 | bytes 8388608 | tf_op jit(solution)/shard_map/fetch/pallas_call | solution.py:428
  54.7 0.0 collective-permute-done.6.m1
  54.7 0.0 collective-permute-done.7.m2
  54.7 0.0 collective-permute-done.8.m3
  54.7 0.0 collective-permute-done.1.arrived
  54.7 0.0 copy-done
  54.7 0.0 copy-done.1
  54.7 1.8 %finish.1 = (bf16[32,128,128]{2,1,0:T(8,128)(2,1)}, bf16[32,128,128]{2,1,0:T(8,128)(2,1)}) custom-call(f32[32,128,128]{2,1,0:T(8,128)S(1)} %get-tuple-element.21.near, f32[32,128,128]{2,1,0:T(8,128)S(1)} %get-tuple-element.22.own, bf16[32,128,128]{2,1,0:T(8,128)(2,1)S(1)} %collective-permute-done.1.arrived, bf16[32,16,128]{2,1,0:T(8,128)(2,1)S(1)} %copy-done, ...), custom_call_target="tpu_custom_call" | custom-call | tf_op jit(solution)/shard_map/finish/pallas_call | solution.py:442
Async XLA Ops:
  0.6 6.8 %copy-start.2 = (f32[1,8,16,16]{3,2,1,0:T(8,128)S(1)}, f32[1,8,16,16]{3,2,1,0:T(8,128)}, u32[]{:S(2)}) copy-start(f32[1,8,16,16]{3,2,1,0:T(8,128)} %param.17) | copy-start | bytes 24580
  0.6 6.8 %copy-start.3 = (s32[1,8]{1,0:T(1,128)S(1)}, s32[1,8]{1,0:T(1,128)}, u32[]{:S(2)}) copy-start(s32[1,8]{1,0:T(1,128)} %far_index.1) | copy-start | bytes 100
  0.7 11.1 %copy-start.7 = (bf16[4096,128]{1,0:T(8,128)(2,1)S(1)}, bf16[4096,128]{1,0:T(8,128)(2,1)}, u32[]{:S(2)}) copy-start(bf16[4096,128]{1,0:T(8,128)(2,1)} %param.10) | copy-start | bytes 3145732
  0.7 26.4 %copy-start.5 = (s32[32,8]{0,1:T(8,128)S(1)}, s32[32,8]{0,1:T(8,128)}, u32[]{:S(2)}) copy-start(s32[32,8]{0,1:T(8,128)} %param.13) | copy-start | bytes 3076
  0.7 26.4 %copy-start.6 = (s32[32]{0:T(128)S(1)}, s32[32]{0:T(128)}, u32[]{:S(2)}) copy-start(s32[32]{0:T(128)} %count.3) | copy-start | bytes 388
  3.3 4.2 %collective-permute-start.2 = (f32[32,128]{1,0:T(8,128)S(1)}, f32[32,128]{1,0:T(8,128)S(1)}, u32[]{:S(2)}, u32[]{:S(2)}) collective-permute-start(f32[32,128]{1,0:T(8,128)S(1)} %get-tuple-element.25), channel_id=1, source_target_pairs={{0,1},{1,0},{2,3},{3,2},{4,5},{5,4},{6,7},{7,6},{8,9},{9,8},{10,11... | collective-permute-start | bytes 49160 | tf_op jit(solution)/shard_map/ppermute | solution.py:355
  8.1 6.5 %collective-permute-start.3 = (f32[56,128]{1,0:T(8,128)S(1)}, f32[56,128]{1,0:T(8,128)S(1)}, u32[]{:S(2)}, u32[]{:S(2)}) collective-permute-start(f32[56,128]{1,0:T(8,128)S(1)} %get-tuple-element.27), channel_id=1, source_target_pairs={{0,2},{2,0},{4,6},{6,4},{8,10},{10,8},{12,14},{14,12},{16,18},{18,... | collective-permute-start | bytes 86024 | tf_op jit(solution)/shard_map/ppermute | solution.py:366
  10.0 4.6 %collective-permute-start.4 = (f32[56,128]{1,0:T(8,128)S(1)}, f32[56,128]{1,0:T(8,128)S(1)}, u32[]{:S(2)}, u32[]{:S(2)}) collective-permute-start(f32[56,128]{1,0:T(8,128)S(1)} %get-tuple-element.28), channel_id=1, source_target_pairs={{0,4},{2,6},{4,0},{6,2},{8,12},{10,14},{12,8},{14,10},{16,20},{18,... | collective-permute-start | bytes 86024 | tf_op jit(solution)/shard_map/ppermute | solution.py:366
  10.9 3.7 %collective-permute-start.5 = (f32[56,128]{1,0:T(8,128)S(1)}, f32[56,128]{1,0:T(8,128)S(1)}, u32[]{:S(2)}, u32[]{:S(2)}) collective-permute-start(f32[56,128]{1,0:T(8,128)S(1)} %get-tuple-element.29), channel_id=1, source_target_pairs={{0,6},{2,4},{4,2},{6,0},{8,14},{10,12},{12,10},{14,8},{16,22},{18,... | collective-permute-start | bytes 86024 | tf_op jit(solution)/shard_map/ppermute | solution.py:366
  11.7 33.1 %collective-permute-start = (bf16[4096,128]{1,0:T(8,128)(2,1)S(1)}, bf16[4096,128]{1,0:T(8,128)(2,1)}, u32[]{:S(2)}, u32[]{:S(2)}) collective-permute-start(bf16[4096,128]{1,0:T(8,128)(2,1)S(1)} %copy-done.7), channel_id=1, source_target_pairs={{0,2},{2,4},{4,6},{6,8},{8,10},{10,12},{12,14},{14,16},{16,18},{18... | collective-permute-start | bytes 3145736 | tf_op jit(solution)/shard_map/ppermute | solution.py:356
  16.1 22.7 %all-to-all-start = ((bf16[32,32,128]{2,1,0:T(8,128)(2,1)}), bf16[32,32,128]{2,1,0:T(8,128)(2,1)S(1)}, u32[]{:S(2)}, u32[]{:S(2)}) async-start(bf16[32,32,128]{2,1,0:T(8,128)(2,1)} %spread.1), calls=%async_computation | async-start | bytes 524288 | tf_op jit(solution)/shard_map/all_to_all | solution.py:397
  27.1 3.4 %copy-start.4 = (bf16[32,8,128,128]{3,2,1,0:T(8,128)(2,1)S(1)}, bf16[32,8,128,128]{3,2,1,0:T(8,128)(2,1)}, u32[]{:S(2)}) copy-start(bf16[32,8,128,128]{3,2,1,0:T(8,128)(2,1)} %near.3) | copy-start | bytes 25165828
  36.4 18.3 %collective-permute-start.1 = (bf16[32,128,128]{2,1,0:T(8,128)(2,1)S(1)}, bf16[32,128,128]{2,1,0:T(8,128)(2,1)S(1)}, u32[]{:S(2)}, u32[]{:S(2)}) collective-permute-start(bf16[32,128,128]{2,1,0:T(8,128)(2,1)S(1)} %get-tuple-element.23), channel_id=1, source_target_pairs={{2,0},{4,2},{6,4},{8,6},{10,8},{12,10},{14,12},{16,14},{18,16},{20... | collective-permute-start | bytes 3145736 | tf_op jit(solution)/shard_map/ppermute | solution.py:381
  39.7 14.9 %collective-permute-start.6 = (bf16[32,128]{1,0:T(8,128)(2,1)S(1)}, bf16[32,128]{1,0:T(8,128)(2,1)S(1)}, u32[]{:S(2)}, u32[]{:S(2)}) collective-permute-start(bf16[32,128]{1,0:T(8,128)(2,1)S(1)} %get-tuple-element.31), channel_id=1, source_target_pairs={{0,2},{2,0},{4,6},{6,4},{8,10},{10,8},{12,14},{14,12},{16,18},{18,... | collective-permute-start | bytes 24584 | tf_op jit(solution)/shard_map/ppermute | solution.py:440
  43.1 11.6 %collective-permute-start.7 = (bf16[32,128]{1,0:T(8,128)(2,1)S(1)}, bf16[32,128]{1,0:T(8,128)(2,1)S(1)}, u32[]{:S(2)}, u32[]{:S(2)}) collective-permute-start(bf16[32,128]{1,0:T(8,128)(2,1)S(1)} %get-tuple-element.32), channel_id=1, source_target_pairs={{0,4},{2,6},{4,0},{6,2},{8,12},{10,14},{12,8},{14,10},{16,20},{18,... | collective-permute-start | bytes 24584 | tf_op jit(solution)/shard_map/ppermute | solution.py:440
  43.1 11.6 %collective-permute-start.8 = (bf16[32,128]{1,0:T(8,128)(2,1)S(1)}, bf16[32,128]{1,0:T(8,128)(2,1)S(1)}, u32[]{:S(2)}, u32[]{:S(2)}) collective-permute-start(bf16[32,128]{1,0:T(8,128)(2,1)S(1)} %get-tuple-element.33), channel_id=1, source_target_pairs={{0,6},{2,4},{4,2},{6,0},{8,14},{10,12},{12,10},{14,8},{16,22},{18,... | collective-permute-start | bytes 24584 | tf_op jit(solution)/shard_map/ppermute | solution.py:440
  52.3 2.4 %copy-start = (bf16[32,16,128]{2,1,0:T(8,128)(2,1)S(1)}, bf16[32,16,128]{2,1,0:T(8,128)(2,1)}, u32[]{:S(2)}) copy-start(bf16[32,16,128]{2,1,0:T(8,128)(2,1)} %b_in.3) | copy-start | bytes 393220
  52.4 2.4 %copy-start.1 = (bf16[32,128,16]{1,2,0:T(8,128)(2,1)S(1)}, bf16[32,128,16]{1,2,0:T(8,128)(2,1)}, u32[]{:S(2)}) copy-start(bf16[32,128,16]{1,2,0:T(8,128)(2,1)} %param.16) | copy-start | bytes 393220
